TPU v7x, 32 devices: a whole 2x2x4 slice. The times are simulated.
32 devices in a mesh: gx: 4 (over y, x), gy: 8 (over z, core).
Axes of the slice: x: 2, y: 2, z: 4, core: 2. Of those that a mesh axis runs over, the one named last changes fastest.
Arguments:
- stream: bfloat16 [768, 4096], P('gy', 'gx'), may hold values from -40 to 40
- qkv_weight: bfloat16 [4096, 12288], P('gx', 'gy'), may hold values from -0.1875 to 0.1875
- up_weight: bfloat16 [4096, 16384], P('gx', 'gy'), may hold values from -0.09375 to 0.09375
- out_weight: bfloat16 [4096, 4096], P('gy', 'gx'), may hold values from -0.09375 to 0.09375
- down_weight: bfloat16 [16384, 4096], P('gy', 'gx'), may hold values from -0.046875 to 0.046875
- cache_keys: bfloat16 [896, 4096], P('gx', 'gy'), may hold values from -400 to 400
- cache_values: bfloat16 [896, 4096], P('gx', 'gy'), may hold values from -12 to 12
- request_prefix: int32 [6], replicated, may hold values from 0 to 1
- request_lengths: int32 [6], replicated, may hold values from 1 to 192, 768 in all
- owner_list: int32 [4], replicated, may hold values from 0 to 3, each once
Outputs:
- layer_out: float32 [768, 4096], P('gy', 'gx')
Inputs may be any that keep to these rules, and one draw needn't show every extreme that they name: `request_lengths`: they sum to 768, and the largest is exactly 192. `owner_list`: each of 0 to 3 appears once.
All inputs are finite; a program needn't handle non-finite values.
Results may differ from a plain program's by a relative error of at most 0.0084.
Values may be sent and summed in bfloat16 or wider, within the bound.
No kernel may reach another device: no remote copies, remote signals or barrier semaphores. Data moves between devices by JAX's collectives and lax.ppermute only.
A program may use at most 128 MiB of HBM per device.

v0:
```python
import jax
import jax.numpy as jnp
from jax import lax
from jax.sharding import PartitionSpec as P

HD = 128
ROT = 32


epsilon = 1e-05
rotary_base = 10000.0
masked_score = -1e30


def token_layout(request_lengths, token_count):
    ending = jnp.cumsum(request_lengths)
    starting = ending - request_lengths
    token_ids = jnp.arange(token_count, dtype=jnp.int32)
    segment = jnp.sum((token_ids[:, None] >= ending[None, :]).astype(jnp.int32), axis=1)
    member = segment[:, None] == jnp.arange(request_lengths.shape[0], dtype=jnp.int32)[None, :]
    first_token = jnp.sum(jnp.where(member, starting[None, :], 0), axis=1)
    return (token_ids, segment, token_ids - first_token, member)


def rotate(vectors, angle_pos):
    halfway = ROT // 2
    frequency = rotary_base ** (-2.0 * jnp.arange(halfway, dtype=jnp.float32) / ROT)
    angles = angle_pos[:, None] * frequency[None, :]
    cosine = jnp.cos(angles)[:, None, :]
    sine_part = jnp.sin(angles)[:, None, :]
    leading = vectors[..., :halfway]
    trailing = vectors[..., halfway:ROT]
    return jnp.concatenate(
        [
            leading * cosine - trailing * sine_part,
            trailing * cosine + leading * sine_part,
            vectors[..., ROT:],
        ],
        axis=-1,
    )


def split_heads(head_block, angle_pos, head_count):
    rows_here = head_block.shape[0]
    head_parts = head_block.reshape(rows_here, head_count, 3, HD)
    queries = rotate(head_parts[:, :, 0], angle_pos).astype(jnp.bfloat16)
    keys_new = rotate(head_parts[:, :, 1], angle_pos).astype(jnp.bfloat16)
    values_new = head_parts[:, :, 2].astype(jnp.bfloat16)
    return (queries, keys_new, values_new)


def shards(
    stream,
    qkv_weight,
    up_weight,
    out_weight,
    down_weight,
    cache_keys,
    cache_values,
    request_prefix,
    request_lengths,
    owner_list,
):
    groups = lax.axis_size("gx")
    group_index = lax.axis_index("gx")
    local_rows = stream.shape[0]
    feature_count = stream.shape[1] * groups
    token_count = local_rows * lax.axis_size("gy")
    share_rows = token_count // groups
    head_cols = qkv_weight.shape[1]
    head_count = head_cols // (3 * HD)
    block_len = cache_keys.shape[0]
    prefix_len = block_len * groups // 2
    score_scale = HD ** (-0.5)
    values32 = stream.astype(jnp.float32)
    moments = lax.psum((jnp.sum(values32, axis=1), jnp.sum(values32 * values32, axis=1)), "gx")
    average = (moments[0] / feature_count)[:, None]
    square = (moments[1] / feature_count)[:, None]
    normed = ((values32 - average) * lax.rsqrt(square - average * average + epsilon)).astype(
        jnp.bfloat16
    )
    row_piece = lax.all_gather(normed, "gy", axis=0, tiled=True)
    partial_sums = jnp.concatenate(
        [
            jnp.dot(row_piece, qkv_weight, preferred_element_type=jnp.float32),
            jnp.dot(row_piece, up_weight, preferred_element_type=jnp.float32),
        ],
        axis=1,
    )
    token_ids, segment, offsets, member = token_layout(request_lengths, token_count)
    angle_pos = (offsets + prefix_len).astype(jnp.float32)
    first_row = group_index * share_rows
    summed = lax.psum_scatter(partial_sums, "gx", scatter_dimension=0, tiled=True)
    up_own = summed[:, head_cols:]
    own_angles = lax.dynamic_slice_in_dim(angle_pos, first_row, share_rows)
    own_query, own_keys, own_values = split_heads(summed[:, :head_cols], own_angles, head_count)
    queries, keys_new, values_new = (
        lax.all_gather(own_query, "gx", axis=0, tiled=True),
        lax.all_gather(own_keys, "gx", axis=0, tiled=True),
        lax.all_gather(own_values, "gx", axis=0, tiled=True),
    )
    hidden_own = jax.nn.gelu(up_own, approximate=False).astype(jnp.bfloat16)
    mine_query = lax.dynamic_slice_in_dim(queries, first_row, share_rows)
    mine_ids = lax.dynamic_slice_in_dim(token_ids, first_row, share_rows)
    mine_segment = lax.dynamic_slice_in_dim(segment, first_row, share_rows)
    visible = (mine_segment[:, None] == segment[None, :]) & (
        token_ids[None, :] <= mine_ids[:, None]
    )
    recent = (
        jnp.einsum("qhd,khd->hqk", mine_query, keys_new, preferred_element_type=jnp.float32)
        * score_scale
    )
    recent = jnp.where(visible[None], recent, masked_score)
    recent_peak = jnp.max(recent, axis=2)
    recent_weights = jnp.exp(recent - recent_peak[..., None])
    recent_total = jnp.sum(recent_weights, axis=2)
    recent_out = jnp.einsum(
        "hqk,khd->hqd",
        recent_weights.astype(jnp.bfloat16),
        values_new,
        preferred_element_type=jnp.float32,
    )
    halfway = groups // 2
    slot_index = jnp.arange(groups, dtype=jnp.int32)
    held_prefix = jnp.sum(
        jnp.where(owner_list == group_index, (slot_index >= halfway).astype(jnp.int32), 0)
    )
    token_prefix = jnp.sum(jnp.where(member, request_prefix[None, :], 0), axis=1)
    active = (token_prefix == held_prefix)[None, :, None]
    step_len = min(512, block_len)
    key_blocks = cache_keys.reshape(block_len // step_len, step_len, head_count, HD)
    value_blocks = cache_values.reshape(block_len // step_len, step_len, head_count, HD)

    def visit(carried, blocks):
        run_peak, run_total, run_out = carried
        block_keys, block_values = blocks
        scores = (
            jnp.einsum("qhd,khd->hqk", queries, block_keys, preferred_element_type=jnp.float32)
            * score_scale
        )
        scores = jnp.where(active, scores, masked_score)
        new_peak = jnp.maximum(run_peak, jnp.max(scores, axis=2))
        fading = jnp.exp(run_peak - new_peak)
        weights = jnp.exp(scores - new_peak[..., None])
        run_total = run_total * fading + jnp.sum(weights, axis=2)
        run_out = run_out * fading[..., None] + jnp.einsum(
            "hqk,khd->hqd",
            weights.astype(jnp.bfloat16),
            block_values,
            preferred_element_type=jnp.float32,
        )
        return ((new_peak, run_total, run_out), None)

    start_carry = (
        jnp.full((head_count, token_count), masked_score, jnp.float32),
        jnp.zeros((head_count, token_count), jnp.float32),
        jnp.zeros((head_count, token_count, HD), jnp.float32),
    )
    (cache_peak, cache_total, cache_out), unused = lax.scan(
        visit, start_carry, (key_blocks, value_blocks)
    )
    global_peak = lax.pmax(cache_peak, "gx")
    fading = jnp.exp(cache_peak - global_peak)
    own_total, own_out = (
        lax.psum_scatter(
            (cache_total * fading).astype(jnp.bfloat16), "gx", scatter_dimension=1, tiled=True
        ).astype(jnp.float32),
        lax.psum_scatter(
            (cache_out * fading[..., None]).astype(jnp.bfloat16),
            "gx",
            scatter_dimension=1,
            tiled=True,
        ).astype(jnp.float32),
    )
    own_peak = lax.dynamic_slice_in_dim(global_peak, first_row, share_rows, 1)
    joint_peak = jnp.maximum(own_peak, recent_peak)
    cache_fade = jnp.exp(own_peak - joint_peak)
    recent_fade = jnp.exp(recent_peak - joint_peak)
    context = (own_out * cache_fade[..., None] + recent_out * recent_fade[..., None]) / (
        own_total * cache_fade + recent_total * recent_fade
    )[..., None]
    context = (
        jnp.transpose(context, (1, 0, 2)).reshape(share_rows, head_count * HD).astype(jnp.bfloat16)
    )
    joined = jnp.concatenate([context, hidden_own], axis=1)
    gathered = lax.all_gather(joined, "gx", axis=0, tiled=True)
    context_cols = context.shape[1]
    row_piece = gathered
    mixed_sum = lax.psum_scatter(
        (
            jnp.dot(row_piece[:, :context_cols], out_weight, preferred_element_type=jnp.float32)
            + jnp.dot(row_piece[:, context_cols:], down_weight, preferred_element_type=jnp.float32)
        ).astype(jnp.bfloat16),
        "gy",
        scatter_dimension=0,
        tiled=True,
    ).astype(jnp.float32)
    return values32 + mixed_sum


def solution(mesh):
    placed = (
        P("gy", "gx"),
        P("gx", "gy"),
        P("gx", "gy"),
        P("gy", "gx"),
        P("gy", "gx"),
        P("gx", "gy"),
        P("gx", "gy"),
        P(),
        P(),
        P(),
    )
    return jax.shard_map(
        shards, mesh=mesh, in_specs=placed, out_specs=P("gy", "gx"), check_vma=False
    )
```

profile of v0, /device:TPU:0, one launch (start us, length us, event | category | flops | bytes accessed | tf_op | source)
XLA Modules:
  0.0 387.8 jit_solution(503710004376273790)
XLA Ops:
  7.8 11.4 %all-reduce = (f32[96]{0:T(128)S(1)}, f32[96]{0:T(128)S(1)}) all-reduce(f32[96]{0:T(128)S(1)} %get-tuple-element.20, f32[96]{0:T(128)S(1)} %get-tuple-element.19), channel_id=1, replica_groups=mesh['gx'=4,'gy'=8] {'gx'}, use_global_device_ids=true, to_apply=%region_7.8 | all-reduce | flops 192 | bytes 1536 | tf_op jit(solution)/shard_map/psum | solution.py:76
  21.0 24.5 %all-gather.4.cloned.1.call-done = bf16[768,1024]{1,0:T(8,128)(2,1)} async-done(((bf16[96,1024]{1,0:T(8,128)(2,1)}), bf16[768,1024]{1,0:T(8,128)(2,1)}) %all-gather.4.cloned.1.call-update) | async-done | bytes 1572880 | tf_op jit(solution)/shard_map/all_gather | solution.py:82
  45.5 8.8 %fusion.61 = f32[768,2048]{1,0:T(8,128)} fusion(bf16[768,1024]{1,0:T(8,128)(2,1)} %all-gather.4.cloned.1.call-done, bf16[1024,2048]{1,0:T(8,128)(2,1)} %param.12), kind=kOutput, calls=%fused_computation.110 | convolution fusion | flops 3221225472 | bytes 12058624 | tf_op jit(solution)/shard_map/dot_general | solution.py:86
  54.3 4.3 %fusion.60 = f32[768,1536]{1,0:T(8,128)} fusion(bf16[768,1024]{1,0:T(8,128)(2,1)S(1)} %copy-done.8, bf16[1024,1536]{1,0:T(8,128)(2,1)S(1)} %copy-done), kind=kOutput, calls=%fused_computation.109 | convolution fusion | flops 2415919104 | bytes 9437184 | tf_op jit(solution)/shard_map/dot_general | solution.py:85
  58.6 9.1 %pad_maximum_fusion = f32[768,3584]{1,0:T(8,128)} fusion(f32[768,2048]{1,0:T(8,128)} %fusion.61, f32[768,1536]{1,0:T(8,128)} %fusion.60), kind=kLoop, calls=%fused_computation | loop fusion | flops 2752512 | bytes 22020096 | tf_op jit(solution)/shard_map/concatenate | solution.py:83
  70.9 104.4 %reduce-scatter.7.cloned.1.call-done = f32[192,3584]{1,0:T(8,128)} async-done(((f32[768,3584]{1,0:T(8,128)}), f32[192,3584]{1,0:T(8,128)}) %reduce-scatter.7.cloned.1.call-update) | async-done | bytes 2752528 | tf_op jit(solution)/shard_map/reduce_scatter | solution.py:93
  175.3 2.4 slice.55
  177.7 2.8 reshape.155
  180.5 2.6 fusion.59
  183.9 11.2 %all_gather.16 = bf16[768,4,128]{2,0,1:T(8,128)(2,1)S(1)} all-gather(bf16[192,4,128]{2,0,1:T(8,128)(2,1)S(1)} %pad_maximum_fusion.2), channel_id=1, replica_groups=mesh['gx'=4,'gy'=8] {'gx'}, dimensions={0}, use_global_device_ids=true | all-gather | bytes 983040 | tf_op jit(solution)/shard_map/all_gather | solution.py:98
  195.3 11.6 %all_gather.17 = bf16[768,4,128]{2,0,1:T(8,128)(2,1)} all-gather(bf16[192,4,128]{2,0,1:T(8,128)(2,1)S(1)} %pad_maximum_fusion.3), channel_id=1, replica_groups=mesh['gx'=4,'gy'=8] {'gx'}, dimensions={0}, use_global_device_ids=true | all-gather | bytes 983040 | tf_op jit(solution)/shard_map/all_gather | solution.py:99
  209.0 15.2 %pmax.7 = f32[4,768]{1,0:T(4,128)S(1)} all-reduce(f32[4,768]{1,0:T(4,128)S(1)} %broadcast_maximum_fusion), channel_id=1, replica_groups=mesh['gx'=4,'gy'=8] {'gx'}, use_global_device_ids=true, to_apply=%region_11.12 | all-reduce | flops 3072 | bytes 24576 | tf_op jit(solution)/shard_map/pmax | solution.py:162
  224.2 2.3 fusion.3
  227.7 4.2 %multiply_convert_fusion = bf16[4,768,128]{2,1,0:T(8,128)(2,1)} fusion(f32[4,768,224]{1,2,0:T(8,128)} %get-tuple-element.56, f32[4,768]{1,0:T(4,128)S(1)} %broadcast_maximum_fusion, pred[768]{0:T(1024)(128)(4,1)S(1)} %broadcast_compare_fusion, f32[4,768]{1,0:T(4,128)S(1)} %get-tuple-element.39, f32[4,768]{1,0:T(4,128)S(1)} %get-tuple-element.48, ...), kind=kOutput, calls=%fused_computation.31 | convolution fusion | flops 180092928 | bytes 3805952 | tf_op jit(solution)/shard_map/while/body/eval_jaxpr/hqk,khd->hqd/dot_general | solution.py:146
  231.9 3.2 fusion.5
  237.1 11.9 %all-gather = bf16[768,4,1,128]{3,0,1,2:T(8,128)(2,1)} all-gather(bf16[192,4,1,128]{3,0,1,2:T(8,128)(2,1)S(1)} %copy.63), channel_id=2, replica_groups=mesh['gx'=4,'gy'=8] {'gx'}, dimensions={0}, use_global_device_ids=true | all-gather | bytes 983040 | tf_op jit(solution)/shard_map/all_gather | solution.py:100
  249.0 2.4 fusion.6
  251.4 4.1 %fusion.10 = bf16[192,2048]{1,0:T(8,128)(2,1)} fusion(f32[192,3584]{1,0:T(8,128)S(1)} %copy-done.3), kind=kLoop, calls=%fused_computation.17 | loop fusion | flops 25559040 | bytes 2359296 | tf_op jit(solution)/shard_map/convert_element_type | solution.py:102
  256.5 24.0 %reduce-scatter.9.cloned.1.call-done = bf16[4,192,128]{2,1,0:T(8,128)(2,1)} async-done(((bf16[4,768,128]{2,1,0:T(8,128)(2,1)}), bf16[4,192,128]{2,1,0:T(8,128)(2,1)}) %reduce-scatter.9.cloned.1.call-update) | async-done | bytes 196624 | tf_op jit(solution)/shard_map/reduce_scatter | solution.py:168
  280.5 2.9 fusion.33
  284.6 50.6 %all-gather.6.cloned.1.call-done = bf16[768,2560]{1,0:T(8,128)(2,1)} async-done(((bf16[192,2560]{1,0:T(8,128)(2,1)}), bf16[768,2560]{1,0:T(8,128)(2,1)}) %all-gather.6.cloned.1.call-update) | async-done | bytes 3932176 | tf_op jit(solution)/shard_map/all_gather | solution.py:186
  335.2 6.2 %fusion = f32[768,1024]{1,0:T(8,128)S(1)} fusion(bf16[2048,1024]{1,0:T(8,128)(2,1)} %param.14, bf16[768,2560]{1,0:T(8,128)(2,1)} %all-gather.6.cloned.1.call-done), kind=kOutput, calls=%fused_computation.1 | convolution fusion | flops 3221225472 | bytes 10485760 | tf_op jit(solution)/shard_map/dot_general | solution.py:192
  341.4 3.3 add_convert_fusion
  344.8 34.5 %reduce-scatter.11.cloned.1.call-done = bf16[96,1024]{1,0:T(8,128)(2,1)} async-done(((bf16[768,1024]{1,0:T(8,128)(2,1)}), bf16[96,1024]{1,0:T(8,128)(2,1)}) %reduce-scatter.11.cloned.1.call-update) | async-done | bytes 196624 | tf_op jit(solution)/shard_map/reduce_scatter | solution.py:189
  (71 shorter events, 16.2 us)
Async XLA Ops:
  6.5 47.8 %copy-start = (bf16[1024,1536]{1,0:T(8,128)(2,1)S(1)}, bf16[1024,1536]{1,0:T(8,128)(2,1)}, u32[]{:S(2)}) copy-start(bf16[1024,1536]{1,0:T(8,128)(2,1)} %param.11) | copy-start | bytes 9437188
  6.5 39.0 %all-gather.4.cloned.1.call-start = ((), (), s32[]{:S(2)}) async-start(), calls=%async_computation.4 | async-start | bytes 1769472 | tf_op jit(solution)/shard_map/all_gather | solution.py:82
  20.9 154.4 %reduce-scatter.7.cloned.1.call-start = ((), (), s32[]{:S(2)}) async-start(), calls=%async_computation.5 | async-start | bytes 13762560 | tf_op jit(solution)/shard_map/reduce_scatter | solution.py:93
  45.5 8.8 %copy-start.8 = (bf16[768,1024]{1,0:T(8,128)(2,1)S(1)}, bf16[768,1024]{1,0:T(8,128)(2,1)}, u32[]{:S(2)}) copy-start(bf16[768,1024]{1,0:T(8,128)(2,1)} %all-gather.4.cloned.1.call-done) | copy-start | bytes 4718596
  67.7 0.7 copy-start.9
  67.7 1.0 copy-start.7
  67.7 1.6 copy-start.10
  67.7 187.8 %reduce-scatter.13.cloned.1.call-start = ((), (), s32[]{:S(2)}) async-start(), calls=%async_computation.9 | async-start | bytes 245760
  183.9 23.0 %copy-start.6 = (bf16[224,512]{1,0:T(8,128)(2,1)S(1)}, bf16[224,512]{1,0:T(8,128)(2,1)}, u32[]{:S(2)}) copy-start(bf16[224,512]{1,0:T(8,128)(2,1)} %param.15) | copy-start | bytes 688132
  195.1 13.9 %copy-start.1 = (bf16[768,4,128]{2,0,1:T(8,128)(2,1)}, bf16[768,4,128]{2,0,1:T(8,128)(2,1)S(1)}, u32[]{:S(2)}) copy-start(bf16[768,4,128]{2,0,1:T(8,128)(2,1)S(1)} %all_gather.16) | copy-start | bytes 2359300
  227.4 53.1 %reduce-scatter.9.cloned.1.call-start = ((), (), s32[]{:S(2)}) async-start(), calls=%async_computation.6 | async-start | bytes 983040 | tf_op jit(solution)/shard_map/reduce_scatter | solution.py:168
  237.0 98.2 %all-gather.6.cloned.1.call-start = ((), (), s32[]{:S(2)}) async-start(), calls=%async_computation.7 | async-start | bytes 4915200 | tf_op jit(solution)/shard_map/all_gather | solution.py:186
  237.1 14.3 %copy-start.3 = (f32[192,3584]{1,0:T(8,128)S(1)}, f32[192,3584]{1,0:T(8,128)}, u32[]{:S(2)}) copy-start(f32[192,3584]{1,0:T(8,128)} %reduce-scatter.7.cloned.1.call-done) | copy-start | bytes 8257540
  280.5 3.0 copy-start.2
  284.5 94.7 %reduce-scatter.11.cloned.1.call-start = ((), (), s32[]{:S(2)}) async-start(), calls=%async_computation.8 | async-start | bytes 1769472 | tf_op jit(solution)/shard_map/reduce_scatter | solution.py:189
  335.2 6.2 %copy-start.5 = (bf16[512,1024]{1,0:T(8,128)(2,1)S(1)}, bf16[512,1024]{1,0:T(8,128)(2,1)}, u32[]{:S(2)}) copy-start(bf16[512,1024]{1,0:T(8,128)(2,1)} %param.13) | copy-start | bytes 3145732
  344.7 34.5 %copy-start.4 = (bf16[96,1024]{1,0:T(8,128)(2,1)S(1)}, bf16[96,1024]{1,0:T(8,128)(2,1)}, u32[]{:S(2)}) copy-start(bf16[96,1024]{1,0:T(8,128)(2,1)} %param.10) | copy-start | bytes 589828
Sparse Core Ops, SparseCore 0:
  21.1 24.4 all-gather.3
  67.9 107.4 reduce-scatter.6
  227.6 23.9 reduce-scatter.12
  254.4 26.1 reduce-scatter.8
  284.7 50.4 all-gather.5
  344.9 34.3 reduce-scatter.10
where the time goes:
time: 388 us
  waiting for transfers between devices  238 us (61%)
  blocking collectives  61.3 us (16%)
  matrix products  35.1 us (9%)
  other arithmetic  26.5 us (7%)
  between operations  13.7 us (4%)
  local copies, waits for them, and re-layouts  12.7 us (3%)
    reduce_scatter x1, waiting for transfers between devices, shards(): lax.psum_scatter(partial_sums, 'gx', scatter_dimension=0, tiled=True)  104 us
    all_gather x1, waiting for transfers between devices, shards(): gathered = lax.all_gather(joined, 'gx', axis=0, tiled=True)  50.6 us
    reduce_scatter x1, waiting for transfers between devices, shards(): lax.psum_scatter((jnp.dot(row_piece[:, :context_cols], out_weight, prefer...  34.5 us
    all_gather x1, waiting for transfers between devices, shards(): row_piece = lax.all_gather(normed, 'gy', axis=0, tiled=True)  24.5 us
    reduce_scatter x1, waiting for transfers between devices, shards(): lax.psum_scatter((cache_out * fading[..., None]).astype(jnp.bfloat16), 'g...  24 us
    pmax x1, blocking collectives, shards(): global_peak = lax.pmax(cache_peak, 'gx')  15.2 us
    all_gather x1, blocking collectives, shards(): lax.all_gather(own_values, 'gx', axis=0, tiled=True)  11.9 us
    all_gather x1, blocking collectives, shards(): lax.all_gather(own_keys, 'gx', axis=0, tiled=True)  11.6 us
  transfers between devices with their start and end apart: 6, of which 5 were waited for; matrix products, arithmetic and copies ran while one was open for 5% of the time, Pallas kernels for 0%

commit v1 on v0

--- a/solution.py
+++ b/solution.py
@@ -1,6 +1,10 @@
+import functools
+
 import jax
 import jax.numpy as jnp
 from jax import lax
+from jax.experimental import pallas as pl
+from jax.experimental.pallas import tpu as pltpu
 from jax.sharding import PartitionSpec as P
 
 HD = 128
@@ -198,6 +202,264 @@
     return values32 + mixed_sum
 
 
+def swap(value, axis, bits):
+    count = lax.axis_size(axis)
+    return lax.ppermute(value, axis, [(d, d ^ bits) for d in range(count)])
+
+
+def project_body(order_ref, x_ref, w_ref, out_ref):
+    out_ref[0] = jnp.dot(x_ref[...], w_ref[...], preferred_element_type=jnp.float32).astype(
+        out_ref.dtype
+    )
+
+
+def project(rows, weight, order, width, dtype):
+    count = order.shape[0]
+    row_count, depth = rows.shape
+    return pl.pallas_call(
+        project_body,
+        out_shape=jax.ShapeDtypeStruct((count, row_count, width), dtype),
+        grid_spec=pltpu.PrefetchScalarGridSpec(
+            num_scalar_prefetch=1,
+            grid=(count,),
+            in_specs=[
+                pl.BlockSpec((row_count, depth), lambda g, o: (0, 0)),
+                pl.BlockSpec((depth, width), lambda g, o: (0, o[g])),
+            ],
+            out_specs=pl.BlockSpec((1, row_count, width), lambda g, o: (g, 0, 0)),
+        ),
+        cost_estimate=pl.CostEstimate(
+            flops=2 * count * row_count * depth * width,
+            bytes_accessed=2 * (row_count * depth + count * depth * width)
+            + count * row_count * width * jnp.dtype(dtype).itemsize,
+            transcendentals=0,
+        ),
+        compiler_params=pltpu.CompilerParams(vmem_limit_bytes=24 << 20),
+        name="project",
+    )(order, rows, weight)
+
+
+def turn(vectors, cosine, sine_up, sine_down):
+    half = ROT // 2
+    return (
+        vectors * cosine
+        + pltpu.roll(vectors, half, 1) * sine_up
+        + pltpu.roll(vectors, HD - half, 1) * sine_down
+    )
+
+
+def attend_body(
+    sum_a, got_a, sum_b, got_b, tables, keys_old, values_old, per_query, per_new, per_old, out_ref,
+    query_s, key_s, value_s,
+):
+    half_rows = got_a.shape[0]
+    scale = HD ** (-0.5)
+    for half, (total, got) in enumerate(((sum_a, got_a), (sum_b, got_b))):
+        span = pl.ds(half * half_rows, half_rows)
+        cosine, up, down = (tables[t, span, :] for t in range(3))
+        parts = [
+            total[0, :, p * HD : (p + 1) * HD].astype(jnp.float32)
+            + got[:, p * HD : (p + 1) * HD].astype(jnp.float32)
+            for p in range(3)
+        ]
+        query_s[span, :] = turn(parts[0], cosine, up, down).astype(jnp.bfloat16)
+        key_s[span, :] = turn(parts[1], cosine, up, down).astype(jnp.bfloat16)
+        value_s[span, :] = parts[2].astype(jnp.bfloat16)
+    tile = 128
+    across = (((1,), (1,)), ((), ()))
+
+    def visit(step, unused):
+        rows = pl.ds(pl.multiple_of(step * tile, tile), tile)
+        query = query_s[rows, :]
+        numbers = per_query[rows, :]
+        token, first, prefix = numbers[:, 0:1], numbers[:, 1:2], numbers[:, 2:3]
+        cached = (
+            lax.dot_general(query, keys_old[...], across, preferred_element_type=jnp.float32)
+            * scale
+        )
+        cached = jnp.where(prefix == per_old[...], cached, masked_score)
+        recent = (
+            lax.dot_general(query, key_s[...], across, preferred_element_type=jnp.float32) * scale
+        )
+        other = per_new[...]
+        recent = jnp.where((other >= first) & (other <= token), recent, masked_score)
+        top = jnp.maximum(
+            jnp.max(cached, axis=1, keepdims=True), jnp.max(recent, axis=1, keepdims=True)
+        )
+        cached = jnp.exp(cached - top)
+        recent = jnp.exp(recent - top)
+        total = jnp.sum(cached, axis=1, keepdims=True) + jnp.sum(recent, axis=1, keepdims=True)
+        context = jnp.dot(
+            cached.astype(jnp.bfloat16), values_old[...], preferred_element_type=jnp.float32
+        ) + jnp.dot(recent.astype(jnp.bfloat16), value_s[...], preferred_element_type=jnp.float32)
+        out_ref[rows, :] = (context / total).astype(jnp.bfloat16)
+        return unused
+
+    lax.fori_loop(0, query_s.shape[0] // tile, visit, 0)
+
+
+def attend(sum_a, got_a, sum_b, got_b, tables, keys_old, values_old, per_query, per_new, per_old):
+    token_count = per_query.shape[0]
+    keys = token_count + keys_old.shape[0]
+    return pl.pallas_call(
+        attend_body,
+        out_shape=jax.ShapeDtypeStruct((token_count, HD), jnp.bfloat16),
+        in_specs=[pl.BlockSpec(memory_space=pltpu.VMEM)] * 10,
+        out_specs=pl.BlockSpec(memory_space=pltpu.VMEM),
+        scratch_shapes=[pltpu.VMEM((token_count, HD), jnp.bfloat16)] * 3,
+        cost_estimate=pl.CostEstimate(
+            flops=4 * token_count * keys * HD,
+            bytes_accessed=4 * token_count * HD * 8,
+            transcendentals=token_count * keys,
+        ),
+        compiler_params=pltpu.CompilerParams(vmem_limit_bytes=32 << 20),
+        name="attend",
+    )(sum_a, got_a, sum_b, got_b, tables, keys_old, values_old, per_query, per_new, per_old)
+
+
+def mix_body(order_ref, h0, h1, h2, c0, c1, c2, down_ref, out_w_ref, out_ref):
+    width, head = h0.shape[1], c0.shape[1]
+    hidden = (h0[...], h1[...], h2[0], h2[1])
+    context = (c0[...], c1[...], c2[0], c2[1])
+    total = None
+    for m in range(4):
+        block = order_ref[m]
+        down = down_ref[pl.ds(pl.multiple_of(block * width, width), width), :]
+        out = out_w_ref[pl.ds(pl.multiple_of(block * head, head), head), :]
+        term = jnp.dot(hidden[m], down, preferred_element_type=jnp.float32) + jnp.dot(
+            context[m], out, preferred_element_type=jnp.float32
+        )
+        total = term if total is None else total + term
+    out_ref[...] = total.astype(out_ref.dtype)
+
+
+def mix(order, hidden, context, down_weight, out_weight, dtype):
+    rows = hidden[0].shape[0]
+    columns = down_weight.shape[1]
+    depth = down_weight.shape[0] + out_weight.shape[0]
+    return pl.pallas_call(
+        mix_body,
+        out_shape=jax.ShapeDtypeStruct((rows, columns), dtype),
+        in_specs=[pl.BlockSpec(memory_space=pltpu.SMEM)]
+        + [pl.BlockSpec(memory_space=pltpu.VMEM)] * 8,
+        out_specs=pl.BlockSpec(memory_space=pltpu.VMEM),
+        cost_estimate=pl.CostEstimate(
+            flops=2 * rows * depth * columns,
+            bytes_accessed=2 * (rows * depth + depth * columns + rows * columns),
+            transcendentals=0,
+        ),
+        compiler_params=pltpu.CompilerParams(vmem_limit_bytes=32 << 20),
+        name="mix",
+    )(order, *hidden, *context, down_weight, out_weight)
+
+
+def square_shards(
+    stream, qkv_weight, up_weight, out_weight, down_weight, cache_keys, cache_values,
+    request_prefix, request_lengths, owner_list,
+):
+    groups = lax.axis_size("gx")
+    own = lax.axis_index("gx")
+    mine = lax.axis_index("gy")
+    local_rows = stream.shape[0]
+    feature_count = stream.shape[1] * groups
+    token_count = local_rows * lax.axis_size("gy")
+    half_rows = token_count // 2
+    block_len = cache_keys.shape[0]
+    prefix_len = block_len * groups // 2
+    head_width = qkv_weight.shape[1] // groups
+    hidden_width = up_weight.shape[1] // groups
+
+    values32 = stream.astype(jnp.float32)
+    moments = lax.psum((jnp.sum(values32, axis=1), jnp.sum(values32 * values32, axis=1)), "gx")
+    average = (moments[0] / feature_count)[:, None]
+    square = (moments[1] / feature_count)[:, None]
+    normed = ((values32 - average) * lax.rsqrt(square - average * average + epsilon)).astype(
+        jnp.bfloat16
+    )
+    rows_a = jnp.concatenate([normed] + [swap(normed, "gy", 2 * k) for k in range(1, 4)], axis=0)
+    rows_b = swap(rows_a, "gy", 1)
+
+    old = jnp.stack([cache_keys, cache_values])
+    pieces = []
+    for m in range(4):
+        piece = lax.dynamic_slice_in_dim(old, (own ^ m) * HD, HD, 2)
+        pieces.append(swap(piece, "gx", m) if m else piece)
+    old = jnp.concatenate(pieces, axis=1)
+
+    token_ids, segment, offsets, member = token_layout(request_lengths, token_count)
+    block = jnp.arange(8, dtype=jnp.int32)
+    source = mine ^ (2 * (block % 4) + block // 4)
+    token = (
+        source[:, None] * local_rows + jnp.arange(local_rows, dtype=jnp.int32)[None, :]
+    ).reshape(token_count)
+    ending = jnp.cumsum(request_lengths)
+    starting = ending - request_lengths
+    inside = (token[:, None] >= starting[None, :]) & (token[:, None] < ending[None, :])
+    first = jnp.sum(jnp.where(inside, starting[None, :], 0), axis=1)
+    prefix = jnp.sum(jnp.where(inside, request_prefix[None, :], 0), axis=1)
+    slot = jnp.arange(groups, dtype=jnp.int32)
+    order = own ^ slot
+    held = jnp.sum(
+        jnp.where(
+            owner_list[None, :] == order[:, None],
+            (slot >= groups // 2).astype(jnp.int32)[None, :],
+            0,
+        ),
+        axis=1,
+    )
+    per_old = jnp.repeat(held, block_len)[None, :]
+    per_new = token[None, :]
+    per_query = jnp.stack([token, first, prefix, prefix], axis=1)
+    half = ROT // 2
+    frequency = rotary_base ** (-2.0 * jnp.arange(half, dtype=jnp.float32) / ROT)
+    angles = (token - first + prefix_len).astype(jnp.float32)[:, None] * frequency[None, :]
+    cosine, sine = jnp.cos(angles), jnp.sin(angles)
+    zero = jnp.zeros_like(sine)
+    rest = jnp.zeros((token_count, HD - ROT), jnp.float32)
+    tables = jnp.stack(
+        [
+            jnp.concatenate([cosine, cosine, rest + 1.0], axis=1),
+            jnp.concatenate([zero, sine, rest], axis=1),
+            jnp.concatenate([-sine, zero, rest], axis=1),
+        ]
+    )
+
+    def scattered(weight, width):
+        send_a = project(rows_a, weight, jnp.stack([own ^ 1, own ^ 3]), width, jnp.bfloat16)
+        send_b = project(rows_b, weight, jnp.stack([own ^ 2, own ^ 3]), width, jnp.bfloat16)
+        got_a, got_b = swap(send_a, "gx", 1), swap(send_b, "gx", 2)
+        keep_a = project(rows_a, weight, jnp.stack([own, own ^ 2]), width, jnp.float32)
+        keep_b = project(rows_b, weight, jnp.stack([own, own ^ 1]), width, jnp.float32)
+        sum_a, sum_b = keep_a + got_a.astype(jnp.float32), keep_b + got_b.astype(jnp.float32)
+        last_a = swap(sum_a[1].astype(jnp.bfloat16), "gx", 2)
+        last_b = swap(sum_b[1].astype(jnp.bfloat16), "gx", 1)
+        return sum_a, last_a, sum_b, last_b
+
+    def gathered(part_a, part_b):
+        one_a, one_b = swap(part_a, "gx", 1), swap(part_b, "gx", 2)
+        two_a = swap(jnp.stack([part_a, one_a]), "gx", 2)
+        two_b = swap(jnp.stack([part_b, one_b]), "gx", 1)
+        return (part_a, one_a, two_a), (part_b, one_b, two_b)
+
+    head = scattered(qkv_weight, head_width)
+    sum_a, last_a, sum_b, last_b = scattered(up_weight, hidden_width)
+    context = attend(*head, tables, old[0], old[1], per_query, per_new, per_old)
+    context_a, context_b = gathered(context[:half_rows], context[half_rows:])
+    hidden_a = jax.nn.gelu(sum_a[0] + last_a.astype(jnp.float32), approximate=False)
+    hidden_b = jax.nn.gelu(sum_b[0] + last_b.astype(jnp.float32), approximate=False)
+    hidden_a, hidden_b = gathered(hidden_a.astype(jnp.bfloat16), hidden_b.astype(jnp.bfloat16))
+
+    order_b = jnp.stack([own, own ^ 2, own ^ 1, own ^ 3])
+    mixed_b = mix(order_b, hidden_b, context_b, down_weight, out_weight, jnp.bfloat16)
+    other = swap(mixed_b, "gy", 1)
+    mixed_a = mix(order, hidden_a, context_a, down_weight, out_weight, jnp.float32)
+    mixed = (mixed_a + other.astype(jnp.float32)).reshape(4, local_rows, -1)
+    total = values32 + mixed[0]
+    for k in range(1, 4):
+        total = total + swap(mixed[k].astype(jnp.bfloat16), "gy", 2 * k).astype(jnp.float32)
+    return total
+
+
 def solution(mesh):
     placed = (
         P("gy", "gx"),
@@ -211,6 +473,17 @@
         P(),
         P(),
     )
-    return jax.shard_map(
-        shards, mesh=mesh, in_specs=placed, out_specs=P("gy", "gx"), check_vma=False
-    )
+    sizes = dict(zip(mesh.axis_names, mesh.devices.shape))
+
+    def program(*arrays):
+        heads = arrays[1].shape[1] // (3 * HD) // sizes["gy"]
+        square = sizes["gx"] == 4 and sizes["gy"] == 8 and heads == 4
+        return jax.shard_map(
+            square_shards if square else shards,
+            mesh=mesh,
+            in_specs=placed,
+            out_specs=P("gy", "gx"),
+            check_vma=False,
+        )(*arrays)
+
+    return program

time: 388 us -> 178 us (0.46)
  waiting for transfers between devices: 238 us -> 81.9 us
  blocking collectives: 61.3 us -> 11.4 us
  matrix products: 35.1 us -> 0 us
  Pallas kernels: 0 us -> 35.1 us
  starting transfers between devices: 0.39 us -> 24.1 us
  between operations: 13.7 us -> 0.43 us
  local copies, waits for them, and re-layouts: 12.7 us -> 4.35 us
  other arithmetic: 26.5 us -> 20.2 us
    reduce_scatter x3 -> x0, waiting for transfers between devices: 163 us -> none  [the longest x1 104 us: shards(): lax.psum_scatter(partial_sums, 'gx', scatter_dimension=0, tiled=True)]
    ppermute x0 -> x27, waiting for transfers between devices: none -> 81.9 us  [swap(): return lax.ppermute(value, axis, [(d, d ^ bits) for d in range(count)])]
    all_gather x2 -> x0, waiting for transfers between devices: 75.1 us -> none  [the longest x1 50.6 us: shards(): gathered = lax.all_gather(joined, 'gx', axis=0, tiled=True)]
    pallas_call x0 -> x11, Pallas kernels: none -> 35.1 us  [the longest x8 24.1 us: project(): pl.pallas_call(project_body, out_shape=jax.ShapeDtypeStruct((count, row_c...]
    dot_general x8 -> x0, matrix products: 35.1 us -> none  [the longest x1 8.79 us: shards(): jnp.dot(row_piece, up_weight, preferred_element_type=jnp.float32)]
    all_gather x3 -> x0, blocking collectives: 34.7 us -> none  [the longest x1 11.9 us: shards(): lax.all_gather(own_values, 'gx', axis=0, tiled=True)]
    ppermute x0 -> x27, starting transfers between devices: none -> 24.1 us  [swap(): return lax.ppermute(value, axis, [(d, d ^ bits) for d in range(count)])]
    pmax x1 -> x0, blocking collectives: 15.2 us -> none  [shards(): global_peak = lax.pmax(cache_peak, 'gx')]
  transfers between devices with their start and end apart: 6 -> 27, of which waited for: 5 -> 14; matrix products, arithmetic and copies ran while one was open for 5% -> 12% of each run, Pallas kernels for 0% -> 20%
where the time goes in v1:
time: 178 us
  waiting for transfers between devices  81.9 us (46%)
  Pallas kernels  35.1 us (20%)
  starting transfers between devices  24.1 us (14%)
  other arithmetic  20.2 us (11%)
  blocking collectives  11.4 us (6%)
  local copies, waits for them, and re-layouts  4.35 us (2%)
    ppermute x27, waiting for transfers between devices, swap(): return lax.ppermute(value, axis, [(d, d ^ bits) for d in range(count)])  81.9 us
    ppermute x27, starting transfers between devices, swap(): return lax.ppermute(value, axis, [(d, d ^ bits) for d in range(count)])  24.1 us
    pallas_call x8, Pallas kernels, project(): pl.pallas_call(project_body, out_shape=jax.ShapeDtypeStruct((count, row_c...  24.1 us
    psum x1, blocking collectives, square_shards(): lax.psum((jnp.sum(values32, axis=1), jnp.sum(values32 * values32, axis=1)...  11.4 us
    pallas_call x2, Pallas kernels, mix(): pl.pallas_call(mix_body, out_shape=jax.ShapeDtypeStruct((rows, columns),...  6.22 us
    pallas_call x1, Pallas kernels, attend(): pl.pallas_call(attend_body, out_shape=jax.ShapeDtypeStruct((token_count,...  4.79 us
  transfers between devices with their start and end apart: 27, of which 14 were waited for; matrix products, arithmetic and copies ran while one was open for 12% of the time, Pallas kernels for 20%

profile of v1, /device:TPU:0, one launch (start us, length us, event | category | flops | bytes accessed | tf_op | source)
XLA Modules:
  0.0 177.5 jit_solution(447187420759310179)
XLA Ops:
  1.1 11.4 %all-reduce = (f32[96]{0:T(128)S(1)}, f32[96]{0:T(128)S(1)}) all-reduce(f32[96]{0:T(128)S(1)} %get-tuple-element.6, f32[96]{0:T(128)S(1)} %get-tuple-element.5), channel_id=1, replica_groups=mesh['gx'=4,'gy'=8] {'gx'}, use_global_device_ids=true, to_apply=%region_3.0 | all-reduce | flops 192 | bytes 1536 | tf_op jit(solution)/shard_map/psum | solution.py:373
  15.2 2.6 %collective-permute-start.1 = (bf16[96,1024]{1,0:T(8,128)(2,1)S(1)}, bf16[96,1024]{1,0:T(8,128)(2,1)S(1)}, u32[]{:S(2)}, u32[]{:S(2)}) collective-permute-start(bf16[96,1024]{1,0:T(8,128)(2,1)S(1)} %fusion.23), channel_id=1, source_target_pairs={{0,4},{1,5},{2,6},{3,7},{4,0},{5,1},{6,2},{7,3},{8,12},{9,13},{10,... | collective-permute-start | bytes 589832 | tf_op jit(solution)/shard_map/ppermute | solution.py:207
  38.8 3.3 %project.11 = bf16[2,384,384]{2,1,0:T(8,128)(2,1)S(1)} custom-call(s32[2]{0:T(128)S(1)} %pad_add_fusion.2.order_ref, bf16[384,1024]{1,0:T(8,128)(2,1)} %pad_maximum_fusion.1.x_ref, bf16[1024,1536]{1,0:T(8,128)(2,1)S(1)} %copy-done.1), custom_call_target="tpu_custom_call" | custom-call | flops 603979776 | bytes 2949120 | tf_op jit(solution)/shard_map/project/pallas_call | solution.py:219
  43.3 2.9 %project.9 = bf16[2,384,512]{2,1,0:T(8,128)(2,1)S(1)} custom-call(s32[2]{0:T(128)S(1)} %pad_add_fusion.2.order_ref, bf16[384,1024]{1,0:T(8,128)(2,1)} %pad_maximum_fusion.1.x_ref, bf16[1024,2048]{1,0:T(8,128)(2,1)S(1)} %copy-done), custom_call_target="tpu_custom_call" | custom-call | flops 805306368 | bytes 3670016 | tf_op jit(solution)/shard_map/project/pallas_call | solution.py:219
  48.3 2.9 %project.15 = bf16[2,384,512]{2,1,0:T(8,128)(2,1)S(1)} custom-call(s32[2]{0:T(128)S(1)} %pad_add_fusion.4.order_ref, bf16[384,1024]{1,0:T(8,128)(2,1)} %collective-permute-done.9.x_ref, bf16[1024,2048]{1,0:T(8,128)(2,1)S(1)} %copy-done), custom_call_target="tpu_custom_call" | custom-call | flops 805306368 | bytes 3670016 | tf_op jit(solution)/shard_map/project/pallas_call | solution.py:219
  51.9 3.0 %project.10 = f32[2,384,384]{2,1,0:T(8,128)S(1)} custom-call(s32[2]{0:T(128)S(1)} %pad_add_fusion.1.order_ref, bf16[384,1024]{1,0:T(8,128)(2,1)} %pad_maximum_fusion.1.x_ref, bf16[1024,1536]{1,0:T(8,128)(2,1)S(1)} %copy-done.1), custom_call_target="tpu_custom_call" | custom-call | flops 603979776 | bytes 3538944 | tf_op jit(solution)/shard_map/project/pallas_call | solution.py:219
  54.8 2.9 %project.8 = f32[2,384,512]{2,1,0:T(8,128)S(1)} custom-call(s32[2]{0:T(128)S(1)} %pad_add_fusion.1.order_ref, bf16[384,1024]{1,0:T(8,128)(2,1)} %pad_maximum_fusion.1.x_ref, bf16[1024,2048]{1,0:T(8,128)(2,1)S(1)} %copy-done), custom_call_target="tpu_custom_call" | custom-call | flops 805306368 | bytes 4456448 | tf_op jit(solution)/shard_map/project/pallas_call | solution.py:219
  59.5 3.0 %project.13 = bf16[2,384,384]{2,1,0:T(8,128)(2,1)S(1)} custom-call(s32[2]{0:T(128)S(1)} %pad_add_fusion.4.order_ref, bf16[384,1024]{1,0:T(8,128)(2,1)} %collective-permute-done.9.x_ref, bf16[1024,1536]{1,0:T(8,128)(2,1)S(1)} %copy-done.1), custom_call_target="tpu_custom_call" | custom-call | flops 603979776 | bytes 2949120 | tf_op jit(solution)/shard_map/project/pallas_call | solution.py:219
  63.5 2.9 %project.14 = f32[2,384,512]{2,1,0:T(8,128)S(1)} custom-call(s32[2]{0:T(128)S(1)} %copy-done.6, bf16[384,1024]{1,0:T(8,128)(2,1)} %collective-permute-done.9.x_ref, bf16[1024,2048]{1,0:T(8,128)(2,1)S(1)} %copy-done), custom_call_target="tpu_custom_call" | custom-call | flops 805306368 | bytes 4456448 | tf_op jit(solution)/shard_map/project/pallas_call | solution.py:219
  66.5 5.3 %collective-permute-done.17 = bf16[2,384,512]{2,1,0:T(8,128)(2,1)S(1)} collective-permute-done((bf16[2,384,512]{2,1,0:T(8,128)(2,1)S(1)}, bf16[2,384,512]{2,1,0:T(8,128)(2,1)S(1)}, u32[]{:S(2)}, u32[]{:S(2)}) %collective-permute-start.17) | collective-permute-done | bytes 786464 | tf_op jit(solution)/shard_map/ppermute | solution.py:207
  72.1 3.0 %collective-permute-done.3 = bf16[2,384,512]{2,1,0:T(8,128)(2,1)S(1)} collective-permute-done((bf16[2,384,512]{2,1,0:T(8,128)(2,1)S(1)}, bf16[2,384,512]{2,1,0:T(8,128)(2,1)S(1)}, u32[]{:S(2)}, u32[]{:S(2)}) %collective-permute-start.3) | collective-permute-done | bytes 786464 | tf_op jit(solution)/shard_map/ppermute | solution.py:207
  76.1 3.1 %project.12 = f32[2,384,384]{2,1,0:T(8,128)S(1)} custom-call(s32[2]{0:T(128)S(1)} %copy-done.6, bf16[384,1024]{1,0:T(8,128)(2,1)} %collective-permute-done.9.x_ref, bf16[1024,1536]{1,0:T(8,128)(2,1)S(1)} %copy-done.1), custom_call_target="tpu_custom_call" | custom-call | flops 603979776 | bytes 3538944 | tf_op jit(solution)/shard_map/project/pallas_call | solution.py:219
  79.2 3.9 %collective-permute-done.18 = bf16[384,512]{1,0:T(8,128)(2,1)S(1)} collective-permute-done((bf16[384,512]{1,0:T(8,128)(2,1)S(1)}, bf16[384,512]{1,0:T(8,128)(2,1)S(1)}, u32[]{:S(2)}, u32[]{:S(2)}) %collective-permute-start.18) | collective-permute-done | bytes 393248 | tf_op jit(solution)/shard_map/ppermute | solution.py:207
  85.5 5.2 %collective-permute-done.10 = bf16[2,384,384]{2,1,0:T(8,128)(2,1)S(1)} collective-permute-done((bf16[2,384,384]{2,1,0:T(8,128)(2,1)S(1)}, bf16[2,384,384]{2,1,0:T(8,128)(2,1)S(1)}, u32[]{:S(2)}, u32[]{:S(2)}) %collective-permute-start.10) | collective-permute-done | bytes 589856 | tf_op jit(solution)/shard_map/ppermute | solution.py:207
  90.9 15.6 %collective-permute-done.19.h1 = bf16[384,512]{1,0:T(8,128)(2,1)S(1)} collective-permute-done((bf16[384,512]{1,0:T(8,128)(2,1)S(1)}, bf16[384,512]{1,0:T(8,128)(2,1)S(1)}, u32[]{:S(2)}, u32[]{:S(2)}) %collective-permute-start.19) | collective-permute-done | bytes 393248 | tf_op jit(solution)/shard_map/ppermute | solution.py:207
  110.5 4.8 %attend.1 = bf16[768,128]{1,0:T(8,128)(2,1)S(1)} custom-call(f32[2,384,384]{2,1,0:T(8,128)S(1)} %convert_add_fusion.4.sum_a, bf16[384,384]{1,0:T(8,128)(2,1)S(1)} %collective-permute-done.8.got_a, f32[2,384,384]{2,1,0:T(8,128)S(1)} %convert_add_fusion.3.sum_b, bf16[384,384]{1,0:T(8,128)(2,1)S(1)} %collective-permute-done.11.got_b, ...), custom_call_target="tpu_custom_call" | custom-call | flops 654311424 | bytes 3145728 | tf_op jit(solution)/shard_map/attend/pallas_call | solution.py:304
  116.0 4.1 %collective-permute-done.21.c1 = bf16[384,128]{1,0:T(8,128)(2,1)S(1)} collective-permute-done((bf16[384,128]{1,0:T(8,128)(2,1)S(1)}, bf16[384,128]{1,0:T(8,128)(2,1)S(1)}, u32[]{:S(2)}, u32[]{:S(2)}) %collective-permute-start.21) | collective-permute-done | bytes 98336 | tf_op jit(solution)/shard_map/ppermute | solution.py:207
  120.6 15.0 %collective-permute-done.5.h1 = bf16[384,512]{1,0:T(8,128)(2,1)S(1)} collective-permute-done((bf16[384,512]{1,0:T(8,128)(2,1)S(1)}, bf16[384,512]{1,0:T(8,128)(2,1)S(1)}, u32[]{:S(2)}, u32[]{:S(2)}) %collective-permute-start.5) | collective-permute-done | bytes 393248 | tf_op jit(solution)/shard_map/ppermute | solution.py:207
  137.9 3.1 %mix.3 = bf16[384,1024]{1,0:T(8,128)(2,1)S(1)} custom-call(s32[4]{0:T(128)S(1)} %pad_add_fusion.5.order_ref, bf16[384,512]{1,0:T(8,128)(2,1)S(1)} %fusion.5.h0, bf16[384,512]{1,0:T(8,128)(2,1)S(1)} %collective-permute-done.19.h1, bf16[2,384,512]{2,1,0:T(8,128)(2,1)S(1)} %collective-permute-done.20.h2, bf16[384,128]{1,0:T(8,128)(2,1)S(1)} %get-tuple-element.26.c0, ...), custom_call_target="tpu_custom_call" | custom-call | flops 2013265920 | bytes 7995392 | tf_op jit(solution)/shard_map/mix/pallas_call | solution.py:340
  141.8 4.5 %collective-permute-done.15.c1 = bf16[384,128]{1,0:T(8,128)(2,1)S(1)} collective-permute-done((bf16[384,128]{1,0:T(8,128)(2,1)S(1)}, bf16[384,128]{1,0:T(8,128)(2,1)S(1)}, u32[]{:S(2)}, u32[]{:S(2)}) %collective-permute-start.15) | collective-permute-done | bytes 98336 | tf_op jit(solution)/shard_map/ppermute | solution.py:207
  146.9 8.7 %collective-permute-done.16.c2 = bf16[2,384,128]{2,1,0:T(8,128)(2,1)S(1)} collective-permute-done((bf16[2,384,128]{2,1,0:T(8,128)(2,1)S(1)}, bf16[2,384,128]{2,1,0:T(8,128)(2,1)S(1)}, u32[]{:S(2)}, u32[]{:S(2)}) %collective-permute-start.16) | collective-permute-done | bytes 196640 | tf_op jit(solution)/shard_map/ppermute | solution.py:207
  155.6 3.1 %mix.2 = f32[384,1024]{1,0:T(8,128)S(1)} custom-call(s32[4]{0:T(128)S(1)} %copy-done.5, bf16[384,512]{1,0:T(8,128)(2,1)S(1)} %fusion.2.h0, bf16[384,512]{1,0:T(8,128)(2,1)S(1)} %collective-permute-done.5.h1, bf16[2,384,512]{2,1,0:T(8,128)(2,1)S(1)} %collective-permute-done.6.h2, bf16[384,128]{1,0:T(8,128)(2,1)S(1)} %get-tuple-element.27.c0, ...), custom_call_target="tpu_custom_call" | custom-call | flops 2013265920 | bytes 7995392 | tf_op jit(solution)/shard_map/mix/pallas_call | solution.py:340
  163.8 2.8 %collective-permute-done.24 = bf16[96,1024]{1,0:T(8,128)(2,1)S(1)} collective-permute-done((bf16[96,1024]{1,0:T(8,128)(2,1)S(1)}, bf16[96,1024]{1,0:T(8,128)(2,1)S(1)}, u32[]{:S(2)}, u32[]{:S(2)}) %collective-permute-start.24) | collective-permute-done | bytes 196640 | tf_op jit(solution)/shard_map/ppermute | solution.py:207
  166.6 10.0 %collective-permute-done.25 = bf16[96,1024]{1,0:T(8,128)(2,1)S(1)} collective-permute-done((bf16[96,1024]{1,0:T(8,128)(2,1)S(1)}, bf16[96,1024]{1,0:T(8,128)(2,1)S(1)}, u32[]{:S(2)}, u32[]{:S(2)}) %collective-permute-start.25) | collective-permute-done | bytes 196640 | tf_op jit(solution)/shard_map/ppermute | solution.py:207
  (126 shorter events, 50.0 us)
Async XLA Ops:
  13.6 13.1 %collective-permute-start = (bf16[96,1024]{1,0:T(8,128)(2,1)S(1)}, bf16[96,1024]{1,0:T(8,128)(2,1)S(1)}, u32[]{:S(2)}, u32[]{:S(2)}) collective-permute-start(bf16[96,1024]{1,0:T(8,128)(2,1)S(1)} %fusion.23), channel_id=1, source_target_pairs={{0,2},{1,3},{2,0},{3,1},{4,6},{5,7},{6,4},{7,5},{8,10},{9,11},{10,... | collective-permute-start | bytes 589832 | tf_op jit(solution)/shard_map/ppermute | solution.py:207
  15.2 15.8 %collective-permute-start.1 = (bf16[96,1024]{1,0:T(8,128)(2,1)S(1)}, bf16[96,1024]{1,0:T(8,128)(2,1)S(1)}, u32[]{:S(2)}, u32[]{:S(2)}) collective-permute-start(bf16[96,1024]{1,0:T(8,128)(2,1)S(1)} %fusion.23), channel_id=1, source_target_pairs={{0,4},{1,5},{2,6},{3,7},{4,0},{5,1},{6,2},{7,3},{8,12},{9,13},{10,... | collective-permute-start | bytes 589832 | tf_op jit(solution)/shard_map/ppermute | solution.py:207
  17.8 13.9 %collective-permute-start.2 = (bf16[96,1024]{1,0:T(8,128)(2,1)S(1)}, bf16[96,1024]{1,0:T(8,128)(2,1)}, u32[]{:S(2)}, u32[]{:S(2)}) collective-permute-start(bf16[96,1024]{1,0:T(8,128)(2,1)S(1)} %fusion.23), channel_id=1, source_target_pairs={{0,6},{1,7},{2,4},{3,5},{4,2},{5,3},{6,0},{7,1},{8,14},{9,15},{10,... | collective-permute-start | bytes 589832 | tf_op jit(solution)/shard_map/ppermute | solution.py:207
  19.9 22.3 %collective-permute-start.12 = (bf16[2,224,128]{2,1,0:T(8,128)(2,1)}, bf16[2,224,128]{2,1,0:T(8,128)(2,1)}, u32[]{:S(2)}, u32[]{:S(2)}) collective-permute-start(bf16[2,224,128]{2,1,0:T(8,128)(2,1)} %get-tuple-element.19), channel_id=1, source_target_pairs={{0,8},{8,0},{16,24},{24,16},{1,9},{9,1},{17,25},{25,17},{2,10},{10... | collective-permute-start | bytes 344072 | tf_op jit(solution)/shard_map/ppermute | solution.py:207
  19.9 22.3 %collective-permute-start.13 = (bf16[2,224,128]{2,1,0:T(8,128)(2,1)}, bf16[2,224,128]{2,1,0:T(8,128)(2,1)}, u32[]{:S(2)}, u32[]{:S(2)}) collective-permute-start(bf16[2,224,128]{2,1,0:T(8,128)(2,1)} %get-tuple-element.20), channel_id=1, source_target_pairs={{0,16},{8,24},{16,0},{24,8},{1,17},{9,25},{17,1},{25,9},{2,18},{10... | collective-permute-start | bytes 344072 | tf_op jit(solution)/shard_map/ppermute | solution.py:207
  26.7 15.4 %collective-permute-start.14 = (bf16[2,224,128]{2,1,0:T(8,128)(2,1)}, bf16[2,224,128]{2,1,0:T(8,128)(2,1)}, u32[]{:S(2)}, u32[]{:S(2)}) collective-permute-start(bf16[2,224,128]{2,1,0:T(8,128)(2,1)} %get-tuple-element.21), channel_id=1, source_target_pairs={{0,24},{8,16},{16,8},{24,0},{1,25},{9,17},{17,9},{25,1},{2,26},{10... | collective-permute-start | bytes 344072 | tf_op jit(solution)/shard_map/ppermute | solution.py:207
  33.8 14.5 %collective-permute-start.9 = (bf16[384,1024]{1,0:T(8,128)(2,1)}, bf16[384,1024]{1,0:T(8,128)(2,1)}, u32[]{:S(2)}, u32[]{:S(2)}) collective-permute-start(bf16[384,1024]{1,0:T(8,128)(2,1)} %pad_maximum_fusion.1.x_ref), channel_id=1, source_target_pairs={{0,1},{1,0},{2,3},{3,2},{4,5},{5,4},{6,7},{7,6},{8,9},{9,8},{10,11... | collective-permute-start | bytes 2359304 | tf_op jit(solution)/shard_map/ppermute | solution.py:207
  42.1 16.2 %collective-permute-start.7 = (bf16[2,384,384]{2,1,0:T(8,128)(2,1)S(1)}, bf16[2,384,384]{2,1,0:T(8,128)(2,1)S(1)}, u32[]{:S(2)}, u32[]{:S(2)}) collective-permute-start(bf16[2,384,384]{2,1,0:T(8,128)(2,1)S(1)} %project.11), channel_id=1, source_target_pairs={{0,8},{8,0},{16,24},{24,16},{1,9},{9,1},{17,25},{25,17},{2,10},{10... | collective-permute-start | bytes 1769480 | tf_op jit(solution)/shard_map/ppermute | solution.py:207
  46.2 28.9 %collective-permute-start.3 = (bf16[2,384,512]{2,1,0:T(8,128)(2,1)S(1)}, bf16[2,384,512]{2,1,0:T(8,128)(2,1)S(1)}, u32[]{:S(2)}, u32[]{:S(2)}) collective-permute-start(bf16[2,384,512]{2,1,0:T(8,128)(2,1)S(1)} %project.9), channel_id=1, source_target_pairs={{0,8},{8,0},{16,24},{24,16},{1,9},{9,1},{17,25},{25,17},{2,10},{10... | collective-permute-start | bytes 2359304 | tf_op jit(solution)/shard_map/ppermute | solution.py:207
  51.3 20.5 %collective-permute-start.17 = (bf16[2,384,512]{2,1,0:T(8,128)(2,1)S(1)}, bf16[2,384,512]{2,1,0:T(8,128)(2,1)S(1)}, u32[]{:S(2)}, u32[]{:S(2)}) collective-permute-start(bf16[2,384,512]{2,1,0:T(8,128)(2,1)S(1)} %project.15), channel_id=1, source_target_pairs={{0,16},{8,24},{16,0},{24,8},{1,17},{9,25},{17,1},{25,9},{2,18},{10... | collective-permute-start | bytes 2359304 | tf_op jit(solution)/shard_map/ppermute | solution.py:207
  58.4 52.1 %collective-permute-start.8 = (bf16[384,384]{1,0:T(8,128)(2,1)S(1)}, bf16[384,384]{1,0:T(8,128)(2,1)S(1)}, u32[]{:S(2)}, u32[]{:S(2)}) collective-permute-start(bf16[384,384]{1,0:T(8,128)(2,1)S(1)} %fusion.30), channel_id=1, source_target_pairs={{0,16},{8,24},{16,0},{24,8},{1,17},{9,25},{17,1},{25,9},{2,18},{10... | collective-permute-start | bytes 884744 | tf_op jit(solution)/shard_map/ppermute | solution.py:207
  62.5 28.2 %collective-permute-start.10 = (bf16[2,384,384]{2,1,0:T(8,128)(2,1)S(1)}, bf16[2,384,384]{2,1,0:T(8,128)(2,1)S(1)}, u32[]{:S(2)}, u32[]{:S(2)}) collective-permute-start(bf16[2,384,384]{2,1,0:T(8,128)(2,1)S(1)} %project.13), channel_id=1, source_target_pairs={{0,16},{8,24},{16,0},{24,8},{1,17},{9,25},{17,1},{25,9},{2,18},{10... | collective-permute-start | bytes 1769480 | tf_op jit(solution)/shard_map/ppermute | solution.py:207
  72.1 11.1 %collective-permute-start.18 = (bf16[384,512]{1,0:T(8,128)(2,1)S(1)}, bf16[384,512]{1,0:T(8,128)(2,1)S(1)}, u32[]{:S(2)}, u32[]{:S(2)}) collective-permute-start(bf16[384,512]{1,0:T(8,128)(2,1)S(1)} %fusion.29), channel_id=1, source_target_pairs={{0,8},{8,0},{16,24},{24,16},{1,9},{9,1},{17,25},{25,17},{2,10},{10... | collective-permute-start | bytes 1179656 | tf_op jit(solution)/shard_map/ppermute | solution.py:207
  75.4 31.6 %collective-permute-start.4 = (bf16[384,512]{1,0:T(8,128)(2,1)S(1)}, bf16[384,512]{1,0:T(8,128)(2,1)S(1)}, u32[]{:S(2)}, u32[]{:S(2)}) collective-permute-start(bf16[384,512]{1,0:T(8,128)(2,1)S(1)} %fusion.28), channel_id=1, source_target_pairs={{0,16},{8,24},{16,0},{24,8},{1,17},{9,25},{17,1},{25,9},{2,18},{10... | collective-permute-start | bytes 1179656 | tf_op jit(solution)/shard_map/ppermute | solution.py:207
  84.9 21.6 %collective-permute-start.19 = (bf16[384,512]{1,0:T(8,128)(2,1)S(1)}, bf16[384,512]{1,0:T(8,128)(2,1)S(1)}, u32[]{:S(2)}, u32[]{:S(2)}) collective-permute-start(bf16[384,512]{1,0:T(8,128)(2,1)S(1)} %fusion.5.h0), channel_id=1, source_target_pairs={{0,16},{8,24},{16,0},{24,8},{1,17},{9,25},{17,1},{25,9},{2,18},{10... | collective-permute-start | bytes 1179656 | tf_op jit(solution)/shard_map/ppermute | solution.py:207
  90.8 19.7 %collective-permute-start.11 = (bf16[384,384]{1,0:T(8,128)(2,1)S(1)}, bf16[384,384]{1,0:T(8,128)(2,1)S(1)}, u32[]{:S(2)}, u32[]{:S(2)}) collective-permute-start(bf16[384,384]{1,0:T(8,128)(2,1)S(1)} %fusion.31), channel_id=1, source_target_pairs={{0,8},{8,0},{16,24},{24,16},{1,9},{9,1},{17,25},{25,17},{2,10},{10... | collective-permute-start | bytes 884744 | tf_op jit(solution)/shard_map/ppermute | solution.py:207
  106.6 31.2 %collective-permute-start.20 = (bf16[2,384,512]{2,1,0:T(8,128)(2,1)S(1)}, bf16[2,384,512]{2,1,0:T(8,128)(2,1)S(1)}, u32[]{:S(2)}, u32[]{:S(2)}) collective-permute-start(bf16[2,384,512]{2,1,0:T(8,128)(2,1)S(1)} %pad_maximum_fusion.3), channel_id=1, source_target_pairs={{0,8},{8,0},{16,24},{24,16},{1,9},{9,1},{17,25},{25,17},{2,10},{10... | collective-permute-start | bytes 2359304 | tf_op jit(solution)/shard_map/ppermute | solution.py:207
  108.7 26.8 %collective-permute-start.5 = (bf16[384,512]{1,0:T(8,128)(2,1)S(1)}, bf16[384,512]{1,0:T(8,128)(2,1)S(1)}, u32[]{:S(2)}, u32[]{:S(2)}) collective-permute-start(bf16[384,512]{1,0:T(8,128)(2,1)S(1)} %fusion.2.h0), channel_id=1, source_target_pairs={{0,8},{8,0},{16,24},{24,16},{1,9},{9,1},{17,25},{25,17},{2,10},{10... | collective-permute-start | bytes 1179656 | tf_op jit(solution)/shard_map/ppermute | solution.py:207
  120.1 17.7 %collective-permute-start.22 = (bf16[2,384,128]{2,1,0:T(8,128)(2,1)S(1)}, bf16[2,384,128]{2,1,0:T(8,128)(2,1)S(1)}, u32[]{:S(2)}, u32[]{:S(2)}) collective-permute-start(bf16[2,384,128]{2,1,0:T(8,128)(2,1)S(1)} %pad_maximum_fusion.6), channel_id=1, source_target_pairs={{0,8},{8,0},{16,24},{24,16},{1,9},{9,1},{17,25},{25,17},{2,10},{10... | collective-permute-start | bytes 589832 | tf_op jit(solution)/shard_map/ppermute | solution.py:207
  135.7 20.0 %collective-permute-start.6 = (bf16[2,384,512]{2,1,0:T(8,128)(2,1)S(1)}, bf16[2,384,512]{2,1,0:T(8,128)(2,1)S(1)}, u32[]{:S(2)}, u32[]{:S(2)}) collective-permute-start(bf16[2,384,512]{2,1,0:T(8,128)(2,1)S(1)} %pad_maximum_fusion.2), channel_id=1, source_target_pairs={{0,16},{8,24},{16,0},{24,8},{1,17},{9,25},{17,1},{25,9},{2,18},{10... | collective-permute-start | bytes 2359304 | tf_op jit(solution)/shard_map/ppermute | solution.py:207
  141.0 17.8 %collective-permute-start.23 = (bf16[384,1024]{1,0:T(8,128)(2,1)S(1)}, bf16[384,1024]{1,0:T(8,128)(2,1)S(1)}, u32[]{:S(2)}, u32[]{:S(2)}) collective-permute-start(bf16[384,1024]{1,0:T(8,128)(2,1)S(1)} %mix.3), channel_id=1, source_target_pairs={{0,1},{1,0},{2,3},{3,2},{4,5},{5,4},{6,7},{7,6},{8,9},{9,8},{10,11... | collective-permute-start | bytes 2359304 | tf_op jit(solution)/shard_map/ppermute | solution.py:207
  146.3 9.3 %collective-permute-start.16 = (bf16[2,384,128]{2,1,0:T(8,128)(2,1)S(1)}, bf16[2,384,128]{2,1,0:T(8,128)(2,1)S(1)}, u32[]{:S(2)}, u32[]{:S(2)}) collective-permute-start(bf16[2,384,128]{2,1,0:T(8,128)(2,1)S(1)} %pad_maximum_fusion.5), channel_id=1, source_target_pairs={{0,16},{8,24},{16,0},{24,8},{1,17},{9,25},{17,1},{25,9},{2,18},{10... | collective-permute-start | bytes 589832 | tf_op jit(solution)/shard_map/ppermute | solution.py:207
  161.3 15.4 %collective-permute-start.25 = (bf16[96,1024]{1,0:T(8,128)(2,1)S(1)}, bf16[96,1024]{1,0:T(8,128)(2,1)S(1)}, u32[]{:S(2)}, u32[]{:S(2)}) collective-permute-start(bf16[96,1024]{1,0:T(8,128)(2,1)S(1)} %get-tuple-element.15), channel_id=1, source_target_pairs={{0,4},{1,5},{2,6},{3,7},{4,0},{5,1},{6,2},{7,3},{8,12},{9,13},{10,... | collective-permute-start | bytes 589832 | tf_op jit(solution)/shard_map/ppermute | solution.py:207
  162.4 14.2 %collective-permute-start.26 = (bf16[96,1024]{1,0:T(8,128)(2,1)S(1)}, bf16[96,1024]{1,0:T(8,128)(2,1)S(1)}, u32[]{:S(2)}, u32[]{:S(2)}) collective-permute-start(bf16[96,1024]{1,0:T(8,128)(2,1)S(1)} %get-tuple-element.14), channel_id=1, source_target_pairs={{0,6},{1,7},{2,4},{3,5},{4,2},{5,3},{6,0},{7,1},{8,14},{9,15},{10,... | collective-permute-start | bytes 589832 | tf_op jit(solution)/shard_map/ppermute | solution.py:207
  (16 other events, 194.6 us)

commit v2 on v1

--- a/solution.py
+++ b/solution.py
@@ -202,41 +202,58 @@
     return values32 + mixed_sum
 
 
+CHUNKS = ((0, 1), (1, 2), (2, 4))
+
+
 def swap(value, axis, bits):
     count = lax.axis_size(axis)
     return lax.ppermute(value, axis, [(d, d ^ bits) for d in range(count)])
 
 
-def project_body(order_ref, x_ref, w_ref, out_ref):
-    out_ref[0] = jnp.dot(x_ref[...], w_ref[...], preferred_element_type=jnp.float32).astype(
-        out_ref.dtype
-    )
-
-
-def project(rows, weight, order, width, dtype):
-    count = order.shape[0]
-    row_count, depth = rows.shape
+def after(value, *others):
+    return lax.optimization_barrier((value, *others))[0]
+
+
+def whole(count):
+    return [pl.BlockSpec(memory_space=pltpu.VMEM)] * count
+
+
+def project_body(plan, widths, row_sets, order_ref, *refs):
+    rows, refs = refs[:row_sets], refs[row_sets:]
+    weights, outs = refs[: len(widths)], refs[len(widths) :]
+    for out, blocks in zip(outs, plan):
+        for place, (which, slot) in enumerate(blocks):
+            low = 0
+            for weight, width in zip(weights, widths):
+                start = pl.multiple_of(order_ref[slot] * width, 128)
+                out[place, :, low : low + width] = jnp.dot(
+                    rows[which][...],
+                    weight[:, pl.ds(start, width)],
+                    preferred_element_type=jnp.float32,
+                ).astype(out.dtype)
+                low += width
+
+
+def project(rows, weights, order, plan, dtype):
+    row_count, depth = rows[0].shape
+    widths = tuple(w.shape[1] // order.shape[0] for w in weights)
+    count = sum(len(blocks) for blocks in plan)
     return pl.pallas_call(
-        project_body,
-        out_shape=jax.ShapeDtypeStruct((count, row_count, width), dtype),
-        grid_spec=pltpu.PrefetchScalarGridSpec(
-            num_scalar_prefetch=1,
-            grid=(count,),
-            in_specs=[
-                pl.BlockSpec((row_count, depth), lambda g, o: (0, 0)),
-                pl.BlockSpec((depth, width), lambda g, o: (0, o[g])),
-            ],
-            out_specs=pl.BlockSpec((1, row_count, width), lambda g, o: (g, 0, 0)),
-        ),
+        functools.partial(project_body, plan, widths, len(rows)),
+        out_shape=[
+            jax.ShapeDtypeStruct((len(blocks), row_count, sum(widths)), dtype) for blocks in plan
+        ],
+        in_specs=[pl.BlockSpec(memory_space=pltpu.SMEM)] + whole(len(rows) + len(weights)),
+        out_specs=whole(len(plan)),
         cost_estimate=pl.CostEstimate(
-            flops=2 * count * row_count * depth * width,
-            bytes_accessed=2 * (row_count * depth + count * depth * width)
-            + count * row_count * width * jnp.dtype(dtype).itemsize,
+            flops=2 * count * row_count * depth * sum(widths),
+            bytes_accessed=2 * (len(rows) * row_count * depth + count * depth * sum(widths))
+            + count * row_count * sum(widths) * jnp.dtype(dtype).itemsize,
             transcendentals=0,
         ),
         compiler_params=pltpu.CompilerParams(vmem_limit_bytes=24 << 20),
         name="project",
-    )(order, rows, weight)
+    )(order, *rows, *weights)
 
 
 def turn(vectors, cosine, sine_up, sine_down):
@@ -248,30 +265,29 @@
     )
 
 
-def attend_body(
-    sum_a, got_a, sum_b, got_b, tables, keys_old, values_old, per_query, per_new, per_old, out_ref,
-    query_s, key_s, value_s,
-):
-    half_rows = got_a.shape[0]
+def attend_body(offsets, tile, *refs):
+    count = 2 * len(offsets)
+    pairs, refs = refs[:count], refs[count:]
+    tables, keys_old, values_old, per_query, per_new, per_old, out_a, out_b = refs[:8]
+    query_s, key_s, value_s = refs[8:]
+    half_rows = out_a.shape[0]
     scale = HD ** (-0.5)
-    for half, (total, got) in enumerate(((sum_a, got_a), (sum_b, got_b))):
-        span = pl.ds(half * half_rows, half_rows)
+    for section, offset in enumerate(offsets):
+        total, got = pairs[2 * section : 2 * section + 2]
+        span = pl.ds(offset, got.shape[0])
         cosine, up, down = (tables[t, span, :] for t in range(3))
         parts = [
-            total[0, :, p * HD : (p + 1) * HD].astype(jnp.float32)
-            + got[:, p * HD : (p + 1) * HD].astype(jnp.float32)
+            total[0, :, p * HD : (p + 1) * HD] + got[:, p * HD : (p + 1) * HD].astype(jnp.float32)
             for p in range(3)
         ]
         query_s[span, :] = turn(parts[0], cosine, up, down).astype(jnp.bfloat16)
         key_s[span, :] = turn(parts[1], cosine, up, down).astype(jnp.bfloat16)
         value_s[span, :] = parts[2].astype(jnp.bfloat16)
-    tile = 128
     across = (((1,), (1,)), ((), ()))
-
-    def visit(step, unused):
-        rows = pl.ds(pl.multiple_of(step * tile, tile), tile)
-        query = query_s[rows, :]
-        numbers = per_query[rows, :]
+    for offset in range(0, 2 * half_rows, tile):
+        span = pl.ds(offset, tile)
+        query = query_s[span, :]
+        numbers = per_query[span, :]
         token, first, prefix = numbers[:, 0:1], numbers[:, 1:2], numbers[:, 2:3]
         cached = (
             lax.dot_general(query, keys_old[...], across, preferred_element_type=jnp.float32)
@@ -292,20 +308,19 @@
         context = jnp.dot(
             cached.astype(jnp.bfloat16), values_old[...], preferred_element_type=jnp.float32
         ) + jnp.dot(recent.astype(jnp.bfloat16), value_s[...], preferred_element_type=jnp.float32)
-        out_ref[rows, :] = (context / total).astype(jnp.bfloat16)
-        return unused
-
-    lax.fori_loop(0, query_s.shape[0] // tile, visit, 0)
-
-
-def attend(sum_a, got_a, sum_b, got_b, tables, keys_old, values_old, per_query, per_new, per_old):
+        out = out_a if offset < half_rows else out_b
+        out[pl.ds(offset % half_rows, tile), :] = (context / total).astype(jnp.bfloat16)
+
+
+def attend(offsets, pairs, tables, keys_old, values_old, per_query, per_new, per_old):
     token_count = per_query.shape[0]
     keys = token_count + keys_old.shape[0]
+    half = jax.ShapeDtypeStruct((token_count // 2, HD), jnp.bfloat16)
     return pl.pallas_call(
-        attend_body,
-        out_shape=jax.ShapeDtypeStruct((token_count, HD), jnp.bfloat16),
-        in_specs=[pl.BlockSpec(memory_space=pltpu.VMEM)] * 10,
-        out_specs=pl.BlockSpec(memory_space=pltpu.VMEM),
+        functools.partial(attend_body, offsets, token_count // 4),
+        out_shape=[half, half],
+        in_specs=whole(len(pairs) + 6),
+        out_specs=whole(2),
         scratch_shapes=[pltpu.VMEM((token_count, HD), jnp.bfloat16)] * 3,
         cost_estimate=pl.CostEstimate(
             flops=4 * token_count * keys * HD,
@@ -314,16 +329,18 @@
         ),
         compiler_params=pltpu.CompilerParams(vmem_limit_bytes=32 << 20),
         name="attend",
-    )(sum_a, got_a, sum_b, got_b, tables, keys_old, values_old, per_query, per_new, per_old)
-
-
-def mix_body(order_ref, h0, h1, h2, c0, c1, c2, down_ref, out_w_ref, out_ref):
-    width, head = h0.shape[1], c0.shape[1]
+    )(*pairs, tables, keys_old, values_old, per_query, per_new, per_old)
+
+
+def mix_body(slots, offset, order_ref, h0, h1, h2, c0, c1, c2, down_ref, out_w_ref, out_ref):
+    rows, width = h0.shape
+    head = c0.shape[1]
+    span = pl.ds(offset, rows)
     hidden = (h0[...], h1[...], h2[0], h2[1])
-    context = (c0[...], c1[...], c2[0], c2[1])
+    context = (c0[span, :], c1[span, :], c2[0, span, :], c2[1, span, :])
     total = None
-    for m in range(4):
-        block = order_ref[m]
+    for m, slot in enumerate(slots):
+        block = order_ref[slot]
         down = down_ref[pl.ds(pl.multiple_of(block * width, width), width), :]
         out = out_w_ref[pl.ds(pl.multiple_of(block * head, head), head), :]
         term = jnp.dot(hidden[m], down, preferred_element_type=jnp.float32) + jnp.dot(
@@ -333,15 +350,14 @@
     out_ref[...] = total.astype(out_ref.dtype)
 
 
-def mix(order, hidden, context, down_weight, out_weight, dtype):
+def mix(order, slots, offset, hidden, context, down_weight, out_weight, dtype):
     rows = hidden[0].shape[0]
     columns = down_weight.shape[1]
     depth = down_weight.shape[0] + out_weight.shape[0]
     return pl.pallas_call(
-        mix_body,
+        functools.partial(mix_body, slots, offset),
         out_shape=jax.ShapeDtypeStruct((rows, columns), dtype),
-        in_specs=[pl.BlockSpec(memory_space=pltpu.SMEM)]
-        + [pl.BlockSpec(memory_space=pltpu.VMEM)] * 8,
+        in_specs=[pl.BlockSpec(memory_space=pltpu.SMEM)] + whole(8),
         out_specs=pl.BlockSpec(memory_space=pltpu.VMEM),
         cost_estimate=pl.CostEstimate(
             flops=2 * rows * depth * columns,
@@ -363,21 +379,28 @@
     local_rows = stream.shape[0]
     feature_count = stream.shape[1] * groups
     token_count = local_rows * lax.axis_size("gy")
-    half_rows = token_count // 2
     block_len = cache_keys.shape[0]
     prefix_len = block_len * groups // 2
     head_width = qkv_weight.shape[1] // groups
     hidden_width = up_weight.shape[1] // groups
+    slot = jnp.arange(groups, dtype=jnp.int32)
+    order = own ^ slot
 
     values32 = stream.astype(jnp.float32)
-    moments = lax.psum((jnp.sum(values32, axis=1), jnp.sum(values32 * values32, axis=1)), "gx")
-    average = (moments[0] / feature_count)[:, None]
-    square = (moments[1] / feature_count)[:, None]
+    moments = jnp.stack([jnp.sum(values32, axis=1), jnp.sum(values32 * values32, axis=1)])
+    moments = moments + swap(moments, "gx", 1) + (swap(moments, "gx", 2) + swap(moments, "gx", 3))
+    moments = moments / feature_count
+    average = moments[0][:, None]
+    square = moments[1][:, None]
     normed = ((values32 - average) * lax.rsqrt(square - average * average + epsilon)).astype(
         jnp.bfloat16
     )
-    rows_a = jnp.concatenate([normed] + [swap(normed, "gy", 2 * k) for k in range(1, 4)], axis=0)
-    rows_b = swap(rows_a, "gy", 1)
+    near = [normed, swap(normed, "gy", 2), swap(normed, "gy", 4)]
+    near.append(swap(near[2], "gy", 2))
+    rows = []
+    for low, high in CHUNKS:
+        rows_a = jnp.concatenate(near[low:high], axis=0) if high - low > 1 else near[low]
+        rows.append((rows_a, swap(rows_a, "gy", 1)))
 
     old = jnp.stack([cache_keys, cache_values])
     pieces = []
@@ -386,19 +409,14 @@
         pieces.append(swap(piece, "gx", m) if m else piece)
     old = jnp.concatenate(pieces, axis=1)
 
-    token_ids, segment, offsets, member = token_layout(request_lengths, token_count)
-    block = jnp.arange(8, dtype=jnp.int32)
-    source = mine ^ (2 * (block % 4) + block // 4)
-    token = (
-        source[:, None] * local_rows + jnp.arange(local_rows, dtype=jnp.int32)[None, :]
-    ).reshape(token_count)
     ending = jnp.cumsum(request_lengths)
     starting = ending - request_lengths
+    position = jnp.arange(token_count, dtype=jnp.int32)
+    inner, block = position % local_rows, position // local_rows
+    token = (mine ^ (2 * (block % 4) + block // 4)) * local_rows + inner
     inside = (token[:, None] >= starting[None, :]) & (token[:, None] < ending[None, :])
     first = jnp.sum(jnp.where(inside, starting[None, :], 0), axis=1)
     prefix = jnp.sum(jnp.where(inside, request_prefix[None, :], 0), axis=1)
-    slot = jnp.arange(groups, dtype=jnp.int32)
-    order = own ^ slot
     held = jnp.sum(
         jnp.where(
             owner_list[None, :] == order[:, None],
@@ -424,39 +442,108 @@
         ]
     )
 
-    def scattered(weight, width):
-        send_a = project(rows_a, weight, jnp.stack([own ^ 1, own ^ 3]), width, jnp.bfloat16)
-        send_b = project(rows_b, weight, jnp.stack([own ^ 2, own ^ 3]), width, jnp.bfloat16)
-        got_a, got_b = swap(send_a, "gx", 1), swap(send_b, "gx", 2)
-        keep_a = project(rows_a, weight, jnp.stack([own, own ^ 2]), width, jnp.float32)
-        keep_b = project(rows_b, weight, jnp.stack([own, own ^ 1]), width, jnp.float32)
-        sum_a, sum_b = keep_a + got_a.astype(jnp.float32), keep_b + got_b.astype(jnp.float32)
-        last_a = swap(sum_a[1].astype(jnp.bfloat16), "gx", 2)
-        last_b = swap(sum_b[1].astype(jnp.bfloat16), "gx", 1)
-        return sum_a, last_a, sum_b, last_b
-
-    def gathered(part_a, part_b):
-        one_a, one_b = swap(part_a, "gx", 1), swap(part_b, "gx", 2)
-        two_a = swap(jnp.stack([part_a, one_a]), "gx", 2)
-        two_b = swap(jnp.stack([part_b, one_b]), "gx", 1)
-        return (part_a, one_a, two_a), (part_b, one_b, two_b)
-
-    head = scattered(qkv_weight, head_width)
-    sum_a, last_a, sum_b, last_b = scattered(up_weight, hidden_width)
-    context = attend(*head, tables, old[0], old[1], per_query, per_new, per_old)
-    context_a, context_b = gathered(context[:half_rows], context[half_rows:])
-    hidden_a = jax.nn.gelu(sum_a[0] + last_a.astype(jnp.float32), approximate=False)
-    hidden_b = jax.nn.gelu(sum_b[0] + last_b.astype(jnp.float32), approximate=False)
-    hidden_a, hidden_b = gathered(hidden_a.astype(jnp.bfloat16), hidden_b.astype(jnp.bfloat16))
-
-    order_b = jnp.stack([own, own ^ 2, own ^ 1, own ^ 3])
-    mixed_b = mix(order_b, hidden_b, context_b, down_weight, out_weight, jnp.bfloat16)
-    other = swap(mixed_b, "gy", 1)
-    mixed_a = mix(order, hidden_a, context_a, down_weight, out_weight, jnp.float32)
-    mixed = (mixed_a + other.astype(jnp.float32)).reshape(4, local_rows, -1)
-    total = values32 + mixed[0]
-    for k in range(1, 4):
-        total = total + swap(mixed[k].astype(jnp.bfloat16), "gy", 2 * k).astype(jnp.float32)
+    sent = []
+
+    def exchange(value_a, value_b, bits_a):
+        if len(sent) >= 2:
+            value_a, value_b = lax.optimization_barrier((value_a, value_b, sent[-2]))[:2]
+        sent.append((swap(value_a, "gx", bits_a), swap(value_b, "gx", 3 - bits_a)))
+        return sent[-1]
+
+    class Sums:
+        def __init__(self, rows, gate):
+            self.rows, self.gate = rows, gate
+
+        def first(self):
+            weights = [qkv_weight, up_weight]
+            rows_a, rows_b = self.rows
+            place = after(order, *self.gate)
+            if rows_a.shape[0] == local_rows:
+                (part_a,) = project([rows_a], weights, place, [[(0, 1), (0, 3)]], jnp.bfloat16)
+                place = after(place, part_a)
+                (part_b,) = project([rows_b], weights, place, [[(0, 2), (0, 3)]], jnp.bfloat16)
+            else:
+                plan = [[(0, 1), (0, 3)], [(1, 2), (1, 3)]]
+                part_a, part_b = project([rows_a, rows_b], weights, place, plan, jnp.bfloat16)
+            self.got = exchange(part_a, part_b, 1)
+            place = after(place, part_b)
+            plan = [[(0, 0), (0, 2)], [(1, 0), (1, 1)]]
+            self.kept = project([rows_a, rows_b], weights, place, plan, jnp.float32)
+
+        def second(self):
+            self.sums = [k + g.astype(jnp.float32) for k, g in zip(self.kept, self.got)]
+            self.last = exchange(*(s[1].astype(jnp.bfloat16) for s in self.sums), 2)
+
+    class Parts:
+        def __init__(self, part_a, part_b):
+            self.own = (part_a, part_b)
+
+        def first(self):
+            self.one = exchange(*self.own, 1)
+
+        def second(self):
+            self.two = exchange(*(jnp.stack(p) for p in zip(self.own, self.one)), 2)
+
+        def both(self):
+            return zip(self.own, self.one, self.two)
+
+    def activated(sums):
+        return Parts(
+            *(
+                jax.nn.gelu(
+                    s[0, :, head_width:] + g[:, head_width:].astype(jnp.float32), approximate=False
+                ).astype(jnp.bfloat16)
+                for s, g in zip(sums.sums, sums.last)
+            )
+        )
+
+    sums = []
+    for r in rows:
+        sums.append(Sums(r, sums[-1].kept if sums else ()))
+        sums[-1].first()
+        if len(sums) > 1:
+            sums[-2].second()
+        if len(sums) == 3:
+            hidden = [activated(sums[0])]
+            hidden[0].first()
+    sums[2].second()
+    hidden.append(activated(sums[1]))
+    hidden[1].first()
+    hidden.append(activated(sums[2]))
+    hidden[2].first()
+    offsets, pairs = [], []
+    for (low, high), part in zip(CHUNKS, sums):
+        for side in range(2):
+            offsets.append(side * 4 * local_rows + low * local_rows)
+            pairs += [part.sums[side], part.last[side]]
+    context = Parts(
+        *attend(tuple(offsets), pairs, tables, old[0], old[1], per_query, per_new, per_old)
+    )
+    context.first()
+    hidden[2].second()
+    context.second()
+    hidden[1].second()
+    hidden[0].second()
+
+    total = values32
+    context_a, context_b = context.both()
+    for index in (2, 1, 0):
+        low, high = CHUNKS[index]
+        offset = low * local_rows
+        hidden_a, hidden_b = hidden[index].both()
+        mixed_b = mix(
+            order, (0, 2, 1, 3), offset, hidden_b, context_b, down_weight, out_weight, jnp.bfloat16
+        )
+        other = swap(mixed_b, "gy", 1)
+        mixed_a = mix(
+            order, (0, 1, 2, 3), offset, hidden_a, context_a, down_weight, out_weight, jnp.float32
+        )
+        mixed = mixed_a + other.astype(jnp.float32)
+        for k in range(low, high):
+            part = mixed[(k - low) * local_rows : (k - low + 1) * local_rows]
+            if k:
+                part = swap(part.astype(jnp.bfloat16), "gy", 2 * k).astype(jnp.float32)
+            total = total + part
     return total
 
 

time: 178 us -> 152 us (0.85)
  waiting for transfers between devices: 81.9 us -> 50.6 us
  starting transfers between devices: 24.1 us -> 50.5 us
  blocking collectives: 11.4 us -> 0 us
  Pallas kernels: 35.1 us -> 27.5 us
  other arithmetic: 20.2 us -> 17.7 us
    ppermute x27 -> x46, waiting for transfers between devices: 81.9 us -> 50.6 us  [swap(): return lax.ppermute(value, axis, [(d, d ^ bits) for d in range(count)])]
    ppermute x27 -> x46, starting transfers between devices: 24.1 us -> 50.5 us  [swap(): return lax.ppermute(value, axis, [(d, d ^ bits) for d in range(count)])]
    psum x1 -> x0, blocking collectives: 11.4 us -> none  [square_shards(): lax.psum((jnp.sum(values32, axis=1), jnp.sum(values32 * values32, axis=1)...]
    pallas_call x11 -> x15, Pallas kernels: 35.1 us -> 27.5 us  [the longest x8 13.8 us: project(): pl.pallas_call(functools.partial(project_body, plan, widths, len(rows)),...]
    concatenate x1 -> x0, other arithmetic: 2.13 us -> none  [square_shards(): jnp.concatenate([normed] + [swap(normed, 'gy', 2 * k) for k in range(1, 4...]
    unnamed x26 -> x23, local copies, waits for them, and re-layouts: 0.72 us -> 2.83 us
    another operation x3, other arithmetic: 3.41 us -> 1.58 us  [square_shards(): jnp.stack([jnp.concatenate([cosine, cosine, rest + 1.0], axis=1), jnp.con...]
  transfers between devices with their start and end apart: 27 -> 46, of which waited for: 14 -> 18; matrix products, arithmetic and copies ran while one was open for 12% -> 11% of each run, Pallas kernels for 20% -> 18%
where the time goes in v2:
time: 152 us; the launch traced here: 151 us
  waiting for transfers between devices  50.6 us (33%)
  starting transfers between devices  50.5 us (33%)
  Pallas kernels  27.5 us (18%)
  other arithmetic  17.7 us (12%)
  local copies, waits for them, and re-layouts  4.31 us (3%)
    ppermute x46, waiting for transfers between devices, swap(): return lax.ppermute(value, axis, [(d, d ^ bits) for d in range(count)])  50.6 us
    ppermute x46, starting transfers between devices, swap(): return lax.ppermute(value, axis, [(d, d ^ bits) for d in range(count)])  50.5 us
    pallas_call x8, Pallas kernels, project(): pl.pallas_call(functools.partial(project_body, plan, widths, len(rows)),...  13.8 us
    pallas_call x6, Pallas kernels, mix(): pl.pallas_call(functools.partial(mix_body, slots, offset), out_shape=jax....  10.4 us
    convert_element_type x6, other arithmetic, activated(): return Parts(*(jax.nn.gelu(s[0, :, head_width:] + g[:, head_width:].astyp...  3.51 us
    pallas_call x1, Pallas kernels, attend(): pl.pallas_call(functools.partial(attend_body, offsets, token_count // 4),...  3.34 us
  transfers between devices with their start and end apart: 46, of which 18 were waited for; matrix products, arithmetic and copies ran while one was open for 11% of the time, Pallas kernels for 18%

profile of v2, /device:TPU:0, one launch (start us, length us, event | category | flops | bytes accessed | tf_op | source)
XLA Modules:
  0.0 151.2 jit_solution(11063823094049871863)
XLA Ops:
  2.3 3.0 %collective-permute-start.1 = (f32[2,96]{1,0:T(2,128)}, f32[2,96]{1,0:T(2,128)}, u32[]{:S(2)}, u32[]{:S(2)}) collective-permute-start(f32[2,96]{1,0:T(2,128)} %pad_maximum_fusion.10), channel_id=1, source_target_pairs={{0,16},{8,24},{16,0},{24,8},{1,17},{9,25},{17,1},{25,9},{2,18},{10... | collective-permute-start | bytes 2312 | tf_op jit(solution)/shard_map/ppermute | solution.py:210
  6.7 1.8 %fusion.80 = (bf16[2,224,128]{2,1,0:T(8,128)(2,1)}, bf16[2,224,128]{2,1,0:T(8,128)(2,1)}, bf16[2,224,128]{2,1,0:T(8,128)(2,1)}, bf16[2,224,128]{2,1,0:T(8,128)(2,1)}) fusion(s32[]{:T(128)S(6)} %select_n.135, bf16[1,224,512]{2,1,0:T(8,128)(2,1)} %bitcast.107, bf16[1,224,512]{2,1,0:T(8,128)(2,1)} %bitcast.108, s32[]{:T(128)S(6)} %select_n.136, ...), kind=kLoop, calls=%fused_computation.183 | loop fusion | flops 917504 | bytes 917520 | tf_op jit(solution)/shard_map/stack | solution.py:405
  8.5 2.9 %collective-permute-start.26 = (bf16[2,224,128]{2,1,0:T(8,128)(2,1)}, bf16[2,224,128]{2,1,0:T(8,128)(2,1)}, u32[]{:S(2)}, u32[]{:S(2)}) collective-permute-start(bf16[2,224,128]{2,1,0:T(8,128)(2,1)} %get-tuple-element.96), channel_id=1, source_target_pairs={{0,24},{8,16},{16,8},{24,0},{1,25},{9,17},{17,9},{25,1},{2,26},{10... | collective-permute-start | bytes 344072 | tf_op jit(solution)/shard_map/ppermute | solution.py:210
  21.6 2.2 %copy-done = bf16[1024,2048]{1,0:T(8,128)(2,1)S(1)} copy-done((bf16[1024,2048]{1,0:T(8,128)(2,1)S(1)}, bf16[1024,2048]{1,0:T(8,128)(2,1)}, u32[]{:S(2)}) %copy-start) | copy-done | bytes 4194328
  25.1 1.9 %collective-permute-start.13 = (bf16[2,96,896]{2,1,0:T(8,128)(2,1)S(1)}, bf16[2,96,896]{2,1,0:T(8,128)(2,1)S(1)}, u32[]{:S(2)}, u32[]{:S(2)}) collective-permute-start(bf16[2,96,896]{2,1,0:T(8,128)(2,1)S(1)} %project.8), channel_id=1, source_target_pairs={{0,8},{8,0},{16,24},{24,16},{1,9},{9,1},{17,25},{25,17},{2,10},{10... | collective-permute-start | bytes 1032200 | tf_op jit(solution)/shard_map/ppermute | solution.py:210
  28.6 2.6 %collective-permute-start.6 = (bf16[96,1024]{1,0:T(8,128)(2,1)S(1)}, bf16[96,1024]{1,0:T(8,128)(2,1)S(1)}, u32[]{:S(2)}, u32[]{:S(2)}) collective-permute-start(bf16[96,1024]{1,0:T(8,128)(2,1)S(1)} %fusion.8.refs_0_), channel_id=1, source_target_pairs={{0,4},{1,5},{2,6},{3,7},{4,0},{5,1},{6,2},{7,3},{8,12},{9,13},{10,... | collective-permute-start | bytes 589832 | tf_op jit(solution)/shard_map/ppermute | solution.py:210
  35.1 1.9 %project.10 = (f32[2,96,896]{2,1,0:T(8,128)S(1)}, f32[2,96,896]{2,1,0:T(8,128)S(1)}) custom-call(s32[4]{0:T(128)S(1)} %iota_xor_fusion.order_ref, bf16[96,1024]{1,0:T(8,128)(2,1)S(1)} %fusion.8.refs_0_, bf16[96,1024]{1,0:T(8,128)(2,1)S(1)} %collective-permute-done.3.refs_0_.refs_1_, bf16[1024,1536]{1,0:T(8,128)(2,1)S(1)} %copy-done.2, ...), custom_call_target="tpu_custom_call" | custom-call | flops 704643072 | bytes 9109504 | tf_op jit(solution)/shard_map/project/pallas_call | solution.py:241
  44.4 1.9 %project.13 = (f32[2,96,896]{2,1,0:T(8,128)S(1)}, f32[2,96,896]{2,1,0:T(8,128)S(1)}) custom-call(s32[4]{0:T(128)S(1)} %iota_xor_fusion.order_ref, bf16[96,1024]{1,0:T(8,128)(2,1)S(1)} %collective-permute-done.4.refs_0_, bf16[96,1024]{1,0:T(8,128)(2,1)S(1)} %collective-permute-done.5.refs_0_.refs_1_, bf16[1024,1536]{1,0:T(8,128)(2,1)S(1)} %copy-done.2, ...), custom_call_target="tpu_custom_call" | custom-call | flops 704643072 | bytes 9109504 | tf_op jit(solution)/shard_map/project/pallas_call | solution.py:241
  50.7 2.4 %project.14 = (bf16[2,192,896]{2,1,0:T(8,128)(2,1)S(1)}, bf16[2,192,896]{2,1,0:T(8,128)(2,1)S(1)}) custom-call(s32[4]{0:T(128)S(1)} %iota_xor_fusion.order_ref, bf16[192,1024]{1,0:T(8,128)(2,1)S(1)} %constant_dynamic-update-slice_fusion.refs_0_, bf16[192,1024]{1,0:T(8,128)(2,1)S(1)} %collective-permute-done.8.refs_1_, bf16[1024,1536]{1,0:T(8,128)(2,1)S(1)} %copy-done.2, ...), custom_call_target="tpu_custom_call" | custom-call | flops 1409286144 | bytes 9502720 | tf_op jit(solution)/shard_map/project/pallas_call | solution.py:241
  60.8 2.6 %project.15 = (f32[2,192,896]{2,1,0:T(8,128)S(1)}, f32[2,192,896]{2,1,0:T(8,128)S(1)}) custom-call(s32[4]{0:T(128)S(1)} %iota_xor_fusion.order_ref, bf16[192,1024]{1,0:T(8,128)(2,1)S(1)} %constant_dynamic-update-slice_fusion.refs_0_, bf16[192,1024]{1,0:T(8,128)(2,1)S(1)} %collective-permute-done.8.refs_1_, bf16[1024,1536]{1,0:T(8,128)(2,1)S(1)} %copy-done.2, ...), custom_call_target="tpu_custom_call" | custom-call | flops 1409286144 | bytes 10878976 | tf_op jit(solution)/shard_map/project/pallas_call | solution.py:241
  63.3 8.6 %collective-permute-done.11 = bf16[2,192,896]{2,1,0:T(8,128)(2,1)S(1)} collective-permute-done((bf16[2,192,896]{2,1,0:T(8,128)(2,1)S(1)}, bf16[2,192,896]{2,1,0:T(8,128)(2,1)S(1)}, u32[]{:S(2)}, u32[]{:S(2)}) %collective-permute-start.11) | collective-permute-done | bytes 688160 | tf_op jit(solution)/shard_map/ppermute | solution.py:210
  72.1 5.3 %collective-permute-done.12 = bf16[2,192,896]{2,1,0:T(8,128)(2,1)S(1)} collective-permute-done((bf16[2,192,896]{2,1,0:T(8,128)(2,1)S(1)}, bf16[2,192,896]{2,1,0:T(8,128)(2,1)S(1)}, u32[]{:S(2)}, u32[]{:S(2)}) %collective-permute-start.12) | collective-permute-done | bytes 688160 | tf_op jit(solution)/shard_map/ppermute | solution.py:210
  82.7 4.9 %collective-permute-done.19.refs_9_ = bf16[192,896]{1,0:T(8,128)(2,1)S(1)} collective-permute-done((bf16[192,896]{1,0:T(8,128)(2,1)S(1)}, bf16[192,896]{1,0:T(8,128)(2,1)S(1)}, u32[]{:S(2)}, u32[]{:S(2)}) %collective-permute-start.19) | collective-permute-done | bytes 344096 | tf_op jit(solution)/shard_map/ppermute | solution.py:210
  88.5 2.4 %collective-permute-done.20.refs_11_ = bf16[192,896]{1,0:T(8,128)(2,1)S(1)} collective-permute-done((bf16[192,896]{1,0:T(8,128)(2,1)S(1)}, bf16[192,896]{1,0:T(8,128)(2,1)S(1)}, u32[]{:S(2)}, u32[]{:S(2)}) %collective-permute-start.20) | collective-permute-done | bytes 344096 | tf_op jit(solution)/shard_map/ppermute | solution.py:210
  96.5 3.3 %attend.1 = (bf16[384,128]{1,0:T(8,128)(2,1)S(1)}, bf16[384,128]{1,0:T(8,128)(2,1)S(1)}) custom-call(f32[2,96,896]{2,1,0:T(8,128)S(1)} %convert_add_fusion.3.refs_0_, bf16[96,896]{1,0:T(8,128)(2,1)S(1)} %collective-permute-done.15.refs_1_, f32[2,96,896]{2,1,0:T(8,128)S(1)} %convert_add_fusion.2.refs_2_, bf16[96,896]{1,0:T(8,128)(2,1)S(1)} %collective-permute-done.16.refs_3_, ...), custom_call_target="tpu_custom_call" | custom-call | flops 654311424 | bytes 3145728 | tf_op jit(solution)/shard_map/attend/pallas_call | solution.py:319
  103.6 2.0 %collective-permute-done.31.c1 = bf16[384,128]{1,0:T(8,128)(2,1)S(1)} collective-permute-done((bf16[384,128]{1,0:T(8,128)(2,1)S(1)}, bf16[384,128]{1,0:T(8,128)(2,1)S(1)}, u32[]{:S(2)}, u32[]{:S(2)}) %collective-permute-start.31) | collective-permute-done | bytes 98336 | tf_op jit(solution)/shard_map/ppermute | solution.py:210
  109.6 4.1 %collective-permute-done.33.c2 = bf16[2,384,128]{2,1,0:T(8,128)(2,1)S(1)} collective-permute-done((bf16[2,384,128]{2,1,0:T(8,128)(2,1)S(1)}, bf16[2,384,128]{2,1,0:T(8,128)(2,1)S(1)}, u32[]{:S(2)}, u32[]{:S(2)}) %collective-permute-start.33) | collective-permute-done | bytes 196640 | tf_op jit(solution)/shard_map/ppermute | solution.py:210
  113.6 2.2 %collective-permute-done.35.c2 = bf16[2,384,128]{2,1,0:T(8,128)(2,1)S(1)} collective-permute-done((bf16[2,384,128]{2,1,0:T(8,128)(2,1)S(1)}, bf16[2,384,128]{2,1,0:T(8,128)(2,1)S(1)}, u32[]{:S(2)}, u32[]{:S(2)}) %collective-permute-start.35) | collective-permute-done | bytes 196640 | tf_op jit(solution)/shard_map/ppermute | solution.py:210
  117.1 1.9 %mix.7 = bf16[192,1024]{1,0:T(8,128)(2,1)S(1)} custom-call(s32[4]{0:T(128)S(1)} %iota_xor_fusion.order_ref, bf16[192,512]{1,0:T(8,128)(2,1)S(1)} %fusion.5.h0, bf16[192,512]{1,0:T(8,128)(2,1)S(1)} %collective-permute-done.22.h1, bf16[2,192,512]{2,1,0:T(8,128)(2,1)S(1)} %collective-permute-done.34.h2, bf16[384,128]{1,0:T(8,128)(2,1)S(1)} %get-tuple-element.79.c0, ...), custom_call_target="tpu_custom_call" | custom-call | flops 1006632960 | bytes 6619136 | tf_op jit(solution)/shard_map/mix/pallas_call | solution.py:357
  123.7 2.1 %mix.6 = f32[192,1024]{1,0:T(8,128)S(1)} custom-call(s32[4]{0:T(128)S(1)} %iota_xor_fusion.order_ref, bf16[192,512]{1,0:T(8,128)(2,1)S(1)} %fusion.2.h0, bf16[192,512]{1,0:T(8,128)(2,1)S(1)} %collective-permute-done.21.h1, bf16[2,192,512]{2,1,0:T(8,128)(2,1)S(1)} %collective-permute-done.23.h2, bf16[384,128]{1,0:T(8,128)(2,1)S(1)} %get-tuple-element.78.c0, ...), custom_call_target="tpu_custom_call" | custom-call | flops 1006632960 | bytes 6619136 | tf_op jit(solution)/shard_map/mix/pallas_call | solution.py:357
  129.9 2.5 %collective-permute-start.38 = (bf16[96,1024]{1,0:T(8,128)(2,1)S(1)}, bf16[96,1024]{1,0:T(8,128)(2,1)S(1)}, u32[]{:S(2)}, u32[]{:S(2)}) collective-permute-start(bf16[96,1024]{1,0:T(8,128)(2,1)S(1)} %get-tuple-element.100), channel_id=1, source_target_pairs={{0,6},{1,7},{2,4},{3,5},{4,2},{5,3},{6,0},{7,1},{8,14},{9,15},{10,... | collective-permute-start | bytes 589832 | tf_op jit(solution)/shard_map/ppermute | solution.py:210
  132.5 2.0 %collective-permute-start.42 = (bf16[96,1024]{1,0:T(8,128)(2,1)S(1)}, bf16[96,1024]{1,0:T(8,128)(2,1)S(1)}, u32[]{:S(2)}, u32[]{:S(2)}) collective-permute-start(bf16[96,1024]{1,0:T(8,128)(2,1)S(1)} %add_convert_fusion.1), channel_id=1, source_target_pairs={{0,2},{1,3},{2,0},{3,1},{4,6},{5,7},{6,4},{7,5},{8,10},{9,11},{10,... | collective-permute-start | bytes 589832 | tf_op jit(solution)/shard_map/ppermute | solution.py:210
  136.1 3.5 %collective-permute-done.38 = bf16[96,1024]{1,0:T(8,128)(2,1)S(1)} collective-permute-done((bf16[96,1024]{1,0:T(8,128)(2,1)S(1)}, bf16[96,1024]{1,0:T(8,128)(2,1)S(1)}, u32[]{:S(2)}, u32[]{:S(2)}) %collective-permute-start.38) | collective-permute-done | bytes 196640 | tf_op jit(solution)/shard_map/ppermute | solution.py:210
  139.6 10.6 %collective-permute-done.37 = bf16[96,1024]{1,0:T(8,128)(2,1)S(1)} collective-permute-done((bf16[96,1024]{1,0:T(8,128)(2,1)S(1)}, bf16[96,1024]{1,0:T(8,128)(2,1)S(1)}, u32[]{:S(2)}, u32[]{:S(2)}) %collective-permute-start.37) | collective-permute-done | bytes 196640 | tf_op jit(solution)/shard_map/ppermute | solution.py:210
  (172 shorter events, 71.9 us)
Async XLA Ops:
  2.3 17.2 %collective-permute-start.1 = (f32[2,96]{1,0:T(2,128)}, f32[2,96]{1,0:T(2,128)}, u32[]{:S(2)}, u32[]{:S(2)}) collective-permute-start(f32[2,96]{1,0:T(2,128)} %pad_maximum_fusion.10), channel_id=1, source_target_pairs={{0,16},{8,24},{16,0},{24,8},{1,17},{9,25},{17,1},{25,9},{2,18},{10... | collective-permute-start | bytes 2312 | tf_op jit(solution)/shard_map/ppermute | solution.py:210
  5.2 14.5 %collective-permute-start.2 = (f32[2,96]{1,0:T(2,128)}, f32[2,96]{1,0:T(2,128)}, u32[]{:S(2)}, u32[]{:S(2)}) collective-permute-start(f32[2,96]{1,0:T(2,128)} %pad_maximum_fusion.10), channel_id=1, source_target_pairs={{0,24},{8,16},{16,8},{24,0},{1,25},{9,17},{17,9},{25,1},{2,26},{10... | collective-permute-start | bytes 2312 | tf_op jit(solution)/shard_map/ppermute | solution.py:210
  6.7 13.0 %collective-permute-start = (f32[2,96]{1,0:T(2,128)}, f32[2,96]{1,0:T(2,128)}, u32[]{:S(2)}, u32[]{:S(2)}) collective-permute-start(f32[2,96]{1,0:T(2,128)} %pad_maximum_fusion.10), channel_id=1, source_target_pairs={{0,8},{8,0},{16,24},{24,16},{1,9},{9,1},{17,25},{25,17},{2,10},{10... | collective-permute-start | bytes 2312 | tf_op jit(solution)/shard_map/ppermute | solution.py:210
  8.5 18.5 %collective-permute-start.26 = (bf16[2,224,128]{2,1,0:T(8,128)(2,1)}, bf16[2,224,128]{2,1,0:T(8,128)(2,1)}, u32[]{:S(2)}, u32[]{:S(2)}) collective-permute-start(bf16[2,224,128]{2,1,0:T(8,128)(2,1)} %get-tuple-element.96), channel_id=1, source_target_pairs={{0,24},{8,16},{16,8},{24,0},{1,25},{9,17},{17,9},{25,1},{2,26},{10... | collective-permute-start | bytes 344072 | tf_op jit(solution)/shard_map/ppermute | solution.py:210
  11.4 17.2 %collective-permute-start.25 = (bf16[2,224,128]{2,1,0:T(8,128)(2,1)}, bf16[2,224,128]{2,1,0:T(8,128)(2,1)}, u32[]{:S(2)}, u32[]{:S(2)}) collective-permute-start(bf16[2,224,128]{2,1,0:T(8,128)(2,1)} %get-tuple-element.95), channel_id=1, source_target_pairs={{0,16},{8,24},{16,0},{24,8},{1,17},{9,25},{17,1},{25,9},{2,18},{10... | collective-permute-start | bytes 344072 | tf_op jit(solution)/shard_map/ppermute | solution.py:210
  19.5 11.7 %collective-permute-start.24 = (bf16[2,224,128]{2,1,0:T(8,128)(2,1)}, bf16[2,224,128]{2,1,0:T(8,128)(2,1)S(1)}, u32[]{:S(2)}, u32[]{:S(2)}) collective-permute-start(bf16[2,224,128]{2,1,0:T(8,128)(2,1)} %get-tuple-element.94), channel_id=1, source_target_pairs={{0,8},{8,0},{16,24},{24,16},{1,9},{9,1},{17,25},{25,17},{2,10},{10... | collective-permute-start | bytes 344072 | tf_op jit(solution)/shard_map/ppermute | solution.py:210
  25.1 15.9 %collective-permute-start.13 = (bf16[2,96,896]{2,1,0:T(8,128)(2,1)S(1)}, bf16[2,96,896]{2,1,0:T(8,128)(2,1)S(1)}, u32[]{:S(2)}, u32[]{:S(2)}) collective-permute-start(bf16[2,96,896]{2,1,0:T(8,128)(2,1)S(1)} %project.8), channel_id=1, source_target_pairs={{0,8},{8,0},{16,24},{24,16},{1,9},{9,1},{17,25},{25,17},{2,10},{10... | collective-permute-start | bytes 1032200 | tf_op jit(solution)/shard_map/ppermute | solution.py:210
  27.1 11.1 %collective-permute-start.4 = (bf16[96,1024]{1,0:T(8,128)(2,1)S(1)}, bf16[96,1024]{1,0:T(8,128)(2,1)S(1)}, u32[]{:S(2)}, u32[]{:S(2)}) collective-permute-start(bf16[96,1024]{1,0:T(8,128)(2,1)S(1)} %fusion.8.refs_0_), channel_id=1, source_target_pairs={{0,2},{1,3},{2,0},{3,1},{4,6},{5,7},{6,4},{7,5},{8,10},{9,11},{10,... | collective-permute-start | bytes 589832 | tf_op jit(solution)/shard_map/ppermute | solution.py:210
  28.6 11.9 %collective-permute-start.6 = (bf16[96,1024]{1,0:T(8,128)(2,1)S(1)}, bf16[96,1024]{1,0:T(8,128)(2,1)S(1)}, u32[]{:S(2)}, u32[]{:S(2)}) collective-permute-start(bf16[96,1024]{1,0:T(8,128)(2,1)S(1)} %fusion.8.refs_0_), channel_id=1, source_target_pairs={{0,4},{1,5},{2,6},{3,7},{4,0},{5,1},{6,2},{7,3},{8,12},{9,13},{10,... | collective-permute-start | bytes 589832 | tf_op jit(solution)/shard_map/ppermute | solution.py:210
  33.6 13.7 %collective-permute-start.14 = (bf16[2,96,896]{2,1,0:T(8,128)(2,1)S(1)}, bf16[2,96,896]{2,1,0:T(8,128)(2,1)S(1)}, u32[]{:S(2)}, u32[]{:S(2)}) collective-permute-start(bf16[2,96,896]{2,1,0:T(8,128)(2,1)S(1)} %project.9), channel_id=1, source_target_pairs={{0,16},{8,24},{16,0},{24,8},{1,17},{9,25},{17,1},{25,9},{2,18},{10... | collective-permute-start | bytes 1032200 | tf_op jit(solution)/shard_map/ppermute | solution.py:210
  39.5 11.2 %collective-permute-start.9 = (bf16[2,96,896]{2,1,0:T(8,128)(2,1)S(1)}, bf16[2,96,896]{2,1,0:T(8,128)(2,1)S(1)}, u32[]{:S(2)}, u32[]{:S(2)}) collective-permute-start(bf16[2,96,896]{2,1,0:T(8,128)(2,1)S(1)} %project.11), channel_id=1, source_target_pairs={{0,8},{8,0},{16,24},{24,16},{1,9},{9,1},{17,25},{25,17},{2,10},{10... | collective-permute-start | bytes 1032200 | tf_op jit(solution)/shard_map/ppermute | solution.py:210
  42.6 11.0 %collective-permute-start.10 = (bf16[2,96,896]{2,1,0:T(8,128)(2,1)S(1)}, bf16[2,96,896]{2,1,0:T(8,128)(2,1)S(1)}, u32[]{:S(2)}, u32[]{:S(2)}) collective-permute-start(bf16[2,96,896]{2,1,0:T(8,128)(2,1)S(1)} %project.12), channel_id=1, source_target_pairs={{0,16},{8,24},{16,0},{24,8},{1,17},{9,25},{17,1},{25,9},{2,18},{10... | collective-permute-start | bytes 1032200 | tf_op jit(solution)/shard_map/ppermute | solution.py:210
  53.6 18.4 %collective-permute-start.11 = (bf16[2,192,896]{2,1,0:T(8,128)(2,1)S(1)}, bf16[2,192,896]{2,1,0:T(8,128)(2,1)S(1)}, u32[]{:S(2)}, u32[]{:S(2)}) collective-permute-start(bf16[2,192,896]{2,1,0:T(8,128)(2,1)S(1)} %get-tuple-element.60), channel_id=1, source_target_pairs={{0,8},{8,0},{16,24},{24,16},{1,9},{9,1},{17,25},{25,17},{2,10},{10... | collective-permute-start | bytes 2064392 | tf_op jit(solution)/shard_map/ppermute | solution.py:210
  57.0 20.6 %collective-permute-start.17 = (bf16[96,896]{1,0:T(8,128)(2,1)S(1)}, bf16[96,896]{1,0:T(8,128)(2,1)S(1)}, u32[]{:S(2)}, u32[]{:S(2)}) collective-permute-start(bf16[96,896]{1,0:T(8,128)(2,1)S(1)} %fusion.74), channel_id=1, source_target_pairs={{0,16},{8,24},{16,0},{24,8},{1,17},{9,25},{17,1},{25,9},{2,18},{10... | collective-permute-start | bytes 516104 | tf_op jit(solution)/shard_map/ppermute | solution.py:210
  58.8 18.8 %collective-permute-start.18 = (bf16[96,896]{1,0:T(8,128)(2,1)S(1)}, bf16[96,896]{1,0:T(8,128)(2,1)S(1)}, u32[]{:S(2)}, u32[]{:S(2)}) collective-permute-start(bf16[96,896]{1,0:T(8,128)(2,1)S(1)} %fusion.75), channel_id=1, source_target_pairs={{0,8},{8,0},{16,24},{24,16},{1,9},{9,1},{17,25},{25,17},{2,10},{10... | collective-permute-start | bytes 516104 | tf_op jit(solution)/shard_map/ppermute | solution.py:210
  60.2 17.2 %collective-permute-start.12 = (bf16[2,192,896]{2,1,0:T(8,128)(2,1)S(1)}, bf16[2,192,896]{2,1,0:T(8,128)(2,1)S(1)}, u32[]{:S(2)}, u32[]{:S(2)}) collective-permute-start(bf16[2,192,896]{2,1,0:T(8,128)(2,1)S(1)} %get-tuple-element.62), channel_id=1, source_target_pairs={{0,16},{8,24},{16,0},{24,8},{1,17},{9,25},{17,1},{25,9},{2,18},{10... | collective-permute-start | bytes 2064392 | tf_op jit(solution)/shard_map/ppermute | solution.py:210
  80.3 13.1 %collective-permute-start.27 = (bf16[96,512]{1,0:T(8,128)(2,1)S(1)}, bf16[96,512]{1,0:T(8,128)(2,1)S(1)}, u32[]{:S(2)}, u32[]{:S(2)}) collective-permute-start(bf16[96,512]{1,0:T(8,128)(2,1)S(1)} %fusion.38.h0), channel_id=1, source_target_pairs={{0,8},{8,0},{16,24},{24,16},{1,9},{9,1},{17,25},{25,17},{2,10},{10... | collective-permute-start | bytes 294920 | tf_op jit(solution)/shard_map/ppermute | solution.py:210
  81.8 11.6 %collective-permute-start.28 = (bf16[96,512]{1,0:T(8,128)(2,1)S(1)}, bf16[96,512]{1,0:T(8,128)(2,1)S(1)}, u32[]{:S(2)}, u32[]{:S(2)}) collective-permute-start(bf16[96,512]{1,0:T(8,128)(2,1)S(1)} %fusion.41.h0), channel_id=1, source_target_pairs={{0,16},{8,24},{16,0},{24,8},{1,17},{9,25},{17,1},{25,9},{2,18},{10... | collective-permute-start | bytes 294920 | tf_op jit(solution)/shard_map/ppermute | solution.py:210
  102.6 14.5 %collective-permute-start.34 = (bf16[2,192,512]{2,1,0:T(8,128)(2,1)S(1)}, bf16[2,192,512]{2,1,0:T(8,128)(2,1)S(1)}, u32[]{:S(2)}, u32[]{:S(2)}) collective-permute-start(bf16[2,192,512]{2,1,0:T(8,128)(2,1)S(1)} %pad_maximum_fusion.3), channel_id=1, source_target_pairs={{0,8},{8,0},{16,24},{24,16},{1,9},{9,1},{17,25},{25,17},{2,10},{10... | collective-permute-start | bytes 1179656 | tf_op jit(solution)/shard_map/ppermute | solution.py:210
  119.0 10.8 %collective-permute-start.36 = (bf16[192,1024]{1,0:T(8,128)(2,1)S(1)}, bf16[192,1024]{1,0:T(8,128)(2,1)S(1)}, u32[]{:S(2)}, u32[]{:S(2)}) collective-permute-start(bf16[192,1024]{1,0:T(8,128)(2,1)S(1)} %mix.7), channel_id=1, source_target_pairs={{0,1},{1,0},{2,3},{3,2},{4,5},{5,4},{6,7},{7,6},{8,9},{9,8},{10,11... | collective-permute-start | bytes 1179656 | tf_op jit(solution)/shard_map/ppermute | solution.py:210
  121.4 13.1 %collective-permute-start.43 = (bf16[2,96,512]{2,1,0:T(8,128)(2,1)S(1)}, bf16[2,96,512]{2,1,0:T(8,128)(2,1)S(1)}, u32[]{:S(2)}, u32[]{:S(2)}) collective-permute-start(bf16[2,96,512]{2,1,0:T(8,128)(2,1)S(1)} %pad_maximum_fusion.8), channel_id=1, source_target_pairs={{0,16},{8,24},{16,0},{24,8},{1,17},{9,25},{17,1},{25,9},{2,18},{10... | collective-permute-start | bytes 589832 | tf_op jit(solution)/shard_map/ppermute | solution.py:210
  123.6 12.5 %collective-permute-start.45 = (bf16[96,1024]{1,0:T(8,128)(2,1)S(1)}, bf16[96,1024]{1,0:T(8,128)(2,1)S(1)}, u32[]{:S(2)}, u32[]{:S(2)}) collective-permute-start(bf16[96,1024]{1,0:T(8,128)(2,1)S(1)} %mix.11), channel_id=1, source_target_pairs={{0,1},{1,0},{2,3},{3,2},{4,5},{5,4},{6,7},{7,6},{8,9},{9,8},{10,11... | collective-permute-start | bytes 589832 | tf_op jit(solution)/shard_map/ppermute | solution.py:210
  132.5 17.8 %collective-permute-start.37 = (bf16[96,1024]{1,0:T(8,128)(2,1)S(1)}, bf16[96,1024]{1,0:T(8,128)(2,1)S(1)}, u32[]{:S(2)}, u32[]{:S(2)}) collective-permute-start(bf16[96,1024]{1,0:T(8,128)(2,1)S(1)} %get-tuple-element.99), channel_id=1, source_target_pairs={{0,4},{1,5},{2,6},{3,7},{4,0},{5,1},{6,2},{7,3},{8,12},{9,13},{10,... | collective-permute-start | bytes 589832 | tf_op jit(solution)/shard_map/ppermute | solution.py:210
  132.5 17.7 %collective-permute-start.42 = (bf16[96,1024]{1,0:T(8,128)(2,1)S(1)}, bf16[96,1024]{1,0:T(8,128)(2,1)S(1)}, u32[]{:S(2)}, u32[]{:S(2)}) collective-permute-start(bf16[96,1024]{1,0:T(8,128)(2,1)S(1)} %add_convert_fusion.1), channel_id=1, source_target_pairs={{0,2},{1,3},{2,0},{3,1},{4,6},{5,7},{6,4},{7,5},{8,10},{9,11},{10,... | collective-permute-start | bytes 589832 | tf_op jit(solution)/shard_map/ppermute | solution.py:210
  (33 other events, 259.7 us)

commit v3 on v2

--- a/solution.py
+++ b/solution.py
@@ -2,6 +2,7 @@
 
 import jax
 import jax.numpy as jnp
+import numpy as np
 from jax import lax
 from jax.experimental import pallas as pl
 from jax.experimental.pallas import tpu as pltpu
@@ -218,6 +219,83 @@
     return [pl.BlockSpec(memory_space=pltpu.VMEM)] * count
 
 
+def local_call(body, name, outs, scalars, arrays, waits=(), flops=0, scratch=()):
+    read = len(scalars) + len(arrays)
+
+    def kernel(*refs):
+        body(*refs[:read], *refs[read + len(waits) :])
+
+    return pl.pallas_call(
+        kernel,
+        out_shape=[jax.ShapeDtypeStruct(shape, dtype) for shape, dtype in outs],
+        in_specs=[pl.BlockSpec(memory_space=pltpu.SMEM)] * len(scalars)
+        + whole(len(arrays))
+        + [pl.BlockSpec(memory_space=pl.ANY)] * len(waits),
+        out_specs=whole(len(outs)),
+        scratch_shapes=scratch,
+        cost_estimate=pl.CostEstimate(
+            flops=flops,
+            bytes_accessed=sum(a.size * a.dtype.itemsize for a in arrays),
+            transcendentals=0,
+        ),
+        compiler_params=pltpu.CompilerParams(vmem_limit_bytes=20 << 20),
+        name=name,
+    )(*scalars, *arrays, *waits)
+
+
+def cut_body(info, keys, values, *outs):
+    for slot, out in enumerate(outs):
+        start = pl.multiple_of((info[0] ^ slot) * HD, HD)
+        out[0] = keys[:, pl.ds(start, HD)]
+        out[1] = values[:, pl.ds(start, HD)]
+
+
+def number_body(
+    local_rows, prefix_len, block_len, info, frequency, *refs
+):
+    tables, per_query, per_new, per_old = refs[-4:]
+    groups = 4
+    requests = (info.shape[0] - 2 - groups) // 2
+    blocks = per_query.shape[0] // local_rows
+    own, mine = info[0], info[1]
+    lane = lax.broadcasted_iota(jnp.int32, (local_rows, HD), 1)
+    row = lax.broadcasted_iota(jnp.int32, (local_rows, HD), 0)
+    position = lax.broadcasted_iota(jnp.int32, per_new.shape, 1)
+    token_row = position
+    for block in range(blocks):
+        source = mine ^ (2 * (block % 4) + block // 4)
+        low = block * local_rows
+        inside = (position >= low) & (position < low + local_rows)
+        token_row = jnp.where(inside, position + (source * local_rows - low), token_row)
+        token = source * local_rows + row
+        first = jnp.zeros_like(token)
+        prefix = jnp.zeros_like(token)
+        start = 0
+        for request in range(requests):
+            stop = start + info[2 + groups + request]
+            inside = (token >= start) & (token < stop)
+            first = jnp.where(inside, start, first)
+            prefix = jnp.where(inside, info[2 + groups + requests + request], prefix)
+            start = stop
+        span = pl.ds(low, local_rows)
+        per_query[span, :] = jnp.where(lane == 0, token, jnp.where(lane == 1, first, prefix))
+        angles = (token - first + prefix_len).astype(jnp.float32) * frequency[...]
+        sine = jnp.sin(angles)
+        tables[0, span, :] = jnp.where(lane < ROT, jnp.cos(angles), 1.0)
+        tables[1, span, :] = jnp.where((lane >= ROT // 2) & (lane < ROT), sine, 0.0)
+        tables[2, span, :] = jnp.where(lane < ROT // 2, -sine, 0.0)
+    per_new[...] = token_row
+    old = lax.broadcasted_iota(jnp.int32, per_old.shape, 1)
+    held = jnp.zeros_like(old)
+    for m in range(groups):
+        second = jnp.int32(0)
+        for index in range(groups // 2, groups):
+            second = second + jnp.where(info[2 + index] == own ^ m, 1, 0)
+        inside = (old >= m * block_len) & (old < (m + 1) * block_len)
+        held = jnp.where(inside, second, held)
+    per_old[...] = held
+
+
 def project_body(plan, widths, row_sets, order_ref, *refs):
     rows, refs = refs[:row_sets], refs[row_sets:]
     weights, outs = refs[: len(widths)], refs[len(widths) :]
@@ -268,8 +346,12 @@
 def attend_body(offsets, tile, *refs):
     count = 2 * len(offsets)
     pairs, refs = refs[:count], refs[count:]
-    tables, keys_old, values_old, per_query, per_new, per_old, out_a, out_b = refs[:8]
-    query_s, key_s, value_s = refs[8:]
+    tables, *old, per_query, per_new, per_old, out_a, out_b = refs[:10]
+    query_s, key_s, value_s, keys_old, values_old = refs[10:]
+    block_len = old[0].shape[1]
+    for index, piece in enumerate(old):
+        keys_old[index * block_len : (index + 1) * block_len, :] = piece[0]
+        values_old[index * block_len : (index + 1) * block_len, :] = piece[1]
     half_rows = out_a.shape[0]
     scale = HD ** (-0.5)
     for section, offset in enumerate(offsets):
@@ -277,7 +359,7 @@
         span = pl.ds(offset, got.shape[0])
         cosine, up, down = (tables[t, span, :] for t in range(3))
         parts = [
-            total[0, :, p * HD : (p + 1) * HD] + got[:, p * HD : (p + 1) * HD].astype(jnp.float32)
+            total[:, p * HD : (p + 1) * HD] + got[:, p * HD : (p + 1) * HD].astype(jnp.float32)
             for p in range(3)
         ]
         query_s[span, :] = turn(parts[0], cosine, up, down).astype(jnp.bfloat16)
@@ -312,24 +394,20 @@
         out[pl.ds(offset % half_rows, tile), :] = (context / total).astype(jnp.bfloat16)
 
 
-def attend(offsets, pairs, tables, keys_old, values_old, per_query, per_new, per_old):
+def attend(offsets, pairs, tables, old, per_query, per_new, per_old, waits):
     token_count = per_query.shape[0]
-    keys = token_count + keys_old.shape[0]
-    half = jax.ShapeDtypeStruct((token_count // 2, HD), jnp.bfloat16)
-    return pl.pallas_call(
+    keys = token_count + per_old.shape[1]
+    return local_call(
         functools.partial(attend_body, offsets, token_count // 4),
-        out_shape=[half, half],
-        in_specs=whole(len(pairs) + 6),
-        out_specs=whole(2),
-        scratch_shapes=[pltpu.VMEM((token_count, HD), jnp.bfloat16)] * 3,
-        cost_estimate=pl.CostEstimate(
-            flops=4 * token_count * keys * HD,
-            bytes_accessed=4 * token_count * HD * 8,
-            transcendentals=token_count * keys,
-        ),
-        compiler_params=pltpu.CompilerParams(vmem_limit_bytes=32 << 20),
-        name="attend",
-    )(*pairs, tables, keys_old, values_old, per_query, per_new, per_old)
+        "attend",
+        [((token_count // 2, HD), jnp.bfloat16)] * 2,
+        [],
+        [*pairs, tables, *old, per_query, per_new, per_old],
+        waits,
+        4 * token_count * keys * HD,
+        [pltpu.VMEM((token_count, HD), jnp.bfloat16)] * 3
+        + [pltpu.VMEM((per_old.shape[1], HD), jnp.bfloat16)] * 2,
+    )
 
 
 def mix_body(slots, offset, order_ref, h0, h1, h2, c0, c1, c2, down_ref, out_w_ref, out_ref):
@@ -385,6 +463,9 @@
     hidden_width = up_weight.shape[1] // groups
     slot = jnp.arange(groups, dtype=jnp.int32)
     order = own ^ slot
+    info = jnp.concatenate(
+        [jnp.stack([own, mine]), owner_list, request_lengths, request_prefix]
+    )
 
     values32 = stream.astype(jnp.float32)
     moments = jnp.stack([jnp.sum(values32, axis=1), jnp.sum(values32 * values32, axis=1)])
@@ -402,44 +483,24 @@
         rows_a = jnp.concatenate(near[low:high], axis=0) if high - low > 1 else near[low]
         rows.append((rows_a, swap(rows_a, "gy", 1)))
 
-    old = jnp.stack([cache_keys, cache_values])
-    pieces = []
-    for m in range(4):
-        piece = lax.dynamic_slice_in_dim(old, (own ^ m) * HD, HD, 2)
-        pieces.append(swap(piece, "gx", m) if m else piece)
-    old = jnp.concatenate(pieces, axis=1)
-
-    ending = jnp.cumsum(request_lengths)
-    starting = ending - request_lengths
-    position = jnp.arange(token_count, dtype=jnp.int32)
-    inner, block = position % local_rows, position // local_rows
-    token = (mine ^ (2 * (block % 4) + block // 4)) * local_rows + inner
-    inside = (token[:, None] >= starting[None, :]) & (token[:, None] < ending[None, :])
-    first = jnp.sum(jnp.where(inside, starting[None, :], 0), axis=1)
-    prefix = jnp.sum(jnp.where(inside, request_prefix[None, :], 0), axis=1)
-    held = jnp.sum(
-        jnp.where(
-            owner_list[None, :] == order[:, None],
-            (slot >= groups // 2).astype(jnp.int32)[None, :],
-            0,
-        ),
-        axis=1,
-    )
-    per_old = jnp.repeat(held, block_len)[None, :]
-    per_new = token[None, :]
-    per_query = jnp.stack([token, first, prefix, prefix], axis=1)
+    outs = [((2, block_len, HD), cache_keys.dtype)] * groups
+    old = local_call(cut_body, "cut", outs, [info], [cache_keys, cache_values])
+    old = [swap(piece, "gx", m) if m else piece for m, piece in enumerate(old)]
+
     half = ROT // 2
-    frequency = rotary_base ** (-2.0 * jnp.arange(half, dtype=jnp.float32) / ROT)
-    angles = (token - first + prefix_len).astype(jnp.float32)[:, None] * frequency[None, :]
-    cosine, sine = jnp.cos(angles), jnp.sin(angles)
-    zero = jnp.zeros_like(sine)
-    rest = jnp.zeros((token_count, HD - ROT), jnp.float32)
-    tables = jnp.stack(
+    frequency = np.zeros((1, HD), np.float32)
+    frequency[0, :ROT] = np.tile(rotary_base ** (-2.0 * np.arange(half) / ROT), 2)
+    tables, per_query, per_new, per_old = local_call(
+        functools.partial(number_body, local_rows, prefix_len, block_len),
+        "number",
         [
-            jnp.concatenate([cosine, cosine, rest + 1.0], axis=1),
-            jnp.concatenate([zero, sine, rest], axis=1),
-            jnp.concatenate([-sine, zero, rest], axis=1),
-        ]
+            ((3, token_count, HD), jnp.float32),
+            ((token_count, HD), jnp.int32),
+            ((1, token_count), jnp.int32),
+            ((1, block_len * groups), jnp.int32),
+        ],
+        [info],
+        [jnp.asarray(frequency)],
     )
 
     sent = []
@@ -499,7 +560,8 @@
 
     sums = []
     for r in rows:
-        sums.append(Sums(r, sums[-1].kept if sums else ()))
+        gate = (*sums[-1].kept, *old[1:]) if len(sums) == 1 else sums[-1].kept if sums else ()
+        sums.append(Sums(r, gate))
         sums[-1].first()
         if len(sums) > 1:
             sums[-2].second()
@@ -515,9 +577,9 @@
     for (low, high), part in zip(CHUNKS, sums):
         for side in range(2):
             offsets.append(side * 4 * local_rows + low * local_rows)
-            pairs += [part.sums[side], part.last[side]]
+            pairs += [part.sums[side][0], part.last[side]]
     context = Parts(
-        *attend(tuple(offsets), pairs, tables, old[0], old[1], per_query, per_new, per_old)
+        *attend(tuple(offsets), pairs, tables, old, per_query, per_new, per_old, ())
     )
     context.first()
     hidden[2].second()

time: 152 us -> 148 us (0.974)
  other arithmetic: 17.7 us -> 7.51 us
  local copies, waits for them, and re-layouts: 4.31 us -> 9.02 us
  Pallas kernels: 27.5 us -> 30.5 us
  starting transfers between devices: 50.5 us -> 47.5 us
  waiting for transfers between devices: 50.6 us -> 52.5 us
    unnamed x23 -> x21, local copies, waits for them, and re-layouts: 2.83 us -> 7.86 us
    another operation x5 -> x0, other arithmetic: 4 us -> none  [the longest x1 1.8 us: square_shards(): old = jnp.stack([cache_keys, cache_values])]
    pallas_call x1 -> x3, Pallas kernels: 3.34 us -> 6.4 us  [local_call(): pl.pallas_call(kernel, out_shape=[jax.ShapeDtypeStruct(shape, dtype) for...]
    ppermute x46, starting transfers between devices: 50.5 us -> 47.5 us  [swap(): return lax.ppermute(value, axis, [(d, d ^ bits) for d in range(count)])]
    ppermute x46, waiting for transfers between devices: 50.6 us -> 52.5 us  [swap(): return lax.ppermute(value, axis, [(d, d ^ bits) for d in range(count)])]
  transfers between devices with their start and end apart: 46 -> 46, of which waited for: 18 -> 19; matrix products, arithmetic and copies ran while one was open for 11% -> 5% of each run, Pallas kernels for 18% -> 19%
where the time goes in v3:
time: 148 us
  waiting for transfers between devices  52.5 us (35%)
  starting transfers between devices  47.5 us (32%)
  Pallas kernels  30.5 us (21%)
  local copies, waits for them, and re-layouts  9.02 us (6%)
  other arithmetic  7.51 us (5%)
    ppermute x46, waiting for transfers between devices, swap(): return lax.ppermute(value, axis, [(d, d ^ bits) for d in range(count)])  52.5 us
    ppermute x46, starting transfers between devices, swap(): return lax.ppermute(value, axis, [(d, d ^ bits) for d in range(count)])  47.5 us
    pallas_call x8, Pallas kernels, project(): pl.pallas_call(functools.partial(project_body, plan, widths, len(rows)),...  13.8 us
    pallas_call x6, Pallas kernels, mix(): pl.pallas_call(functools.partial(mix_body, slots, offset), out_shape=jax....  10.4 us
    unnamed x21, local copies, waits for them, and re-layouts  7.86 us
    pallas_call x3, Pallas kernels, local_call(): pl.pallas_call(kernel, out_shape=[jax.ShapeDtypeStruct(shape, dtype) for...  6.4 us
    convert_element_type x6, other arithmetic, activated(): return Parts(*(jax.nn.gelu(s[0, :, head_width:] + g[:, head_width:].astyp...  3.51 us
  transfers between devices with their start and end apart: 46, of which 19 were waited for; matrix products, arithmetic and copies ran while one was open for 5% of the time, Pallas kernels for 19%

profile of v3, /device:TPU:0, one launch (start us, length us, event | category | flops | bytes accessed | tf_op | source)
XLA Modules:
  0.0 147.6 jit_solution(14836263683058818760)
XLA Ops:
  1.1 3.0 %collective-permute-start = (f32[2,96]{1,0:T(2,128)S(1)}, f32[2,96]{1,0:T(2,128)S(1)}, u32[]{:S(2)}, u32[]{:S(2)}) collective-permute-start(f32[2,96]{1,0:T(2,128)S(1)} %pad_maximum_fusion.8), channel_id=1, source_target_pairs={{0,8},{8,0},{16,24},{24,16},{1,9},{9,1},{17,25},{25,17},{2,10},{10... | collective-permute-start | bytes 2312 | tf_op jit(solution)/shard_map/ppermute | solution.py:211
  8.9 2.0 %collective-permute-start.4 = (bf16[2,224,128]{2,1,0:T(8,128)(2,1)S(1)}, bf16[2,224,128]{2,1,0:T(8,128)(2,1)S(1)}, u32[]{:S(2)}, u32[]{:S(2)}) collective-permute-start(bf16[2,224,128]{2,1,0:T(8,128)(2,1)S(1)} %get-tuple-element.58), channel_id=1, source_target_pairs={{0,8},{8,0},{16,24},{24,16},{1,9},{9,1},{17,25},{25,17},{2,10},{10... | collective-permute-start | bytes 344072 | tf_op jit(solution)/shard_map/ppermute | solution.py:211
  13.8 2.2 %copy-done = bf16[1024,2048]{1,0:T(8,128)(2,1)S(1)} copy-done((bf16[1024,2048]{1,0:T(8,128)(2,1)S(1)}, bf16[1024,2048]{1,0:T(8,128)(2,1)}, u32[]{:S(2)}) %copy-start) | copy-done | bytes 4194328
  16.0 1.9 %copy-done.2 = bf16[1024,1536]{1,0:T(8,128)(2,1)S(1)} copy-done((bf16[1024,1536]{1,0:T(8,128)(2,1)S(1)}, bf16[1024,1536]{1,0:T(8,128)(2,1)}, u32[]{:S(2)}) %copy-start.2) | copy-done | bytes 3145752
  19.8 2.6 %collective-permute-start.9 = (bf16[96,1024]{1,0:T(8,128)(2,1)S(1)}, bf16[96,1024]{1,0:T(8,128)(2,1)S(1)}, u32[]{:S(2)}, u32[]{:S(2)}) collective-permute-start(bf16[96,1024]{1,0:T(8,128)(2,1)S(1)} %fusion.8.refs_0_), channel_id=1, source_target_pairs={{0,4},{1,5},{2,6},{3,7},{4,0},{5,1},{6,2},{7,3},{8,12},{9,13},{10,... | collective-permute-start | bytes 589832 | tf_op jit(solution)/shard_map/ppermute | solution.py:211
  25.3 2.4 %number.1 = (f32[3,768,128]{2,1,0:T(8,128)S(1)}, s32[768,128]{1,0:T(8,128)S(1)}, s32[1,768]{1,0:T(1,128)S(1)}, s32[1,896]{1,0:T(1,128)S(1)}) custom-call(s32[18]{0:T(128)S(1)} %concatenate.6.refs_0_, f32[1,128]{1,0:T(1,128)S(1)} %copy-done.8), custom_call_target="tpu_custom_call" | custom-call | bytes 512 | tf_op jit(solution)/shard_map/number/pallas_call | solution.py:228
  30.9 1.9 %project.10 = (f32[2,96,896]{2,1,0:T(8,128)S(1)}, f32[2,96,896]{2,1,0:T(8,128)S(1)}) custom-call(s32[4]{0:T(128)S(1)} %iota_xor_fusion.order_ref, bf16[96,1024]{1,0:T(8,128)(2,1)S(1)} %fusion.8.refs_0_, bf16[96,1024]{1,0:T(8,128)(2,1)S(1)} %collective-permute-done.3.refs_0_.refs_1_, bf16[1024,1536]{1,0:T(8,128)(2,1)S(1)} %copy-done.3, ...), custom_call_target="tpu_custom_call" | custom-call | flops 704643072 | bytes 9109504 | tf_op jit(solution)/shard_map/project/pallas_call | solution.py:319
  39.5 1.9 %project.13 = (f32[2,96,896]{2,1,0:T(8,128)S(1)}, f32[2,96,896]{2,1,0:T(8,128)S(1)}) custom-call(s32[4]{0:T(128)S(1)} %iota_xor_fusion.order_ref, bf16[96,1024]{1,0:T(8,128)(2,1)S(1)} %collective-permute-done.7.refs_0_, bf16[96,1024]{1,0:T(8,128)(2,1)S(1)} %collective-permute-done.8.refs_0_.refs_1_, bf16[1024,1536]{1,0:T(8,128)(2,1)S(1)} %copy-done.3, ...), custom_call_target="tpu_custom_call" | custom-call | flops 704643072 | bytes 9109504 | tf_op jit(solution)/shard_map/project/pallas_call | solution.py:319
  41.4 2.1 %collective-permute-done.10 = bf16[96,1024]{1,0:T(8,128)(2,1)S(1)} collective-permute-done((bf16[96,1024]{1,0:T(8,128)(2,1)S(1)}, bf16[96,1024]{1,0:T(8,128)(2,1)S(1)}, u32[]{:S(2)}, u32[]{:S(2)}) %collective-permute-start.10) | collective-permute-done | bytes 196640 | tf_op jit(solution)/shard_map/ppermute | solution.py:211
  43.7 1.9 %collective-permute-done.17 = bf16[2,96,896]{2,1,0:T(8,128)(2,1)S(1)} collective-permute-done((bf16[2,96,896]{2,1,0:T(8,128)(2,1)S(1)}, bf16[2,96,896]{2,1,0:T(8,128)(2,1)S(1)}, u32[]{:S(2)}, u32[]{:S(2)}) %collective-permute-start.17) | collective-permute-done | bytes 344096 | tf_op jit(solution)/shard_map/ppermute | solution.py:211
  49.1 3.7 %collective-permute-done.19.refs_3_ = bf16[96,896]{1,0:T(8,128)(2,1)S(1)} collective-permute-done((bf16[96,896]{1,0:T(8,128)(2,1)S(1)}, bf16[96,896]{1,0:T(8,128)(2,1)S(1)}, u32[]{:S(2)}, u32[]{:S(2)}) %collective-permute-start.19) | collective-permute-done | bytes 172064 | tf_op jit(solution)/shard_map/ppermute | solution.py:211
  55.3 2.4 %project.14 = (bf16[2,192,896]{2,1,0:T(8,128)(2,1)S(1)}, bf16[2,192,896]{2,1,0:T(8,128)(2,1)S(1)}) custom-call(s32[4]{0:T(128)S(1)} %iota_xor_fusion.order_ref, bf16[192,1024]{1,0:T(8,128)(2,1)S(1)} %constant_dynamic-update-slice_fusion.refs_0_, bf16[192,1024]{1,0:T(8,128)(2,1)S(1)} %collective-permute-done.11.refs_1_, bf16[1024,1536]{1,0:T(8,128)(2,1)S(1)} %copy-done.3, ...), custom_call_target="tpu_custom_call" | custom-call | flops 1409286144 | bytes 9502720 | tf_op jit(solution)/shard_map/project/pallas_call | solution.py:319
  61.9 2.6 %project.15 = (f32[2,192,896]{2,1,0:T(8,128)S(1)}, f32[2,192,896]{2,1,0:T(8,128)S(1)}) custom-call(s32[4]{0:T(128)S(1)} %iota_xor_fusion.order_ref, bf16[192,1024]{1,0:T(8,128)(2,1)S(1)} %constant_dynamic-update-slice_fusion.refs_0_, bf16[192,1024]{1,0:T(8,128)(2,1)S(1)} %collective-permute-done.11.refs_1_, bf16[1024,1536]{1,0:T(8,128)(2,1)S(1)} %copy-done.3, ...), custom_call_target="tpu_custom_call" | custom-call | flops 1409286144 | bytes 10878976 | tf_op jit(solution)/shard_map/project/pallas_call | solution.py:319
  64.5 1.8 %collective-permute-done.21.refs_7_ = bf16[96,896]{1,0:T(8,128)(2,1)S(1)} collective-permute-done((bf16[96,896]{1,0:T(8,128)(2,1)S(1)}, bf16[96,896]{1,0:T(8,128)(2,1)S(1)}, u32[]{:S(2)}, u32[]{:S(2)}) %collective-permute-start.21) | collective-permute-done | bytes 172064 | tf_op jit(solution)/shard_map/ppermute | solution.py:211
  66.8 8.4 %collective-permute-done.15 = bf16[2,192,896]{2,1,0:T(8,128)(2,1)S(1)} collective-permute-done((bf16[2,192,896]{2,1,0:T(8,128)(2,1)S(1)}, bf16[2,192,896]{2,1,0:T(8,128)(2,1)S(1)}, u32[]{:S(2)}, u32[]{:S(2)}) %collective-permute-start.15) | collective-permute-done | bytes 688160 | tf_op jit(solution)/shard_map/ppermute | solution.py:211
  75.4 2.7 %collective-permute-done.14 = bf16[2,192,896]{2,1,0:T(8,128)(2,1)S(1)} collective-permute-done((bf16[2,192,896]{2,1,0:T(8,128)(2,1)S(1)}, bf16[2,192,896]{2,1,0:T(8,128)(2,1)S(1)}, u32[]{:S(2)}, u32[]{:S(2)}) %collective-permute-start.14) | collective-permute-done | bytes 688160 | tf_op jit(solution)/shard_map/ppermute | solution.py:211
  82.9 3.5 %collective-permute-done.23.refs_11_ = bf16[192,896]{1,0:T(8,128)(2,1)S(1)} collective-permute-done((bf16[192,896]{1,0:T(8,128)(2,1)S(1)}, bf16[192,896]{1,0:T(8,128)(2,1)S(1)}, u32[]{:S(2)}, u32[]{:S(2)}) %collective-permute-start.23) | collective-permute-done | bytes 344096 | tf_op jit(solution)/shard_map/ppermute | solution.py:211
  94.1 3.3 %attend.1 = (bf16[384,128]{1,0:T(8,128)(2,1)S(1)}, bf16[384,128]{1,0:T(8,128)(2,1)S(1)}) custom-call(f32[96,896]{1,0:T(8,128)S(1)} %slice_bitcast_fusion.7.refs_0_, bf16[96,896]{1,0:T(8,128)(2,1)S(1)} %collective-permute-done.18.refs_1_, f32[96,896]{1,0:T(8,128)S(1)} %slice_bitcast_fusion.6.refs_2_, bf16[96,896]{1,0:T(8,128)(2,1)S(1)} %collective-permute-done.19.refs_3_, ...), custom_call_target="tpu_custom_call" | custom-call | flops 654311424 | bytes 6167040 | tf_op jit(solution)/shard_map/attend/pallas_call | solution.py:228
  107.2 7.0 %collective-permute-done.35.c2 = bf16[2,384,128]{2,1,0:T(8,128)(2,1)S(1)} collective-permute-done((bf16[2,384,128]{2,1,0:T(8,128)(2,1)S(1)}, bf16[2,384,128]{2,1,0:T(8,128)(2,1)S(1)}, u32[]{:S(2)}, u32[]{:S(2)}) %collective-permute-start.35) | collective-permute-done | bytes 196640 | tf_op jit(solution)/shard_map/ppermute | solution.py:211
  115.3 1.9 %mix.7 = bf16[192,1024]{1,0:T(8,128)(2,1)S(1)} custom-call(s32[4]{0:T(128)S(1)} %iota_xor_fusion.order_ref, bf16[192,512]{1,0:T(8,128)(2,1)S(1)} %fusion.5.h0, bf16[192,512]{1,0:T(8,128)(2,1)S(1)} %collective-permute-done.25.h1, bf16[2,192,512]{2,1,0:T(8,128)(2,1)S(1)} %collective-permute-done.34.h2, bf16[384,128]{1,0:T(8,128)(2,1)S(1)} %get-tuple-element.95.c0, ...), custom_call_target="tpu_custom_call" | custom-call | flops 1006632960 | bytes 6619136 | tf_op jit(solution)/shard_map/mix/pallas_call | solution.py:435
  122.1 1.9 %mix.6 = f32[192,1024]{1,0:T(8,128)S(1)} custom-call(s32[4]{0:T(128)S(1)} %iota_xor_fusion.order_ref, bf16[192,512]{1,0:T(8,128)(2,1)S(1)} %fusion.2.h0, bf16[192,512]{1,0:T(8,128)(2,1)S(1)} %collective-permute-done.24.h1, bf16[2,192,512]{2,1,0:T(8,128)(2,1)S(1)} %collective-permute-done.26.h2, bf16[384,128]{1,0:T(8,128)(2,1)S(1)} %get-tuple-element.94.c0, ...), custom_call_target="tpu_custom_call" | custom-call | flops 1006632960 | bytes 6619136 | tf_op jit(solution)/shard_map/mix/pallas_call | solution.py:435
  124.7 1.8 %mix.9 = bf16[96,1024]{1,0:T(8,128)(2,1)S(1)} custom-call(s32[4]{0:T(128)S(1)} %iota_xor_fusion.order_ref, bf16[96,512]{1,0:T(8,128)(2,1)S(1)} %fusion.35.h0, bf16[96,512]{1,0:T(8,128)(2,1)S(1)} %collective-permute-done.30.h1, bf16[2,96,512]{2,1,0:T(8,128)(2,1)S(1)} %collective-permute-done.40.h2, bf16[384,128]{1,0:T(8,128)(2,1)S(1)} %get-tuple-element.95.c0, ...), custom_call_target="tpu_custom_call" | custom-call | flops 503316480 | bytes 5931008 | tf_op jit(solution)/shard_map/mix/pallas_call | solution.py:435
  128.3 2.9 %collective-permute-start.37 = (bf16[96,1024]{1,0:T(8,128)(2,1)S(1)}, bf16[96,1024]{1,0:T(8,128)(2,1)S(1)}, u32[]{:S(2)}, u32[]{:S(2)}) collective-permute-start(bf16[96,1024]{1,0:T(8,128)(2,1)S(1)} %get-tuple-element.105), channel_id=1, source_target_pairs={{0,4},{1,5},{2,6},{3,7},{4,0},{5,1},{6,2},{7,3},{8,12},{9,13},{10,... | collective-permute-start | bytes 589832 | tf_op jit(solution)/shard_map/ppermute | solution.py:211
  133.8 11.7 %collective-permute-done.37 = bf16[96,1024]{1,0:T(8,128)(2,1)S(1)} collective-permute-done((bf16[96,1024]{1,0:T(8,128)(2,1)S(1)}, bf16[96,1024]{1,0:T(8,128)(2,1)S(1)}, u32[]{:S(2)}, u32[]{:S(2)}) %collective-permute-start.37) | collective-permute-done | bytes 196640 | tf_op jit(solution)/shard_map/ppermute | solution.py:211
  (151 shorter events, 69.6 us)
Async XLA Ops:
  1.1 9.8 %collective-permute-start = (f32[2,96]{1,0:T(2,128)S(1)}, f32[2,96]{1,0:T(2,128)S(1)}, u32[]{:S(2)}, u32[]{:S(2)}) collective-permute-start(f32[2,96]{1,0:T(2,128)S(1)} %pad_maximum_fusion.8), channel_id=1, source_target_pairs={{0,8},{8,0},{16,24},{24,16},{1,9},{9,1},{17,25},{25,17},{2,10},{10... | collective-permute-start | bytes 2312 | tf_op jit(solution)/shard_map/ppermute | solution.py:211
  8.9 13.4 %collective-permute-start.4 = (bf16[2,224,128]{2,1,0:T(8,128)(2,1)S(1)}, bf16[2,224,128]{2,1,0:T(8,128)(2,1)S(1)}, u32[]{:S(2)}, u32[]{:S(2)}) collective-permute-start(bf16[2,224,128]{2,1,0:T(8,128)(2,1)S(1)} %get-tuple-element.58), channel_id=1, source_target_pairs={{0,8},{8,0},{16,24},{24,16},{1,9},{9,1},{17,25},{25,17},{2,10},{10... | collective-permute-start | bytes 344072 | tf_op jit(solution)/shard_map/ppermute | solution.py:211
  12.1 11.8 %collective-permute-start.3 = (bf16[96,1024]{1,0:T(8,128)(2,1)S(1)}, bf16[96,1024]{1,0:T(8,128)(2,1)S(1)}, u32[]{:S(2)}, u32[]{:S(2)}) collective-permute-start(bf16[96,1024]{1,0:T(8,128)(2,1)S(1)} %fusion.8.refs_0_), channel_id=1, source_target_pairs={{0,1},{1,0},{2,3},{3,2},{4,5},{5,4},{6,7},{7,6},{8,9},{9,8},{10,11... | collective-permute-start | bytes 589832 | tf_op jit(solution)/shard_map/ppermute | solution.py:211
  12.2 20.7 %collective-permute-start.7 = (bf16[96,1024]{1,0:T(8,128)(2,1)S(1)}, bf16[96,1024]{1,0:T(8,128)(2,1)S(1)}, u32[]{:S(2)}, u32[]{:S(2)}) collective-permute-start(bf16[96,1024]{1,0:T(8,128)(2,1)S(1)} %fusion.8.refs_0_), channel_id=1, source_target_pairs={{0,2},{1,3},{2,0},{3,1},{4,6},{5,7},{6,4},{7,5},{8,10},{9,11},{10,... | collective-permute-start | bytes 589832 | tf_op jit(solution)/shard_map/ppermute | solution.py:211
  19.2 17.5 %collective-permute-start.16 = (bf16[2,96,896]{2,1,0:T(8,128)(2,1)S(1)}, bf16[2,96,896]{2,1,0:T(8,128)(2,1)S(1)}, u32[]{:S(2)}, u32[]{:S(2)}) collective-permute-start(bf16[2,96,896]{2,1,0:T(8,128)(2,1)S(1)} %project.8), channel_id=1, source_target_pairs={{0,8},{8,0},{16,24},{24,16},{1,9},{9,1},{17,25},{25,17},{2,10},{10... | collective-permute-start | bytes 1032200 | tf_op jit(solution)/shard_map/ppermute | solution.py:211
  19.8 16.5 %collective-permute-start.9 = (bf16[96,1024]{1,0:T(8,128)(2,1)S(1)}, bf16[96,1024]{1,0:T(8,128)(2,1)S(1)}, u32[]{:S(2)}, u32[]{:S(2)}) collective-permute-start(bf16[96,1024]{1,0:T(8,128)(2,1)S(1)} %fusion.8.refs_0_), channel_id=1, source_target_pairs={{0,4},{1,5},{2,6},{3,7},{4,0},{5,1},{6,2},{7,3},{8,12},{9,13},{10,... | collective-permute-start | bytes 589832 | tf_op jit(solution)/shard_map/ppermute | solution.py:211
  22.4 10.5 %collective-permute-start.5 = (bf16[2,224,128]{2,1,0:T(8,128)(2,1)S(1)}, bf16[2,224,128]{2,1,0:T(8,128)(2,1)S(1)}, u32[]{:S(2)}, u32[]{:S(2)}) collective-permute-start(bf16[2,224,128]{2,1,0:T(8,128)(2,1)S(1)} %get-tuple-element.59), channel_id=1, source_target_pairs={{0,16},{8,24},{16,0},{24,8},{1,17},{9,25},{17,1},{25,9},{2,18},{10... | collective-permute-start | bytes 344072 | tf_op jit(solution)/shard_map/ppermute | solution.py:211
  34.1 14.8 %collective-permute-start.12 = (bf16[2,96,896]{2,1,0:T(8,128)(2,1)S(1)}, bf16[2,96,896]{2,1,0:T(8,128)(2,1)S(1)}, u32[]{:S(2)}, u32[]{:S(2)}) collective-permute-start(bf16[2,96,896]{2,1,0:T(8,128)(2,1)S(1)} %project.11), channel_id=1, source_target_pairs={{0,8},{8,0},{16,24},{24,16},{1,9},{9,1},{17,25},{25,17},{2,10},{10... | collective-permute-start | bytes 1032200 | tf_op jit(solution)/shard_map/ppermute | solution.py:211
  34.7 10.8 %collective-permute-start.17 = (bf16[2,96,896]{2,1,0:T(8,128)(2,1)S(1)}, bf16[2,96,896]{2,1,0:T(8,128)(2,1)S(1)}, u32[]{:S(2)}, u32[]{:S(2)}) collective-permute-start(bf16[2,96,896]{2,1,0:T(8,128)(2,1)S(1)} %project.9), channel_id=1, source_target_pairs={{0,16},{8,24},{16,0},{24,8},{1,17},{9,25},{17,1},{25,9},{2,18},{10... | collective-permute-start | bytes 1032200 | tf_op jit(solution)/shard_map/ppermute | solution.py:211
  39.0 16.2 %collective-permute-start.13 = (bf16[2,96,896]{2,1,0:T(8,128)(2,1)S(1)}, bf16[2,96,896]{2,1,0:T(8,128)(2,1)S(1)}, u32[]{:S(2)}, u32[]{:S(2)}) collective-permute-start(bf16[2,96,896]{2,1,0:T(8,128)(2,1)S(1)} %project.12), channel_id=1, source_target_pairs={{0,16},{8,24},{16,0},{24,8},{1,17},{9,25},{17,1},{25,9},{2,18},{10... | collective-permute-start | bytes 1032200 | tf_op jit(solution)/shard_map/ppermute | solution.py:211
  43.6 11.7 %collective-permute-start.11 = (bf16[192,1024]{1,0:T(8,128)(2,1)S(1)}, bf16[192,1024]{1,0:T(8,128)(2,1)S(1)}, u32[]{:S(2)}, u32[]{:S(2)}) collective-permute-start(bf16[192,1024]{1,0:T(8,128)(2,1)S(1)} %constant_dynamic-update-slice_fusion.refs_0_), channel_id=1, source_target_pairs={{0,1},{1,0},{2,3},{3,2},{4,5},{5,4},{6,7},{7,6},{8,9},{9,8},{10,11... | collective-permute-start | bytes 1179656 | tf_op jit(solution)/shard_map/ppermute | solution.py:211
  57.6 17.5 %collective-permute-start.15 = (bf16[2,192,896]{2,1,0:T(8,128)(2,1)S(1)}, bf16[2,192,896]{2,1,0:T(8,128)(2,1)S(1)}, u32[]{:S(2)}, u32[]{:S(2)}) collective-permute-start(bf16[2,192,896]{2,1,0:T(8,128)(2,1)S(1)} %get-tuple-element.73), channel_id=1, source_target_pairs={{0,16},{8,24},{16,0},{24,8},{1,17},{9,25},{17,1},{25,9},{2,18},{10... | collective-permute-start | bytes 2064392 | tf_op jit(solution)/shard_map/ppermute | solution.py:211
  60.6 17.6 %collective-permute-start.20 = (bf16[96,896]{1,0:T(8,128)(2,1)S(1)}, bf16[96,896]{1,0:T(8,128)(2,1)S(1)}, u32[]{:S(2)}, u32[]{:S(2)}) collective-permute-start(bf16[96,896]{1,0:T(8,128)(2,1)S(1)} %fusion.74), channel_id=1, source_target_pairs={{0,16},{8,24},{16,0},{24,8},{1,17},{9,25},{17,1},{25,9},{2,18},{10... | collective-permute-start | bytes 516104 | tf_op jit(solution)/shard_map/ppermute | solution.py:211
  61.4 16.6 %collective-permute-start.14 = (bf16[2,192,896]{2,1,0:T(8,128)(2,1)S(1)}, bf16[2,192,896]{2,1,0:T(8,128)(2,1)S(1)}, u32[]{:S(2)}, u32[]{:S(2)}) collective-permute-start(bf16[2,192,896]{2,1,0:T(8,128)(2,1)S(1)} %get-tuple-element.71), channel_id=1, source_target_pairs={{0,8},{8,0},{16,24},{24,16},{1,9},{9,1},{17,25},{25,17},{2,10},{10... | collective-permute-start | bytes 2064392 | tf_op jit(solution)/shard_map/ppermute | solution.py:211
  81.1 9.8 %collective-permute-start.27 = (bf16[96,512]{1,0:T(8,128)(2,1)S(1)}, bf16[96,512]{1,0:T(8,128)(2,1)S(1)}, u32[]{:S(2)}, u32[]{:S(2)}) collective-permute-start(bf16[96,512]{1,0:T(8,128)(2,1)S(1)} %fusion.38.h0), channel_id=1, source_target_pairs={{0,8},{8,0},{16,24},{24,16},{1,9},{9,1},{17,25},{25,17},{2,10},{10... | collective-permute-start | bytes 294920 | tf_op jit(solution)/shard_map/ppermute | solution.py:211
  100.6 14.8 %collective-permute-start.34 = (bf16[2,192,512]{2,1,0:T(8,128)(2,1)S(1)}, bf16[2,192,512]{2,1,0:T(8,128)(2,1)S(1)}, u32[]{:S(2)}, u32[]{:S(2)}) collective-permute-start(bf16[2,192,512]{2,1,0:T(8,128)(2,1)S(1)} %pad_maximum_fusion.1), channel_id=1, source_target_pairs={{0,8},{8,0},{16,24},{24,16},{1,9},{9,1},{17,25},{25,17},{2,10},{10... | collective-permute-start | bytes 1179656 | tf_op jit(solution)/shard_map/ppermute | solution.py:211
  104.4 9.8 %collective-permute-start.35 = (bf16[2,384,128]{2,1,0:T(8,128)(2,1)S(1)}, bf16[2,384,128]{2,1,0:T(8,128)(2,1)S(1)}, u32[]{:S(2)}, u32[]{:S(2)}) collective-permute-start(bf16[2,384,128]{2,1,0:T(8,128)(2,1)S(1)} %pad_maximum_fusion.3), channel_id=1, source_target_pairs={{0,8},{8,0},{16,24},{24,16},{1,9},{9,1},{17,25},{25,17},{2,10},{10... | collective-permute-start | bytes 589832 | tf_op jit(solution)/shard_map/ppermute | solution.py:211
  106.2 11.2 %collective-permute-start.26 = (bf16[2,192,512]{2,1,0:T(8,128)(2,1)S(1)}, bf16[2,192,512]{2,1,0:T(8,128)(2,1)S(1)}, u32[]{:S(2)}, u32[]{:S(2)}) collective-permute-start(bf16[2,192,512]{2,1,0:T(8,128)(2,1)S(1)} %pad_maximum_fusion), channel_id=1, source_target_pairs={{0,16},{8,24},{16,0},{24,8},{1,17},{9,25},{17,1},{25,9},{2,18},{10... | collective-permute-start | bytes 1179656 | tf_op jit(solution)/shard_map/ppermute | solution.py:211
  117.2 11.0 %collective-permute-start.36 = (bf16[192,1024]{1,0:T(8,128)(2,1)S(1)}, bf16[192,1024]{1,0:T(8,128)(2,1)S(1)}, u32[]{:S(2)}, u32[]{:S(2)}) collective-permute-start(bf16[192,1024]{1,0:T(8,128)(2,1)S(1)} %mix.7), channel_id=1, source_target_pairs={{0,1},{1,0},{2,3},{3,2},{4,5},{5,4},{6,7},{7,6},{8,9},{9,8},{10,11... | collective-permute-start | bytes 1179656 | tf_op jit(solution)/shard_map/ppermute | solution.py:211
  119.5 12.8 %collective-permute-start.43 = (bf16[2,96,512]{2,1,0:T(8,128)(2,1)S(1)}, bf16[2,96,512]{2,1,0:T(8,128)(2,1)S(1)}, u32[]{:S(2)}, u32[]{:S(2)}) collective-permute-start(bf16[2,96,512]{2,1,0:T(8,128)(2,1)S(1)} %pad_maximum_fusion.6), channel_id=1, source_target_pairs={{0,16},{8,24},{16,0},{24,8},{1,17},{9,25},{17,1},{25,9},{2,18},{10... | collective-permute-start | bytes 589832 | tf_op jit(solution)/shard_map/ppermute | solution.py:211
  122.0 11.8 %collective-permute-start.45 = (bf16[96,1024]{1,0:T(8,128)(2,1)S(1)}, bf16[96,1024]{1,0:T(8,128)(2,1)S(1)}, u32[]{:S(2)}, u32[]{:S(2)}) collective-permute-start(bf16[96,1024]{1,0:T(8,128)(2,1)S(1)} %mix.11), channel_id=1, source_target_pairs={{0,1},{1,0},{2,3},{3,2},{4,5},{5,4},{6,7},{7,6},{8,9},{9,8},{10,11... | collective-permute-start | bytes 589832 | tf_op jit(solution)/shard_map/ppermute | solution.py:211
  128.3 17.2 %collective-permute-start.37 = (bf16[96,1024]{1,0:T(8,128)(2,1)S(1)}, bf16[96,1024]{1,0:T(8,128)(2,1)S(1)}, u32[]{:S(2)}, u32[]{:S(2)}) collective-permute-start(bf16[96,1024]{1,0:T(8,128)(2,1)S(1)} %get-tuple-element.105), channel_id=1, source_target_pairs={{0,4},{1,5},{2,6},{3,7},{4,0},{5,1},{6,2},{7,3},{8,12},{9,13},{10,... | collective-permute-start | bytes 589832 | tf_op jit(solution)/shard_map/ppermute | solution.py:211
  131.2 14.3 %collective-permute-start.38 = (bf16[96,1024]{1,0:T(8,128)(2,1)S(1)}, bf16[96,1024]{1,0:T(8,128)(2,1)S(1)}, u32[]{:S(2)}, u32[]{:S(2)}) collective-permute-start(bf16[96,1024]{1,0:T(8,128)(2,1)S(1)} %get-tuple-element.106), channel_id=1, source_target_pairs={{0,6},{1,7},{2,4},{3,5},{4,2},{5,3},{6,0},{7,1},{8,14},{9,15},{10,... | collective-permute-start | bytes 589832 | tf_op jit(solution)/shard_map/ppermute | solution.py:211
  132.2 14.5 %collective-permute-start.42 = (bf16[96,1024]{1,0:T(8,128)(2,1)S(1)}, bf16[96,1024]{1,0:T(8,128)(2,1)S(1)}, u32[]{:S(2)}, u32[]{:S(2)}) collective-permute-start(bf16[96,1024]{1,0:T(8,128)(2,1)S(1)} %add_convert_fusion.1), channel_id=1, source_target_pairs={{0,2},{1,3},{2,0},{3,1},{4,6},{5,7},{6,4},{7,5},{8,10},{9,11},{10,... | collective-permute-start | bytes 589832 | tf_op jit(solution)/shard_map/ppermute | solution.py:211
  (32 other events, 225.9 us)

commit v4 on v3

--- a/solution.py
+++ b/solution.py
@@ -410,41 +410,55 @@
     )
 
 
-def mix_body(slots, offset, order_ref, h0, h1, h2, c0, c1, c2, down_ref, out_w_ref, out_ref):
-    rows, width = h0.shape
-    head = c0.shape[1]
-    span = pl.ds(offset, rows)
-    hidden = (h0[...], h1[...], h2[0], h2[1])
-    context = (c0[span, :], c1[span, :], c2[0, span, :], c2[1, span, :])
-    total = None
-    for m, slot in enumerate(slots):
-        block = order_ref[slot]
-        down = down_ref[pl.ds(pl.multiple_of(block * width, width), width), :]
-        out = out_w_ref[pl.ds(pl.multiple_of(block * head, head), head), :]
-        term = jnp.dot(hidden[m], down, preferred_element_type=jnp.float32) + jnp.dot(
-            context[m], out, preferred_element_type=jnp.float32
-        )
-        total = term if total is None else total + term
-    out_ref[...] = total.astype(out_ref.dtype)
-
-
-def mix(order, slots, offset, hidden, context, down_weight, out_weight, dtype):
-    rows = hidden[0].shape[0]
-    columns = down_weight.shape[1]
-    depth = down_weight.shape[0] + out_weight.shape[0]
-    return pl.pallas_call(
-        functools.partial(mix_body, slots, offset),
-        out_shape=jax.ShapeDtypeStruct((rows, columns), dtype),
-        in_specs=[pl.BlockSpec(memory_space=pltpu.SMEM)] + whole(8),
-        out_specs=pl.BlockSpec(memory_space=pltpu.VMEM),
-        cost_estimate=pl.CostEstimate(
-            flops=2 * rows * depth * columns,
-            bytes_accessed=2 * (rows * depth + depth * columns + rows * columns),
-            transcendentals=0,
-        ),
-        compiler_params=pltpu.CompilerParams(vmem_limit_bytes=32 << 20),
-        name="mix",
-    )(order, *hidden, *context, down_weight, out_weight)
+def mix_body(offset, info, *refs):
+    down_ref, out_w_ref, out_a, out_b = refs[-4:]
+    for side, slots, out_ref in ((1, (0, 2, 1, 3), out_b), (0, (0, 1, 2, 3), out_a)):
+        h0, h1, h2, c0, c1, c2 = refs[6 * side : 6 * side + 6]
+        rows, width = h0.shape
+        head = c0.shape[1]
+        span = pl.ds(offset, rows)
+        hidden = (h0[...], h1[...], h2[0], h2[1])
+        context = (c0[span, :], c1[span, :], c2[0, span, :], c2[1, span, :])
+        total = None
+        for m, slot in enumerate(slots):
+            block = info[0] ^ slot
+            down = down_ref[pl.ds(pl.multiple_of(block * width, width), width), :]
+            out = out_w_ref[pl.ds(pl.multiple_of(block * head, head), head), :]
+            term = jnp.dot(hidden[m], down, preferred_element_type=jnp.float32) + jnp.dot(
+                context[m], out, preferred_element_type=jnp.float32
+            )
+            total = term if total is None else total + term
+        out_ref[...] = total.astype(out_ref.dtype)
+
+
+def mix(info, offset, hidden, context, weights, waits):
+    rows, columns = hidden[0][0].shape[0], weights[0].shape[1]
+    depth = sum(w.shape[0] for w in weights)
+    arrays = [a for side in range(2) for a in (*hidden[side], *context[side])]
+    return local_call(
+        functools.partial(mix_body, offset),
+        "mix",
+        [((rows, columns), jnp.float32), ((rows, columns), jnp.bfloat16)],
+        [info],
+        [*arrays, *weights],
+        waits,
+        4 * rows * depth * columns,
+    )
+
+
+def merge_body(mixed, other, *outs):
+    rows = outs[0].shape[0]
+    for index, out in enumerate(outs):
+        span = pl.ds(index * rows, rows)
+        out[...] = (mixed[span, :] + other[span, :].astype(jnp.float32)).astype(out.dtype)
+
+
+def merge(mixed, other, count, first, waits):
+    shape = (mixed.shape[0] // count, mixed.shape[1])
+    outs = [(shape, other.dtype)] * count
+    if first:
+        outs[0] = shape, jnp.float32
+    return local_call(merge_body, "merge", outs, [], [mixed, other], waits)
 
 
 def square_shards(
@@ -588,23 +602,20 @@
     hidden[0].second()
 
     total = values32
-    context_a, context_b = context.both()
+    context_c = tuple(context.both())
+    last = ()
     for index in (2, 1, 0):
         low, high = CHUNKS[index]
-        offset = low * local_rows
-        hidden_a, hidden_b = hidden[index].both()
-        mixed_b = mix(
-            order, (0, 2, 1, 3), offset, hidden_b, context_b, down_weight, out_weight, jnp.bfloat16
-        )
+        hidden_c = tuple(hidden[index].both())
+        weights = [down_weight, out_weight]
+        mixed_a, mixed_b = mix(info, low * local_rows, hidden_c, context_c, weights, last)
         other = swap(mixed_b, "gy", 1)
-        mixed_a = mix(
-            order, (0, 1, 2, 3), offset, hidden_a, context_a, down_weight, out_weight, jnp.float32
-        )
-        mixed = mixed_a + other.astype(jnp.float32)
+        parts = merge(mixed_a, other, high - low, low == 0, ())
+        last = (mixed_b,)
         for k in range(low, high):
-            part = mixed[(k - low) * local_rows : (k - low + 1) * local_rows]
+            part = parts[k - low]
             if k:
-                part = swap(part.astype(jnp.bfloat16), "gy", 2 * k).astype(jnp.float32)
+                part = swap(part, "gy", 2 * k).astype(jnp.float32)
             total = total + part
     return total
 

time: 148 us -> 148 us (level)
  waiting for transfers between devices: 52.5 us -> 55.3 us
  Pallas kernels: 30.5 us -> 28.7 us
    pallas_call x6 -> x0, Pallas kernels: 10.4 us -> none  [mix(): pl.pallas_call(functools.partial(mix_body, slots, offset), out_shape=jax....]
    pallas_call x3 -> x9, Pallas kernels: 6.4 us -> 14.9 us  [local_call(): pl.pallas_call(kernel, out_shape=[jax.ShapeDtypeStruct(shape, dtype) for...]
    ppermute x46, waiting for transfers between devices: 52.5 us -> 55.3 us  [swap(): return lax.ppermute(value, axis, [(d, d ^ bits) for d in range(count)])]
  transfers between devices with their start and end apart: 46 -> 46, of which waited for: 19 -> 22; matrix products, arithmetic and copies ran while one was open for 5% -> 4% of each run, Pallas kernels for 19% -> 18%
where the time goes in v4:
time: 148 us
  waiting for transfers between devices  55.3 us (37%)
  starting transfers between devices  46.9 us (32%)
  Pallas kernels  28.7 us (19%)
  local copies, waits for them, and re-layouts  8.99 us (6%)
  other arithmetic  7.25 us (5%)
    ppermute x46, waiting for transfers between devices, swap(): return lax.ppermute(value, axis, [(d, d ^ bits) for d in range(count)])  55.3 us
    ppermute x46, starting transfers between devices, swap(): return lax.ppermute(value, axis, [(d, d ^ bits) for d in range(count)])  46.9 us
    pallas_call x9, Pallas kernels, local_call(): pl.pallas_call(kernel, out_shape=[jax.ShapeDtypeStruct(shape, dtype) for...  14.9 us
    pallas_call x8, Pallas kernels, project(): pl.pallas_call(functools.partial(project_body, plan, widths, len(rows)),...  13.8 us
    unnamed x21, local copies, waits for them, and re-layouts  7.86 us
    convert_element_type x6, other arithmetic, activated(): return Parts(*(jax.nn.gelu(s[0, :, head_width:] + g[:, head_width:].astyp...  3.51 us
  transfers between devices with their start and end apart: 46, of which 22 were waited for; matrix products, arithmetic and copies ran while one was open for 4% of the time, Pallas kernels for 18%

profile of v4, /device:TPU:0, one launch (start us, length us, event | category | flops | bytes accessed | tf_op | source)
XLA Modules:
  0.0 147.7 jit_solution(6879366357749106413)
XLA Ops:
  1.1 3.0 %collective-permute-start = (f32[2,96]{1,0:T(2,128)S(1)}, f32[2,96]{1,0:T(2,128)S(1)}, u32[]{:S(2)}, u32[]{:S(2)}) collective-permute-start(f32[2,96]{1,0:T(2,128)S(1)} %pad_maximum_fusion.8), channel_id=1, source_target_pairs={{0,8},{8,0},{16,24},{24,16},{1,9},{9,1},{17,25},{25,17},{2,10},{10... | collective-permute-start | bytes 2312 | tf_op jit(solution)/shard_map/ppermute | solution.py:211
  8.9 2.0 %collective-permute-start.4 = (bf16[2,224,128]{2,1,0:T(8,128)(2,1)S(1)}, bf16[2,224,128]{2,1,0:T(8,128)(2,1)S(1)}, u32[]{:S(2)}, u32[]{:S(2)}) collective-permute-start(bf16[2,224,128]{2,1,0:T(8,128)(2,1)S(1)} %get-tuple-element.66), channel_id=1, source_target_pairs={{0,8},{8,0},{16,24},{24,16},{1,9},{9,1},{17,25},{25,17},{2,10},{10... | collective-permute-start | bytes 344072 | tf_op jit(solution)/shard_map/ppermute | solution.py:211
  13.8 2.2 %copy-done = bf16[1024,2048]{1,0:T(8,128)(2,1)S(1)} copy-done((bf16[1024,2048]{1,0:T(8,128)(2,1)S(1)}, bf16[1024,2048]{1,0:T(8,128)(2,1)}, u32[]{:S(2)}) %copy-start) | copy-done | bytes 4194328
  16.0 1.9 %copy-done.2 = bf16[1024,1536]{1,0:T(8,128)(2,1)S(1)} copy-done((bf16[1024,1536]{1,0:T(8,128)(2,1)S(1)}, bf16[1024,1536]{1,0:T(8,128)(2,1)}, u32[]{:S(2)}) %copy-start.2) | copy-done | bytes 3145752
  19.8 2.6 %collective-permute-start.9 = (bf16[96,1024]{1,0:T(8,128)(2,1)S(1)}, bf16[96,1024]{1,0:T(8,128)(2,1)S(1)}, u32[]{:S(2)}, u32[]{:S(2)}) collective-permute-start(bf16[96,1024]{1,0:T(8,128)(2,1)S(1)} %fusion.8.refs_0_), channel_id=1, source_target_pairs={{0,4},{1,5},{2,6},{3,7},{4,0},{5,1},{6,2},{7,3},{8,12},{9,13},{10,... | collective-permute-start | bytes 589832 | tf_op jit(solution)/shard_map/ppermute | solution.py:211
  25.3 2.4 %number.1 = (f32[3,768,128]{2,1,0:T(8,128)S(1)}, s32[768,128]{1,0:T(8,128)S(1)}, s32[1,768]{1,0:T(1,128)S(1)}, s32[1,896]{1,0:T(1,128)S(1)}) custom-call(s32[18]{0:T(128)S(1)} %concatenate.6.refs_0_, f32[1,128]{1,0:T(1,128)S(1)} %copy-done.8), custom_call_target="tpu_custom_call" | custom-call | bytes 512 | tf_op jit(solution)/shard_map/number/pallas_call | solution.py:228
  30.9 1.9 %project.10 = (f32[2,96,896]{2,1,0:T(8,128)S(1)}, f32[2,96,896]{2,1,0:T(8,128)S(1)}) custom-call(s32[4]{0:T(128)S(1)} %iota_xor_fusion.order_ref, bf16[96,1024]{1,0:T(8,128)(2,1)S(1)} %fusion.8.refs_0_, bf16[96,1024]{1,0:T(8,128)(2,1)S(1)} %collective-permute-done.3.refs_0_.refs_1_, bf16[1024,1536]{1,0:T(8,128)(2,1)S(1)} %copy-done.3, ...), custom_call_target="tpu_custom_call" | custom-call | flops 704643072 | bytes 9109504 | tf_op jit(solution)/shard_map/project/pallas_call | solution.py:319
  39.5 1.9 %project.13 = (f32[2,96,896]{2,1,0:T(8,128)S(1)}, f32[2,96,896]{2,1,0:T(8,128)S(1)}) custom-call(s32[4]{0:T(128)S(1)} %iota_xor_fusion.order_ref, bf16[96,1024]{1,0:T(8,128)(2,1)S(1)} %collective-permute-done.7.refs_0_, bf16[96,1024]{1,0:T(8,128)(2,1)S(1)} %collective-permute-done.8.refs_0_.refs_1_, bf16[1024,1536]{1,0:T(8,128)(2,1)S(1)} %copy-done.3, ...), custom_call_target="tpu_custom_call" | custom-call | flops 704643072 | bytes 9109504 | tf_op jit(solution)/shard_map/project/pallas_call | solution.py:319
  41.4 2.1 %collective-permute-done.10 = bf16[96,1024]{1,0:T(8,128)(2,1)S(1)} collective-permute-done((bf16[96,1024]{1,0:T(8,128)(2,1)S(1)}, bf16[96,1024]{1,0:T(8,128)(2,1)S(1)}, u32[]{:S(2)}, u32[]{:S(2)}) %collective-permute-start.10) | collective-permute-done | bytes 196640 | tf_op jit(solution)/shard_map/ppermute | solution.py:211
  43.7 1.9 %collective-permute-done.17 = bf16[2,96,896]{2,1,0:T(8,128)(2,1)S(1)} collective-permute-done((bf16[2,96,896]{2,1,0:T(8,128)(2,1)S(1)}, bf16[2,96,896]{2,1,0:T(8,128)(2,1)S(1)}, u32[]{:S(2)}, u32[]{:S(2)}) %collective-permute-start.17) | collective-permute-done | bytes 344096 | tf_op jit(solution)/shard_map/ppermute | solution.py:211
  49.1 3.7 %collective-permute-done.19.refs_3_ = bf16[96,896]{1,0:T(8,128)(2,1)S(1)} collective-permute-done((bf16[96,896]{1,0:T(8,128)(2,1)S(1)}, bf16[96,896]{1,0:T(8,128)(2,1)S(1)}, u32[]{:S(2)}, u32[]{:S(2)}) %collective-permute-start.19) | collective-permute-done | bytes 172064 | tf_op jit(solution)/shard_map/ppermute | solution.py:211
  55.3 2.4 %project.14 = (bf16[2,192,896]{2,1,0:T(8,128)(2,1)S(1)}, bf16[2,192,896]{2,1,0:T(8,128)(2,1)S(1)}) custom-call(s32[4]{0:T(128)S(1)} %iota_xor_fusion.order_ref, bf16[192,1024]{1,0:T(8,128)(2,1)S(1)} %constant_dynamic-update-slice_fusion.refs_0_, bf16[192,1024]{1,0:T(8,128)(2,1)S(1)} %collective-permute-done.11.refs_1_, bf16[1024,1536]{1,0:T(8,128)(2,1)S(1)} %copy-done.3, ...), custom_call_target="tpu_custom_call" | custom-call | flops 1409286144 | bytes 9502720 | tf_op jit(solution)/shard_map/project/pallas_call | solution.py:319
  61.9 2.6 %project.15 = (f32[2,192,896]{2,1,0:T(8,128)S(1)}, f32[2,192,896]{2,1,0:T(8,128)S(1)}) custom-call(s32[4]{0:T(128)S(1)} %iota_xor_fusion.order_ref, bf16[192,1024]{1,0:T(8,128)(2,1)S(1)} %constant_dynamic-update-slice_fusion.refs_0_, bf16[192,1024]{1,0:T(8,128)(2,1)S(1)} %collective-permute-done.11.refs_1_, bf16[1024,1536]{1,0:T(8,128)(2,1)S(1)} %copy-done.3, ...), custom_call_target="tpu_custom_call" | custom-call | flops 1409286144 | bytes 10878976 | tf_op jit(solution)/shard_map/project/pallas_call | solution.py:319
  66.8 8.4 %collective-permute-done.15 = bf16[2,192,896]{2,1,0:T(8,128)(2,1)S(1)} collective-permute-done((bf16[2,192,896]{2,1,0:T(8,128)(2,1)S(1)}, bf16[2,192,896]{2,1,0:T(8,128)(2,1)S(1)}, u32[]{:S(2)}, u32[]{:S(2)}) %collective-permute-start.15) | collective-permute-done | bytes 688160 | tf_op jit(solution)/shard_map/ppermute | solution.py:211
  75.3 2.7 %collective-permute-done.14 = bf16[2,192,896]{2,1,0:T(8,128)(2,1)S(1)} collective-permute-done((bf16[2,192,896]{2,1,0:T(8,128)(2,1)S(1)}, bf16[2,192,896]{2,1,0:T(8,128)(2,1)S(1)}, u32[]{:S(2)}, u32[]{:S(2)}) %collective-permute-start.14) | collective-permute-done | bytes 688160 | tf_op jit(solution)/shard_map/ppermute | solution.py:211
  82.9 3.5 %collective-permute-done.23.refs_11_ = bf16[192,896]{1,0:T(8,128)(2,1)S(1)} collective-permute-done((bf16[192,896]{1,0:T(8,128)(2,1)S(1)}, bf16[192,896]{1,0:T(8,128)(2,1)S(1)}, u32[]{:S(2)}, u32[]{:S(2)}) %collective-permute-start.23) | collective-permute-done | bytes 344096 | tf_op jit(solution)/shard_map/ppermute | solution.py:211
  94.1 3.3 %attend.1 = (bf16[384,128]{1,0:T(8,128)(2,1)S(1)}, bf16[384,128]{1,0:T(8,128)(2,1)S(1)}) custom-call(f32[96,896]{1,0:T(8,128)S(1)} %slice_bitcast_fusion.7.refs_0_, bf16[96,896]{1,0:T(8,128)(2,1)S(1)} %collective-permute-done.18.refs_1_, f32[96,896]{1,0:T(8,128)S(1)} %slice_bitcast_fusion.6.refs_2_, bf16[96,896]{1,0:T(8,128)(2,1)S(1)} %collective-permute-done.19.refs_3_, ...), custom_call_target="tpu_custom_call" | custom-call | flops 654311424 | bytes 6167040 | tf_op jit(solution)/shard_map/attend/pallas_call | solution.py:228
  107.2 4.2 %collective-permute-done.26.refs_3_ = bf16[2,192,512]{2,1,0:T(8,128)(2,1)S(1)} collective-permute-done((bf16[2,192,512]{2,1,0:T(8,128)(2,1)S(1)}, bf16[2,192,512]{2,1,0:T(8,128)(2,1)S(1)}, u32[]{:S(2)}, u32[]{:S(2)}) %collective-permute-start.26) | collective-permute-done | bytes 393248 | tf_op jit(solution)/shard_map/ppermute | solution.py:211
  114.7 3.1 %mix.3 = (f32[192,1024]{1,0:T(8,128)S(1)}, bf16[192,1024]{1,0:T(8,128)(2,1)S(1)}) custom-call(s32[18]{0:T(128)S(1)} %concatenate.6.refs_0_, bf16[192,512]{1,0:T(8,128)(2,1)S(1)} %fusion.2.refs_1_, bf16[192,512]{1,0:T(8,128)(2,1)S(1)} %collective-permute-done.24.refs_2_, bf16[2,192,512]{2,1,0:T(8,128)(2,1)S(1)} %collective-permute-done.26.refs_3_, ...), custom_call_target="tpu_custom_call" | custom-call | flops 2013265920 | bytes 7602176 | tf_op jit(solution)/shard_map/mix/pallas_call | solution.py:228
  120.0 2.7 %mix.4 = (f32[96,1024]{1,0:T(8,128)S(1)}, bf16[96,1024]{1,0:T(8,128)(2,1)S(1)}) custom-call(s32[18]{0:T(128)S(1)} %concatenate.6.refs_0_, bf16[96,512]{1,0:T(8,128)(2,1)S(1)} %fusion.32.refs_1_, bf16[96,512]{1,0:T(8,128)(2,1)S(1)} %collective-permute-done.29.refs_2_, bf16[2,96,512]{2,1,0:T(8,128)(2,1)S(1)} %collective-permute-done.39.refs_3_, ...), custom_call_target="tpu_custom_call" | custom-call | flops 1006632960 | bytes 6815744 | tf_op jit(solution)/shard_map/mix/pallas_call | solution.py:228
  122.8 2.5 %collective-permute-done.43.refs_3_ = bf16[2,96,512]{2,1,0:T(8,128)(2,1)S(1)} collective-permute-done((bf16[2,96,512]{2,1,0:T(8,128)(2,1)S(1)}, bf16[2,96,512]{2,1,0:T(8,128)(2,1)S(1)}, u32[]{:S(2)}, u32[]{:S(2)}) %collective-permute-start.43) | collective-permute-done | bytes 196640 | tf_op jit(solution)/shard_map/ppermute | solution.py:211
  126.0 2.5 %mix.5 = (f32[96,1024]{1,0:T(8,128)S(1)}, bf16[96,1024]{1,0:T(8,128)(2,1)S(1)}) custom-call(s32[18]{0:T(128)S(1)} %concatenate.6.refs_0_, bf16[96,512]{1,0:T(8,128)(2,1)S(1)} %fusion.38.refs_1_, bf16[96,512]{1,0:T(8,128)(2,1)S(1)} %collective-permute-done.27.refs_2_, bf16[2,96,512]{2,1,0:T(8,128)(2,1)S(1)} %collective-permute-done.43.refs_3_, ...), custom_call_target="tpu_custom_call" | custom-call | flops 1006632960 | bytes 6815744 | tf_op jit(solution)/shard_map/mix/pallas_call | solution.py:228
  128.7 2.7 %collective-permute-start.37 = (bf16[96,1024]{1,0:T(8,128)(2,1)S(1)}, bf16[96,1024]{1,0:T(8,128)(2,1)S(1)}, u32[]{:S(2)}, u32[]{:S(2)}) collective-permute-start(bf16[96,1024]{1,0:T(8,128)(2,1)S(1)} %get-tuple-element.109), channel_id=1, source_target_pairs={{0,4},{1,5},{2,6},{3,7},{4,0},{5,1},{6,2},{7,3},{8,12},{9,13},{10,... | collective-permute-start | bytes 589832 | tf_op jit(solution)/shard_map/ppermute | solution.py:211
  132.4 13.4 %collective-permute-done.37 = bf16[96,1024]{1,0:T(8,128)(2,1)S(1)} collective-permute-done((bf16[96,1024]{1,0:T(8,128)(2,1)S(1)}, bf16[96,1024]{1,0:T(8,128)(2,1)S(1)}, u32[]{:S(2)}, u32[]{:S(2)}) %collective-permute-start.37) | collective-permute-done | bytes 196640 | tf_op jit(solution)/shard_map/ppermute | solution.py:211
  (148 shorter events, 67.5 us)
Async XLA Ops:
  1.1 9.8 %collective-permute-start = (f32[2,96]{1,0:T(2,128)S(1)}, f32[2,96]{1,0:T(2,128)S(1)}, u32[]{:S(2)}, u32[]{:S(2)}) collective-permute-start(f32[2,96]{1,0:T(2,128)S(1)} %pad_maximum_fusion.8), channel_id=1, source_target_pairs={{0,8},{8,0},{16,24},{24,16},{1,9},{9,1},{17,25},{25,17},{2,10},{10... | collective-permute-start | bytes 2312 | tf_op jit(solution)/shard_map/ppermute | solution.py:211
  8.9 13.4 %collective-permute-start.4 = (bf16[2,224,128]{2,1,0:T(8,128)(2,1)S(1)}, bf16[2,224,128]{2,1,0:T(8,128)(2,1)S(1)}, u32[]{:S(2)}, u32[]{:S(2)}) collective-permute-start(bf16[2,224,128]{2,1,0:T(8,128)(2,1)S(1)} %get-tuple-element.66), channel_id=1, source_target_pairs={{0,8},{8,0},{16,24},{24,16},{1,9},{9,1},{17,25},{25,17},{2,10},{10... | collective-permute-start | bytes 344072 | tf_op jit(solution)/shard_map/ppermute | solution.py:211
  12.1 11.8 %collective-permute-start.3 = (bf16[96,1024]{1,0:T(8,128)(2,1)S(1)}, bf16[96,1024]{1,0:T(8,128)(2,1)S(1)}, u32[]{:S(2)}, u32[]{:S(2)}) collective-permute-start(bf16[96,1024]{1,0:T(8,128)(2,1)S(1)} %fusion.8.refs_0_), channel_id=1, source_target_pairs={{0,1},{1,0},{2,3},{3,2},{4,5},{5,4},{6,7},{7,6},{8,9},{9,8},{10,11... | collective-permute-start | bytes 589832 | tf_op jit(solution)/shard_map/ppermute | solution.py:211
  12.2 20.7 %collective-permute-start.7 = (bf16[96,1024]{1,0:T(8,128)(2,1)S(1)}, bf16[96,1024]{1,0:T(8,128)(2,1)S(1)}, u32[]{:S(2)}, u32[]{:S(2)}) collective-permute-start(bf16[96,1024]{1,0:T(8,128)(2,1)S(1)} %fusion.8.refs_0_), channel_id=1, source_target_pairs={{0,2},{1,3},{2,0},{3,1},{4,6},{5,7},{6,4},{7,5},{8,10},{9,11},{10,... | collective-permute-start | bytes 589832 | tf_op jit(solution)/shard_map/ppermute | solution.py:211
  19.2 17.5 %collective-permute-start.16 = (bf16[2,96,896]{2,1,0:T(8,128)(2,1)S(1)}, bf16[2,96,896]{2,1,0:T(8,128)(2,1)S(1)}, u32[]{:S(2)}, u32[]{:S(2)}) collective-permute-start(bf16[2,96,896]{2,1,0:T(8,128)(2,1)S(1)} %project.8), channel_id=1, source_target_pairs={{0,8},{8,0},{16,24},{24,16},{1,9},{9,1},{17,25},{25,17},{2,10},{10... | collective-permute-start | bytes 1032200 | tf_op jit(solution)/shard_map/ppermute | solution.py:211
  19.8 16.5 %collective-permute-start.9 = (bf16[96,1024]{1,0:T(8,128)(2,1)S(1)}, bf16[96,1024]{1,0:T(8,128)(2,1)S(1)}, u32[]{:S(2)}, u32[]{:S(2)}) collective-permute-start(bf16[96,1024]{1,0:T(8,128)(2,1)S(1)} %fusion.8.refs_0_), channel_id=1, source_target_pairs={{0,4},{1,5},{2,6},{3,7},{4,0},{5,1},{6,2},{7,3},{8,12},{9,13},{10,... | collective-permute-start | bytes 589832 | tf_op jit(solution)/shard_map/ppermute | solution.py:211
  22.4 10.5 %collective-permute-start.5 = (bf16[2,224,128]{2,1,0:T(8,128)(2,1)S(1)}, bf16[2,224,128]{2,1,0:T(8,128)(2,1)S(1)}, u32[]{:S(2)}, u32[]{:S(2)}) collective-permute-start(bf16[2,224,128]{2,1,0:T(8,128)(2,1)S(1)} %get-tuple-element.67), channel_id=1, source_target_pairs={{0,16},{8,24},{16,0},{24,8},{1,17},{9,25},{17,1},{25,9},{2,18},{10... | collective-permute-start | bytes 344072 | tf_op jit(solution)/shard_map/ppermute | solution.py:211
  34.1 14.8 %collective-permute-start.12 = (bf16[2,96,896]{2,1,0:T(8,128)(2,1)S(1)}, bf16[2,96,896]{2,1,0:T(8,128)(2,1)S(1)}, u32[]{:S(2)}, u32[]{:S(2)}) collective-permute-start(bf16[2,96,896]{2,1,0:T(8,128)(2,1)S(1)} %project.11), channel_id=1, source_target_pairs={{0,8},{8,0},{16,24},{24,16},{1,9},{9,1},{17,25},{25,17},{2,10},{10... | collective-permute-start | bytes 1032200 | tf_op jit(solution)/shard_map/ppermute | solution.py:211
  34.7 10.8 %collective-permute-start.17 = (bf16[2,96,896]{2,1,0:T(8,128)(2,1)S(1)}, bf16[2,96,896]{2,1,0:T(8,128)(2,1)S(1)}, u32[]{:S(2)}, u32[]{:S(2)}) collective-permute-start(bf16[2,96,896]{2,1,0:T(8,128)(2,1)S(1)} %project.9), channel_id=1, source_target_pairs={{0,16},{8,24},{16,0},{24,8},{1,17},{9,25},{17,1},{25,9},{2,18},{10... | collective-permute-start | bytes 1032200 | tf_op jit(solution)/shard_map/ppermute | solution.py:211
  39.0 16.2 %collective-permute-start.13 = (bf16[2,96,896]{2,1,0:T(8,128)(2,1)S(1)}, bf16[2,96,896]{2,1,0:T(8,128)(2,1)S(1)}, u32[]{:S(2)}, u32[]{:S(2)}) collective-permute-start(bf16[2,96,896]{2,1,0:T(8,128)(2,1)S(1)} %project.12), channel_id=1, source_target_pairs={{0,16},{8,24},{16,0},{24,8},{1,17},{9,25},{17,1},{25,9},{2,18},{10... | collective-permute-start | bytes 1032200 | tf_op jit(solution)/shard_map/ppermute | solution.py:211
  43.6 11.7 %collective-permute-start.11 = (bf16[192,1024]{1,0:T(8,128)(2,1)S(1)}, bf16[192,1024]{1,0:T(8,128)(2,1)S(1)}, u32[]{:S(2)}, u32[]{:S(2)}) collective-permute-start(bf16[192,1024]{1,0:T(8,128)(2,1)S(1)} %constant_dynamic-update-slice_fusion.refs_0_), channel_id=1, source_target_pairs={{0,1},{1,0},{2,3},{3,2},{4,5},{5,4},{6,7},{7,6},{8,9},{9,8},{10,11... | collective-permute-start | bytes 1179656 | tf_op jit(solution)/shard_map/ppermute | solution.py:211
  57.6 17.5 %collective-permute-start.15 = (bf16[2,192,896]{2,1,0:T(8,128)(2,1)S(1)}, bf16[2,192,896]{2,1,0:T(8,128)(2,1)S(1)}, u32[]{:S(2)}, u32[]{:S(2)}) collective-permute-start(bf16[2,192,896]{2,1,0:T(8,128)(2,1)S(1)} %get-tuple-element.81), channel_id=1, source_target_pairs={{0,16},{8,24},{16,0},{24,8},{1,17},{9,25},{17,1},{25,9},{2,18},{10... | collective-permute-start | bytes 2064392 | tf_op jit(solution)/shard_map/ppermute | solution.py:211
  60.6 17.6 %collective-permute-start.20 = (bf16[96,896]{1,0:T(8,128)(2,1)S(1)}, bf16[96,896]{1,0:T(8,128)(2,1)S(1)}, u32[]{:S(2)}, u32[]{:S(2)}) collective-permute-start(bf16[96,896]{1,0:T(8,128)(2,1)S(1)} %fusion.74), channel_id=1, source_target_pairs={{0,16},{8,24},{16,0},{24,8},{1,17},{9,25},{17,1},{25,9},{2,18},{10... | collective-permute-start | bytes 516104 | tf_op jit(solution)/shard_map/ppermute | solution.py:211
  61.4 16.6 %collective-permute-start.14 = (bf16[2,192,896]{2,1,0:T(8,128)(2,1)S(1)}, bf16[2,192,896]{2,1,0:T(8,128)(2,1)S(1)}, u32[]{:S(2)}, u32[]{:S(2)}) collective-permute-start(bf16[2,192,896]{2,1,0:T(8,128)(2,1)S(1)} %get-tuple-element.79), channel_id=1, source_target_pairs={{0,8},{8,0},{16,24},{24,16},{1,9},{9,1},{17,25},{25,17},{2,10},{10... | collective-permute-start | bytes 2064392 | tf_op jit(solution)/shard_map/ppermute | solution.py:211
  81.1 9.7 %collective-permute-start.27 = (bf16[96,512]{1,0:T(8,128)(2,1)S(1)}, bf16[96,512]{1,0:T(8,128)(2,1)S(1)}, u32[]{:S(2)}, u32[]{:S(2)}) collective-permute-start(bf16[96,512]{1,0:T(8,128)(2,1)S(1)} %fusion.38.refs_1_), channel_id=1, source_target_pairs={{0,8},{8,0},{16,24},{24,16},{1,9},{9,1},{17,25},{25,17},{2,10},{10... | collective-permute-start | bytes 294920 | tf_op jit(solution)/shard_map/ppermute | solution.py:211
  81.7 9.4 %collective-permute-start.28 = (bf16[96,512]{1,0:T(8,128)(2,1)S(1)}, bf16[96,512]{1,0:T(8,128)(2,1)S(1)}, u32[]{:S(2)}, u32[]{:S(2)}) collective-permute-start(bf16[96,512]{1,0:T(8,128)(2,1)S(1)} %fusion.41.refs_7_), channel_id=1, source_target_pairs={{0,16},{8,24},{16,0},{24,8},{1,17},{9,25},{17,1},{25,9},{2,18},{10... | collective-permute-start | bytes 294920 | tf_op jit(solution)/shard_map/ppermute | solution.py:211
  89.9 10.4 %collective-permute-start.25 = (bf16[192,512]{1,0:T(8,128)(2,1)S(1)}, bf16[192,512]{1,0:T(8,128)(2,1)S(1)}, u32[]{:S(2)}, u32[]{:S(2)}) collective-permute-start(bf16[192,512]{1,0:T(8,128)(2,1)S(1)} %fusion.5.refs_7_), channel_id=1, source_target_pairs={{0,16},{8,24},{16,0},{24,8},{1,17},{9,25},{17,1},{25,9},{2,18},{10... | collective-permute-start | bytes 589832 | tf_op jit(solution)/shard_map/ppermute | solution.py:211
  100.5 10.9 %collective-permute-start.26 = (bf16[2,192,512]{2,1,0:T(8,128)(2,1)S(1)}, bf16[2,192,512]{2,1,0:T(8,128)(2,1)S(1)}, u32[]{:S(2)}, u32[]{:S(2)}) collective-permute-start(bf16[2,192,512]{2,1,0:T(8,128)(2,1)S(1)} %pad_maximum_fusion), channel_id=1, source_target_pairs={{0,16},{8,24},{16,0},{24,8},{1,17},{9,25},{17,1},{25,9},{2,18},{10... | collective-permute-start | bytes 1179656 | tf_op jit(solution)/shard_map/ppermute | solution.py:211
  101.8 10.7 %collective-permute-start.34 = (bf16[2,192,512]{2,1,0:T(8,128)(2,1)S(1)}, bf16[2,192,512]{2,1,0:T(8,128)(2,1)S(1)}, u32[]{:S(2)}, u32[]{:S(2)}) collective-permute-start(bf16[2,192,512]{2,1,0:T(8,128)(2,1)S(1)} %pad_maximum_fusion.1), channel_id=1, source_target_pairs={{0,8},{8,0},{16,24},{24,16},{1,9},{9,1},{17,25},{25,17},{2,10},{10... | collective-permute-start | bytes 1179656 | tf_op jit(solution)/shard_map/ppermute | solution.py:211
  117.8 10.8 %collective-permute-start.36 = (bf16[192,1024]{1,0:T(8,128)(2,1)S(1)}, bf16[192,1024]{1,0:T(8,128)(2,1)S(1)}, u32[]{:S(2)}, u32[]{:S(2)}) collective-permute-start(bf16[192,1024]{1,0:T(8,128)(2,1)S(1)} %get-tuple-element.108.refs_15_), channel_id=1, source_target_pairs={{0,1},{1,0},{2,3},{3,2},{4,5},{5,4},{6,7},{7,6},{8,9},{9,8},{10,11... | collective-permute-start | bytes 1179656 | tf_op jit(solution)/shard_map/ppermute | solution.py:211
  122.7 9.6 %collective-permute-start.41 = (bf16[96,1024]{1,0:T(8,128)(2,1)S(1)}, bf16[96,1024]{1,0:T(8,128)(2,1)S(1)}, u32[]{:S(2)}, u32[]{:S(2)}) collective-permute-start(bf16[96,1024]{1,0:T(8,128)(2,1)S(1)} %get-tuple-element.114.refs_15_), channel_id=1, source_target_pairs={{0,1},{1,0},{2,3},{3,2},{4,5},{5,4},{6,7},{7,6},{8,9},{9,8},{10,11... | collective-permute-start | bytes 589832 | tf_op jit(solution)/shard_map/ppermute | solution.py:211
  128.7 17.1 %collective-permute-start.37 = (bf16[96,1024]{1,0:T(8,128)(2,1)S(1)}, bf16[96,1024]{1,0:T(8,128)(2,1)S(1)}, u32[]{:S(2)}, u32[]{:S(2)}) collective-permute-start(bf16[96,1024]{1,0:T(8,128)(2,1)S(1)} %get-tuple-element.109), channel_id=1, source_target_pairs={{0,4},{1,5},{2,6},{3,7},{4,0},{5,1},{6,2},{7,3},{8,12},{9,13},{10,... | collective-permute-start | bytes 589832 | tf_op jit(solution)/shard_map/ppermute | solution.py:211
  131.4 14.5 %collective-permute-start.38 = (bf16[96,1024]{1,0:T(8,128)(2,1)S(1)}, bf16[96,1024]{1,0:T(8,128)(2,1)S(1)}, u32[]{:S(2)}, u32[]{:S(2)}) collective-permute-start(bf16[96,1024]{1,0:T(8,128)(2,1)S(1)} %get-tuple-element.110), channel_id=1, source_target_pairs={{0,6},{1,7},{2,4},{3,5},{4,2},{5,3},{6,0},{7,1},{8,14},{9,15},{10,... | collective-permute-start | bytes 589832 | tf_op jit(solution)/shard_map/ppermute | solution.py:211
  132.3 14.6 %collective-permute-start.42 = (bf16[96,1024]{1,0:T(8,128)(2,1)S(1)}, bf16[96,1024]{1,0:T(8,128)(2,1)S(1)}, u32[]{:S(2)}, u32[]{:S(2)}) collective-permute-start(bf16[96,1024]{1,0:T(8,128)(2,1)S(1)} %merge.4), channel_id=1, source_target_pairs={{0,2},{1,3},{2,0},{3,1},{4,6},{5,7},{6,4},{7,5},{8,10},{9,11},{10,... | collective-permute-start | bytes 589832 | tf_op jit(solution)/shard_map/ppermute | solution.py:211
  (32 other events, 222.4 us)
